TPU v7x, 32 devices: a whole 2x2x4 slice. The times are simulated.
32 devices in a mesh: gx: 2 (over core), gy: 4 (over y, x), gz: 4 (over z).
Axes of the slice: x: 2, y: 2, z: 4, core: 2. Of those that a mesh axis runs over, the one named last changes fastest.
Arguments:
- heights: float32 [8192, 1024], P(('gy', 'gz'), 'gx'), may hold values from -6 to 6
- scene_ids: int32 [8192, 1024], P(('gy', 'gz'), 'gx'), may hold values from 0 to 15, as said below
- scene_offset: float32 [16], replicated, may hold values from -4 to 4
- scene_weight: float32 [16], replicated, may hold values from 0.2 to 5
- band_gain: float32 [6], replicated, may hold values from 0.3 to 1.5
Outputs:
- blended: float32 [8192, 1024], P(('gy', 'gz'), 'gx')
Inputs may be any that keep to these rules, and one draw needn't show every extreme that they name: `scene_ids`: scene index of each cell.
All inputs are finite; a program needn't handle non-finite values.
Results may differ from a plain program's by a relative error of at most 0.00002.
Values sent between devices are 32-bit elements; how exact they have to be, the bound alone decides.
A program may use at most 128 MiB of HBM per device.

v0:
```python
import functools

import jax
import jax.numpy as jnp
import numpy as np
from jax import lax
from jax.experimental import pallas as pl
from jax.experimental.pallas import tpu as pltpu
from jax.sharding import PartitionSpec as P

F32, BF16 = jnp.float32, jnp.bfloat16
FAR = 1 << 20
HALO = 16
SIDE = 128
EDGE3 = 24
TAPS = (0.375, 0.25, 0.0625)
LEVELS = 6


def reach(count):
    weights = np.ones(count >> LEVELS, np.float64)
    for _ in range(LEVELS):
        fine = np.zeros(2 * weights.size + 4, np.float64)
        for tap, value in zip(range(-2, 3), (0.0625, 0.25, 0.375, 0.25, 0.0625)):
            fine[2 + tap : 2 + tap + 2 * weights.size : 2] += value * weights
        weights = fine[2:-2]
    return weights.astype(np.float32)


def split(x):
    high = x.astype(BF16)
    return high, (x - high.astype(F32)).astype(BF16)


def right(x, c):
    high, low = split(x)
    return jnp.dot(high, c, preferred_element_type=F32) + jnp.dot(
        low, c, preferred_element_type=F32
    )


def left(r, x):
    high, low = split(x)
    return jnp.dot(r, high, preferred_element_type=F32) + jnp.dot(
        r, low, preferred_element_type=F32
    )


def band(distance, scale):
    far = jnp.abs(distance)
    value = jnp.where(far == 2, TAPS[2] * scale, 0.0)
    value = jnp.where(far == 1, TAPS[1] * scale, value)
    value = jnp.where(far == 0, TAPS[0] * scale, value)
    return value.astype(F32).astype(BF16)


def kernel(
    sizes, off_ref, wgt_ref, gain_ref, h_ref, s_ref, u_ref, v_ref, z1_ref, q0_ref,
    q0, h_buf, s_buf, u_buf, v_buf, nh, nl, dh, dl, b3, part, slots,
    own_sem, send0, recv0, send3, recv3, psend, precv,
):
    nr, nc, nx, ny, nz, rows_total, cols_total = sizes
    cx, cy, cz = lax.axis_index("gx"), lax.axis_index("gy"), lax.axis_index("gz")
    row = cy * nz + cz
    blocks = ny * nz
    w3 = nc // 8
    t3 = nr // 8

    def device(drow, dcol):
        target = row + drow
        return {"gx": cx + dcol, "gy": target // nz, "gz": target % nz}

    has = {-1: (row > 0, cx > 0), 0: None, 1: (row < blocks - 1, cx < nx - 1)}

    def there(drow, dcol):
        ok = None
        if drow:
            ok = has[drow][0]
        if dcol:
            ok = has[dcol][1] if ok is None else jnp.logical_and(ok, has[dcol][1])
        return ok

    dirs = [(a, b) for a in (-1, 0, 1) for b in (-1, 0, 1) if a or b]
    axes = (("gx", nx, cx), ("gz", nz, cz), ("gy", ny, cy))

    own = []
    for i, (src, dst) in enumerate(
        (
            (h_ref, h_buf.at[pl.ds(0, nr), pl.ds(0, nc)]),
            (s_ref, s_buf.at[pl.ds(0, nr), pl.ds(0, nc)]),
            (u_ref.at[row], u_buf),
            (v_ref.at[cx], v_buf),
        )
    ):
        copy = pltpu.make_async_copy(src, dst, own_sem.at[i])
        copy.start()
        own.append(copy)

    barrier = pltpu.get_barrier_semaphore()
    for d in dirs:
        @pl.when(there(*d))
        def _():
            pl.semaphore_signal(barrier, inc=1, device_id=device(*d))
    for name, count, me in axes:
        for step in range(1, count):
            pl.semaphore_signal(barrier, inc=1, device_id={name: (me + step) % count})

    def iota(n, dim):
        return lax.broadcasted_iota(jnp.int32, (n, 1) if dim == 0 else (1, n), dim)

    def fold(index, first, total, level):
        base = first >> level
        ok = jnp.logical_and(index + base >= 0, index + base < (total >> level))
        return jnp.where(ok, index, FAR)

    row0, col0 = row * nr, cx * nc
    r1, r2 = nr // 2 + 16, nr // 4 + 16
    c1, c2 = nc // 2 + 128, nc // 4 + 128
    r3, r4, r5, r6 = t3 + 2 * EDGE3, nr // 16 + 32, nr // 32 + 16, nr // 64 + 8

    def rows_at(level, dim):
        if level == 0:
            p = iota(nr + 2 * HALO, dim)
            return jnp.where(p < nr, p, jnp.where(p < nr + HALO, p - nr - HALO, p - HALO))
        count, shift = ((r1, 8), (r2, 8), (r3, EDGE3), (r4, 16), (r5, 8), (r6, 4))[level - 1]
        return iota(count, dim) - shift

    def cols_at(level, dim):
        if level == 0:
            p = iota(nc + 2 * SIDE, dim)
            return jnp.where(p < nc, p, jnp.where(p < nc + SIDE, p - nc - SIDE, p - SIDE))
        if level < 3:
            return iota((c1, c2)[level - 1], dim) - 8
        if level == 3:
            p = iota(6 * w3, dim)
            return (p // (2 * w3) - 1) * w3 + p % w3
        return iota(2 * w3, dim) % w3 - (16, 8, 4)[level - 4]

    def kind(count, dim):
        return (iota(count, dim) // w3) % 2

    def reduce_rows(level):
        out = fold(rows_at(level + 1, 0), row0, rows_total, level + 1)
        return band(rows_at(level, 1) - 2 * out, 1.0)

    def reduce_cols(level):
        out = fold(cols_at(level + 1, 1), col0, cols_total, level + 1)
        distance = cols_at(level, 0) - 2 * out
        if level >= 3:
            same = kind(distance.shape[0], 0) == kind(distance.shape[1], 1)
            distance = jnp.where(same, distance, FAR)
        return band(distance, 1.0)

    def expand_rows(level):
        out = iota(nr, 0) if level == 0 else rows_at(level, 0)
        return band(2 * rows_at(level + 1, 1) - out, 2.0)

    def expand_cols(level):
        out = iota(nc, 1) if level == 0 else cols_at(level, 1)
        return band(2 * cols_at(level + 1, 0) - out, 2.0)

    def lookup(masks, table):
        values = [table[i] for i in range(table.shape[0])]
        for mask in masks:
            values = [
                jnp.where(mask, values[i + 1], values[i]) for i in range(0, len(values), 2)
            ]
        return values[0]

    bits = (off_ref.shape[0] - 1).bit_length()

    def level0(rows, cols, valid):
        ids = s_buf[rows, cols]
        masks = [(ids & (1 << bit)) != 0 for bit in range(bits)]
        weight = lookup(masks, wgt_ref)
        moved = h_buf[rows, cols] + lookup(masks, off_ref)
        numer = weight * moved
        if valid is not None:
            weight = jnp.where(valid, weight, 0.0)
            numer = jnp.where(valid, numer, 0.0)
        nh[rows, cols], nl[rows, cols] = split(numer)
        dh[rows, cols], dl[rows, cols] = split(weight)
        return moved

    for copy in own:
        copy.wait()

    step = 32

    def own_rows(i, carry):
        rows = pl.ds(pl.multiple_of(i * step, step), step)
        q0[rows, :] = level0(rows, pl.ds(0, nc), None)
        return carry

    lax.fori_loop(0, nr // step, own_rows, 0)

    near = sum(there(*d).astype(jnp.int32) for d in dirs)
    pl.semaphore_wait(barrier, near + (nx + ny + nz - 3))

    def rim(i, a, d):
        drow, dcol = d
        src, dst = ((h_ref, h_buf), (s_ref, s_buf))[a]
        rs = {-1: (0, nr + HALO, HALO), 0: (0, 0, nr), 1: (nr - HALO, nr, HALO)}[drow]
        cs = {-1: (0, nc + SIDE, SIDE), 0: (0, 0, nc), 1: (nc - SIDE, nc, SIDE)}[dcol]
        return pltpu.make_async_remote_copy(
            src_ref=src.at[pl.ds(rs[0], rs[2]), pl.ds(cs[0], cs[2])],
            dst_ref=dst.at[pl.ds(rs[1], rs[2]), pl.ds(cs[1], cs[2])],
            send_sem=send0.at[2 * i + a],
            recv_sem=recv0.at[2 * i + a],
            device_id=device(*d),
        )

    for i, d in enumerate(dirs):
        @pl.when(there(*d))
        def _():
            for a in range(2):
                rim(i, a, d).start()

    def dot(a, b):
        return jnp.dot(a, b, preferred_element_type=F32)

    own_out = iota(2 * w3, 1)
    in2 = cols_at(2, 0)
    pick_n = band(jnp.where(own_out < w3, in2 - 2 * own_out, FAR), 1.0)
    pick_d = band(jnp.where(own_out < w3, FAR, in2 - 2 * (own_out - w3)), 1.0)
    own_rows3 = band(rows_at(2, 1) - 2 * iota(t3, 0), 1.0)
    reduce0, rows1 = reduce_rows(0), reduce_rows(1)
    rows03 = dot(dot(own_rows3, rows1).astype(BF16), reduce0)
    rows03 = jnp.concatenate(split(rows03), axis=0)
    u_high, u_low = split(u_buf[...])
    pick = iota(16, 0)
    u_rows = jnp.where(
        pick == 0, u_high.astype(F32), jnp.where(pick == 1, u_low.astype(F32), 0.0)
    ).astype(BF16)
    top = jnp.concatenate([rows03[:, :nr], u_rows], axis=0)

    def own_part(high, low):
        rows, cols = pl.ds(0, nr), pl.ds(0, nc)
        return dot(top, high[rows, cols]) + dot(top, low[rows, cols])

    tn, td = own_part(nh, nl), own_part(dh, dl)
    v_row = v_buf[...]
    sum_n = jnp.sum(tn[2 * t3 :, :] * v_row)
    sum_d = jnp.sum(td[2 * t3 :, :] * v_row)

    tile_row = lax.broadcasted_iota(jnp.int32, (8, 128), 0)
    part[0] = jnp.where(tile_row == 0, sum_n, jnp.where(tile_row == 1, sum_d, 0.0))

    starts = (0, nx - 1, nx + nz - 2)

    def phase(k):
        name, count, me = axes[k]
        return [
            pltpu.make_async_remote_copy(
                src_ref=part.at[k],
                dst_ref=slots.at[starts[k] + s - 1],
                send_sem=psend.at[starts[k] + s - 1],
                recv_sem=precv.at[starts[k] + s - 1],
                device_id={name: (me + s) % count},
            )
            for s in range(1, count)
        ]

    def finish(k):
        total = part[k]
        for s, copy in enumerate(phase(k)):
            copy.wait()
            total = total + slots[starts[k] + s]
        return total

    for copy in phase(0):
        copy.start()

    q0_copy = pltpu.make_async_copy(q0, q0_ref, own_sem.at[4])
    q0_copy.start()

    def take(ds):
        for i, d in enumerate(dirs):
            if d in ds:
                @pl.when(there(*d))
                def _():
                    for a in range(2):
                        rim(i, a, d).wait_send()

                @pl.when(there(-d[0], -d[1]))
                def _():
                    for a in range(2):
                        rim(i, a, d).wait_recv()

    def yes(flag):
        return flag.astype(jnp.int32)

    up, down = yes(row > 0), yes(row < blocks - 1)
    west, east = yes(cx > 0), yes(cx < nx - 1)
    side_ok = jnp.where(iota(2 * SIDE, 1) < SIDE, west, east)
    rim_ok = jnp.where(iota(2 * HALO, 0) < HALO, up, down)
    body, rim_r = pl.ds(0, nr), pl.ds(nr, 2 * HALO)
    middle, side_c = pl.ds(0, nc), pl.ds(nc, 2 * SIDE)

    take([d for d in dirs if d[0] == 0])

    def side_rows(i, carry):
        rows = pl.ds(pl.multiple_of(i * step, step), step)
        level0(rows, side_c, jnp.broadcast_to(side_ok, (step, 2 * SIDE)) > 0)
        return carry

    lax.fori_loop(0, nr // step, side_rows, 0)

    cols0, cols1 = reduce_cols(0), reduce_cols(1)
    cols02 = dot(cols0, cols1).astype(BF16)
    cols03 = [split(dot(cols02, pick)) for pick in (pick_n, pick_d)]

    def side_part(t, high, low):
        t_side = dot(rows03[:, :nr], high[body, side_c]) + dot(rows03[:, :nr], low[body, side_c])
        t = jnp.concatenate([t[: 2 * t3], t_side], axis=1)
        return t[:t3] + t[t3:]

    tn, td = side_part(tn, nh, nl), side_part(td, dh, dl)

    part[1] = finish(0)
    for copy in phase(1):
        copy.start()

    half, start = nr // 4, nr // 2 - 32
    reduce0_b = band(
        start + iota(nr - start, 1) - 2 * fold(iota(r1 - half, 0) + (half - 8), row0, rows_total, 1), 1.0
    )

    def level1(x):
        t = [dot(reduce0[:half, : nr // 2], part_[pl.ds(0, nr // 2), :]) for part_ in x]
        b = [dot(reduce0_b, part_[pl.ds(start, nr - start), :]) for part_ in x]
        t = jnp.concatenate([t[0] + t[1], b[0] + b[1]], axis=0)
        low, high = split(t)

        def wide(k0, k1, n0, n1):
            return dot(low[:, k0:k1], cols0[k0:k1, n0:n1]) + dot(high[:, k0:k1], cols0[k0:k1, n0:n1])

        edge = nc // 2
        return jnp.concatenate(
            [
                wide(0, nc + SIDE, 0, edge),
                wide(nc - SIDE, nc, edge, c1) + wide(nc + SIDE, nc + 2 * SIDE, edge, c1),
            ],
            axis=1,
        )

    n1, d1 = level1((nh, nl)), level1((dh, dl))

    take([d for d in dirs if d[0] != 0])
    level0(rim_r, middle, jnp.broadcast_to(rim_ok, (2 * HALO, nc)) > 0)
    level0(rim_r, side_c, jnp.broadcast_to(rim_ok * side_ok, (2 * HALO, 2 * SIDE)) > 0)

    def rim_part(t, high, low, cols):
        e = dot(rows03[:, nr:], high[rim_r, :]) + dot(rows03[:, nr:], low[rim_r, :])
        t = t + e[:t3] + e[t3:]
        t_high, t_low = split(t)
        return dot(t_high, cols[0]) + dot(t_low, cols[0]) + dot(t_high, cols[1])

    b3[1, pl.ds(EDGE3, t3), :] = rim_part(tn, nh, nl, cols03[0]) + rim_part(td, dh, dl, cols03[1])

    def rim3(i, d):
        drow, dcol = d
        rs = {
            -1: (EDGE3, EDGE3 + t3, EDGE3),
            0: (EDGE3, EDGE3, t3),
            1: (t3, 0, EDGE3),
        }[drow]
        return pltpu.make_async_remote_copy(
            src_ref=b3.at[1, pl.ds(rs[0], rs[2]), :],
            dst_ref=b3.at[1 - dcol, pl.ds(rs[1], rs[2]), :],
            send_sem=send3.at[i],
            recv_sem=recv3.at[i],
            device_id=device(*d),
        )

    for i, d in enumerate(dirs):
        @pl.when(there(*d))
        def _():
            rim3(i, d).start()

    def ends(count):
        p = iota(32, 0)
        return jnp.where(p < 16, p, count - 32 + p)

    rim_in = iota(2 * HALO, 1)
    rim_in = rim_in + jnp.where(rim_in < HALO, -HALO, nr - HALO)
    ends0 = band(rim_in - 2 * fold(ends(r1) - 8, row0, rows_total, 1), 1.0)

    def patch(x, high, low):
        e = left(ends0, dot(high[rim_r, :], cols0) + dot(low[rim_r, :], cols0))
        n = x.shape[0]
        return jnp.concatenate([x[:16] + e[:16], x[16 : n - 16], x[n - 16 :] + e[16:]], axis=0)

    n1, d1 = patch(n1, nh, nl), patch(d1, dh, dl)
    part[2] = finish(1)
    for copy in phase(2):
        copy.start()
    q1 = jnp.where(d1 > 0, n1 / d1, 0.0)
    n2, d2 = left(rows1, right(n1, cols1)), left(rows1, right(d1, cols1))
    q2 = jnp.where(d2 > 0, n2 / d2, 0.0)

    rows_ = [None, None, None] + [reduce_rows(level) for level in (3, 4, 5)]
    cols_ = [None, None, None] + [reduce_cols(level) for level in (3, 4, 5)]
    up_rows = [None] + [expand_rows(level) for level in range(1, 6)]
    up_cols = [None] + [expand_cols(level) for level in range(1, 6)]

    for i, d in enumerate(dirs):
        @pl.when(there(*d))
        def _():
            rim3(i, d).wait_send()

        @pl.when(there(-d[0], -d[1]))
        def _():
            rim3(i, d).wait_recv()

    p3 = iota(r3, 0)
    ok3 = jnp.where(p3 < EDGE3, up, jnp.where(p3 < EDGE3 + t3, 1, down))
    lane = iota(2 * w3, 1)

    def ratio(packed):
        weights = pltpu.roll(packed, w3, axis=1)
        ok = jnp.logical_and(weights > 0, jnp.broadcast_to(lane, packed.shape) < w3)
        return jnp.where(ok, packed / weights, 0.0), ok

    pieces = []
    for block, flag in ((0, west), (1, None), (2, east)):
        ok = ok3 if flag is None else ok3 * flag
        piece = b3[block]
        pieces.append(jnp.where(jnp.broadcast_to(ok, piece.shape) > 0, piece, 0.0))
    packed = jnp.concatenate(pieces, axis=1)
    q3 = [ratio(piece) for piece in pieces]
    q3, ok_3 = [q for q, _ in q3], [jnp.where(ok, 1.0, 0.0) for _, ok in q3]
    q3, ok_3 = jnp.concatenate(q3, axis=1), jnp.concatenate(ok_3, axis=1) > 0

    v4 = left(rows_[3], right(packed, cols_[3]))
    v5 = left(rows_[4], right(v4, cols_[4]))
    v6 = left(rows_[5], right(v5, cols_[5]))
    q4, ok_4 = ratio(v4)
    q5, ok_5 = ratio(v5)
    q6, ok_6 = ratio(v6)

    total = finish(2)
    top_sum = jnp.sum(jnp.where(tile_row == 0, total, 0.0), axis=0, keepdims=True)
    top_weight = jnp.sum(jnp.where(tile_row == 1, total, 0.0), axis=0, keepdims=True)
    top_mean = (top_sum / top_weight)[:, :1]

    z = jnp.where(ok_6, top_mean - gain_ref[5] * q6, 0.0)
    levels = ((5, q5, ok_5), (4, q4, ok_4), (3, q3, ok_3), (2, q2, d2 > 0), (1, q1, d1 > 0))
    for level, q, ok in levels:
        grown = left(up_rows[level], right(z, up_cols[level]))
        z = jnp.where(ok, grown + (gain_ref[level] - gain_ref[level - 1]) * q, 0.0)
    z1_ref[...] = z
    q0_copy.wait()


def last(gain_ref, z_ref, q_hbm, out_ref, q_buf, out_buf, sem):
    nr, nc = out_buf.shape
    block = nr // 4
    copies = [
        pltpu.make_async_copy(
            q_hbm.at[pl.ds(i * block, block), :], q_buf.at[pl.ds(i * block, block), :], sem.at[i]
        )
        for i in range(4)
    ]
    for copy in copies:
        copy.start()
    tall = block // 2 + 16

    def iota(n, dim):
        return lax.broadcasted_iota(jnp.int32, (n, 1) if dim == 0 else (1, n), dim)

    cols = band(2 * (iota(z_ref.shape[1], 0) - 8) - iota(nc, 1), 2.0)
    rows = band(2 * (iota(tall, 1) - 8) - iota(block, 0), 2.0)
    gain = gain_ref[0]
    wide = right(z_ref[...], cols)
    writes = []
    for i in range(4):
        grown = left(rows, wide[i * block // 2 : i * block // 2 + tall])
        copies[i].wait()
        here = pl.ds(i * block, block)
        out_buf[here, :] = gain * q_buf[here, :] + grown
        writes.append(pltpu.make_async_copy(out_buf.at[here, :], out_ref.at[here, :], sem.at[4 + i]))
        writes[-1].start()
    for write in writes:
        write.wait()


def local(mesh_shape, heights, scene_ids, scene_offset, scene_weight, band_gain):
    nx, ny, nz = mesh_shape
    nr, nc = heights.shape
    rows_total, cols_total = nr * ny * nz, nc * nx
    u = jnp.asarray(reach(rows_total).reshape(ny * nz, 1, nr))
    v = jnp.asarray(reach(cols_total).reshape(nx, 1, nc))
    sizes = (nr, nc, nx, ny, nz, rows_total, cols_total)
    ext = (nr + 2 * HALO, nc + 2 * SIDE)
    peers = nx + ny + nz - 3
    smem = pl.BlockSpec(memory_space=pltpu.SMEM)
    hbm = pl.BlockSpec(memory_space=pl.ANY)
    z1, q0 = pl.pallas_call(
        functools.partial(kernel, sizes),
        out_shape=(
            jax.ShapeDtypeStruct((nr // 2 + 16, nc // 2 + 128), F32),
            jax.ShapeDtypeStruct((nr, nc), F32),
        ),
        in_specs=[smem, smem, smem, hbm, hbm, hbm, hbm],
        out_specs=(pl.BlockSpec(memory_space=pltpu.VMEM), hbm),
        scratch_shapes=[
            pltpu.VMEM((nr, nc), F32),
            pltpu.VMEM(ext, F32),
            pltpu.VMEM(ext, jnp.int32),
            pltpu.VMEM((1, nr), F32),
            pltpu.VMEM((1, nc), F32),
            pltpu.VMEM(ext, BF16),
            pltpu.VMEM(ext, BF16),
            pltpu.VMEM(ext, BF16),
            pltpu.VMEM(ext, BF16),
            pltpu.VMEM((3, nr // 8 + 2 * EDGE3, nc // 4), F32),
            pltpu.VMEM((3, 8, 128), F32),
            pltpu.VMEM((peers, 8, 128), F32),
            pltpu.SemaphoreType.DMA((5,)),
            pltpu.SemaphoreType.DMA((16,)),
            pltpu.SemaphoreType.DMA((16,)),
            pltpu.SemaphoreType.DMA((8,)),
            pltpu.SemaphoreType.DMA((8,)),
            pltpu.SemaphoreType.DMA((peers,)),
            pltpu.SemaphoreType.DMA((peers,)),
        ],
        compiler_params=pltpu.CompilerParams(collective_id=0, has_side_effects=True),
    )(scene_offset, scene_weight, band_gain, heights, scene_ids, u, v)
    vmem = pl.BlockSpec(memory_space=pltpu.VMEM)
    return pl.pallas_call(
        last,
        out_shape=jax.ShapeDtypeStruct((nr, nc), F32),
        in_specs=[smem, vmem, hbm],
        out_specs=hbm,
        scratch_shapes=[
            pltpu.VMEM((nr, nc), F32),
            pltpu.VMEM((nr, nc), F32),
            pltpu.SemaphoreType.DMA((8,)),
        ],
    )(band_gain, z1, q0)


def solution(mesh):
    placed = (P(("gy", "gz"), "gx"), P(("gy", "gz"), "gx"), P(), P(), P())
    shape = tuple(mesh.shape[name] for name in ("gx", "gy", "gz"))
    return jax.shard_map(
        functools.partial(local, shape), mesh=mesh, in_specs=placed,
        out_specs=P(("gy", "gz"), "gx"), check_vma=False,
    )
```

profile of v0, /device:TPU:0, one launch (start us, length us, event | category | flops | bytes accessed | tf_op | source)
XLA Modules:
  0.0 26.9 jit_solution(10998826809693551660)
XLA Ops:
  0.0 23.4 %shard_map.73 = (f32[272,384]{1,0:T(8,128)}, f32[512,512]{1,0:T(8,128)}) custom-call(f32[16]{0:T(128)} %off_ref.1, f32[16]{0:T(128)} %wgt_ref.1, f32[6]{0:T(128)} %gain_ref.3, f32[512,512]{1,0:T(8,128)} %h_ref.1, s32[512,512]{1,0:T(8,128)} %s_ref.1, f32[16,1,512]{2,1,0:T(1,128)} %constant.4.clone.u_ref, f32[2,1,512]{2,1,0:T(1,128)} %constant.5.clone.v_ref), custom_call_target="tpu_custom_call" | custom-call | tf_op jit(solution)/shard_map/pallas_call | solution.py:499
  23.5 3.4 %shard_map.74 = f32[512,512]{1,0:T(8,128)} custom-call(f32[6]{0:T(128)} %gain_ref.3, f32[272,384]{1,0:T(8,128)} %get-tuple-element.7.z_ref, f32[512,512]{1,0:T(8,128)} %get-tuple-element.8.q_hbm), custom_call_target="tpu_custom_call" | custom-call | tf_op jit(solution)/shard_map/pallas_call | solution.py:531
where the time goes:
time: 27.1 us; the launch traced here: 26.9 us
  Pallas kernels  26.9 us (99%)
    pallas_call x1, Pallas kernels, local(): pl.pallas_call(functools.partial(kernel, sizes), out_shape=(jax.ShapeDtyp...  23.4 us
    pallas_call x1, Pallas kernels, local(): pl.pallas_call(last, out_shape=jax.ShapeDtypeStruct((nr, nc), F32), in_sp...  3.41 us

commit v1 on v0

--- a/solution.py
+++ b/solution.py
@@ -55,8 +55,8 @@
 
 
 def kernel(
-    sizes, off_ref, wgt_ref, gain_ref, h_ref, s_ref, u_ref, v_ref, z1_ref, q0_ref,
-    q0, h_buf, s_buf, u_buf, v_buf, nh, nl, dh, dl, b3, part, slots,
+    sizes, off_hbm, wgt_hbm, gain_hbm, h_ref, s_ref, u_ref, v_ref, out_ref,
+    off_ref, wgt_ref, gain_ref, wide, q0, h_buf, s_buf, u_buf, v_buf, nh, nl, dh, dl, b3, part, slots,
     own_sem, send0, recv0, send3, recv3, psend, precv,
 ):
     nr, nc, nx, ny, nz, rows_total, cols_total = sizes
@@ -90,6 +90,9 @@
             (s_ref, s_buf.at[pl.ds(0, nr), pl.ds(0, nc)]),
             (u_ref.at[row], u_buf),
             (v_ref.at[cx], v_buf),
+            (off_hbm, off_ref),
+            (wgt_hbm, wgt_ref),
+            (gain_hbm, gain_ref),
         )
     ):
         copy = pltpu.make_async_copy(src, dst, own_sem.at[i])
@@ -159,21 +162,34 @@
         out = iota(nc, 1) if level == 0 else cols_at(level, 1)
         return band(2 * cols_at(level + 1, 0) - out, 2.0)
 
-    def lookup(masks, table):
-        values = [table[i] for i in range(table.shape[0])]
-        for mask in masks:
-            values = [
-                jnp.where(mask, values[i + 1], values[i]) for i in range(0, len(values), 2)
-            ]
-        return values[0]
-
-    bits = (off_ref.shape[0] - 1).bit_length()
+    lane128 = lax.broadcasted_iota(jnp.int32, (8, 128), 1)
+
+    def spread(table):
+        row = jnp.zeros((8, 128), F32)
+        for i in range(table.shape[0]):
+            row = jnp.where(lane128 == i, table[i], row)
+        return row
+
+    def lookup(ids, table):
+        n, m = ids.shape
+        return jnp.concatenate(
+            [
+                jnp.concatenate(
+                    [
+                        jnp.take_along_axis(table, ids[r : r + 8, c : c + 128], axis=1)
+                        for c in range(0, m, 128)
+                    ],
+                    axis=1,
+                )
+                for r in range(0, n, 8)
+            ],
+            axis=0,
+        )
 
     def level0(rows, cols, valid):
         ids = s_buf[rows, cols]
-        masks = [(ids & (1 << bit)) != 0 for bit in range(bits)]
-        weight = lookup(masks, wgt_ref)
-        moved = h_buf[rows, cols] + lookup(masks, off_ref)
+        weight = lookup(ids, wgt_row)
+        moved = h_buf[rows, cols] + lookup(ids, off_row)
         numer = weight * moved
         if valid is not None:
             weight = jnp.where(valid, weight, 0.0)
@@ -184,12 +200,15 @@
 
     for copy in own:
         copy.wait()
+    wgt_row, off_row = spread(wgt_ref), spread(off_ref)
 
     step = 32
 
     def own_rows(i, carry):
         rows = pl.ds(pl.multiple_of(i * step, step), step)
-        q0[rows, :] = level0(rows, pl.ds(0, nc), None)
+        moved = level0(rows, pl.ds(0, nc), None)
+        for c in range(nc // 128):
+            q0[c, rows, :] = moved[:, c * 128 : (c + 1) * 128]
         return carry
 
     lax.fori_loop(0, nr // step, own_rows, 0)
@@ -271,8 +290,6 @@
     for copy in phase(0):
         copy.start()
 
-    q0_copy = pltpu.make_async_copy(q0, q0_ref, own_sem.at[4])
-    q0_copy.start()
 
     def take(ds):
         for i, d in enumerate(dirs):
@@ -449,40 +466,19 @@
     for level, q, ok in levels:
         grown = left(up_rows[level], right(z, up_cols[level]))
         z = jnp.where(ok, grown + (gain_ref[level] - gain_ref[level - 1]) * q, 0.0)
-    z1_ref[...] = z
-    q0_copy.wait()
-
-
-def last(gain_ref, z_ref, q_hbm, out_ref, q_buf, out_buf, sem):
-    nr, nc = out_buf.shape
-    block = nr // 4
-    copies = [
-        pltpu.make_async_copy(
-            q_hbm.at[pl.ds(i * block, block), :], q_buf.at[pl.ds(i * block, block), :], sem.at[i]
-        )
-        for i in range(4)
-    ]
-    for copy in copies:
-        copy.start()
-    tall = block // 2 + 16
-
-    def iota(n, dim):
-        return lax.broadcasted_iota(jnp.int32, (n, 1) if dim == 0 else (1, n), dim)
-
-    cols = band(2 * (iota(z_ref.shape[1], 0) - 8) - iota(nc, 1), 2.0)
-    rows = band(2 * (iota(tall, 1) - 8) - iota(block, 0), 2.0)
+    full = right(z, expand_cols(0))
+    tiles = nc // 128
+    for c in range(tiles):
+        wide[c] = full[:, c * 128 : (c + 1) * 128]
     gain = gain_ref[0]
-    wide = right(z_ref[...], cols)
-    writes = []
-    for i in range(4):
-        grown = left(rows, wide[i * block // 2 : i * block // 2 + tall])
-        copies[i].wait()
-        here = pl.ds(i * block, block)
-        out_buf[here, :] = gain * q_buf[here, :] + grown
-        writes.append(pltpu.make_async_copy(out_buf.at[here, :], out_ref.at[here, :], sem.at[4 + i]))
-        writes[-1].start()
-    for write in writes:
-        write.wait()
+    chunk = 32
+    for c in range(tiles):
+        for m in range(0, nr // 2, chunk):
+            x, y, w = (wide[c, pl.ds(m + k, chunk), :] for k in (7, 8, 9))
+            even, odd = pl.ds(2 * m, chunk, stride=2), pl.ds(2 * m + 1, chunk, stride=2)
+            q0[c, even, :] = gain * q0[c, even, :] + (0.125 * (x + w) + 0.75 * y)
+            q0[c, odd, :] = gain * q0[c, odd, :] + 0.5 * (y + w)
+            out_ref[pl.ds(2 * m, 2 * chunk), c * 128 : (c + 1) * 128] = q0[c, pl.ds(2 * m, 2 * chunk), :]
 
 
 def local(mesh_shape, heights, scene_ids, scene_offset, scene_weight, band_gain):
@@ -494,18 +490,18 @@
     sizes = (nr, nc, nx, ny, nz, rows_total, cols_total)
     ext = (nr + 2 * HALO, nc + 2 * SIDE)
     peers = nx + ny + nz - 3
-    smem = pl.BlockSpec(memory_space=pltpu.SMEM)
-    hbm = pl.BlockSpec(memory_space=pl.ANY)
-    z1, q0 = pl.pallas_call(
+    hbm = pl.BlockSpec(memory_space=pltpu.HBM)
+    return pl.pallas_call(
         functools.partial(kernel, sizes),
-        out_shape=(
-            jax.ShapeDtypeStruct((nr // 2 + 16, nc // 2 + 128), F32),
-            jax.ShapeDtypeStruct((nr, nc), F32),
-        ),
-        in_specs=[smem, smem, smem, hbm, hbm, hbm, hbm],
-        out_specs=(pl.BlockSpec(memory_space=pltpu.VMEM), hbm),
+        out_shape=pltpu.VMEM((nr, nc), F32),
+        in_specs=[hbm] * 7,
+        out_specs=pl.BlockSpec(memory_space=pltpu.VMEM),
         scratch_shapes=[
-            pltpu.VMEM((nr, nc), F32),
+            pltpu.SMEM(scene_offset.shape, F32),
+            pltpu.SMEM(scene_weight.shape, F32),
+            pltpu.SMEM(band_gain.shape, F32),
+            pltpu.VMEM((nc // 128, nr // 2 + 16, 128), F32),
+            pltpu.VMEM((nc // 128, nr, 128), F32),
             pltpu.VMEM(ext, F32),
             pltpu.VMEM(ext, jnp.int32),
             pltpu.VMEM((1, nr), F32),
@@ -517,7 +513,7 @@
             pltpu.VMEM((3, nr // 8 + 2 * EDGE3, nc // 4), F32),
             pltpu.VMEM((3, 8, 128), F32),
             pltpu.VMEM((peers, 8, 128), F32),
-            pltpu.SemaphoreType.DMA((5,)),
+            pltpu.SemaphoreType.DMA((7,)),
             pltpu.SemaphoreType.DMA((16,)),
             pltpu.SemaphoreType.DMA((16,)),
             pltpu.SemaphoreType.DMA((8,)),
@@ -527,18 +523,6 @@
         ],
         compiler_params=pltpu.CompilerParams(collective_id=0, has_side_effects=True),
     )(scene_offset, scene_weight, band_gain, heights, scene_ids, u, v)
-    vmem = pl.BlockSpec(memory_space=pltpu.VMEM)
-    return pl.pallas_call(
-        last,
-        out_shape=jax.ShapeDtypeStruct((nr, nc), F32),
-        in_specs=[smem, vmem, hbm],
-        out_specs=hbm,
-        scratch_shapes=[
-            pltpu.VMEM((nr, nc), F32),
-            pltpu.VMEM((nr, nc), F32),
-            pltpu.SemaphoreType.DMA((8,)),
-        ],
-    )(band_gain, z1, q0)
 
 
 def solution(mesh):

time: 27.1 us -> 25.1 us (0.926)
  Pallas kernels: 26.9 us -> 23.9 us
  local copies, waits for them, and re-layouts: 0 us -> 0.97 us
    pallas_call x2 -> x1, Pallas kernels: 26.9 us -> 23.9 us  [local(): pl.pallas_call(functools.partial(kernel, sizes), out_shape=pltpu.VMEM((nr...]
    unnamed x0 -> x1, local copies, waits for them, and re-layouts: none -> 0.97 us
where the time goes in v1:
time: 25.1 us; the launch traced here: 24.9 us
  Pallas kernels  23.9 us (95%)
  local copies, waits for them, and re-layouts  0.97 us (4%)
    pallas_call x1, Pallas kernels, local(): pl.pallas_call(functools.partial(kernel, sizes), out_shape=pltpu.VMEM((nr...  23.9 us
    unnamed x1, local copies, waits for them, and re-layouts  0.97 us

profile of v1, /device:TPU:0, one launch (start us, length us, event | category | flops | bytes accessed | tf_op | source)
XLA Modules:
  0.0 24.9 jit_solution(8323753825923011624)
XLA Ops:
  0.0 23.9 %shard_map.73 = f32[512,512]{1,0:T(8,128)S(1)} custom-call(f32[16]{0:T(128)} %off_hbm.1, f32[16]{0:T(128)} %wgt_hbm.1, f32[6]{0:T(128)} %gain_hbm.1, f32[512,512]{1,0:T(8,128)} %h_ref.1, s32[512,512]{1,0:T(8,128)} %s_ref.1, f32[16,1,512]{2,1,0:T(1,128)} %constant.4.clone.u_ref, f32[2,1,512]{2,1,0:T(1,128)} %constant.5.clone.v_ref), custom_call_target="tpu_custom_call" | custom-call | tf_op jit(solution)/shard_map/pallas_call | solution.py:494
  23.9 1.0 %copy.9 = f32[512,512]{1,0:T(8,128)} copy(f32[512,512]{1,0:T(8,128)S(1)} %shard_map.73) | data formatting | bytes 2097152

commit v2 on v1

v2 whole, which is shorter than its diff:
```python
import functools

import jax
import jax.numpy as jnp
import numpy as np
from jax import lax
from jax.experimental import pallas as pl
from jax.experimental.pallas import tpu as pltpu
from jax.sharding import PartitionSpec as P

F32, BF16 = jnp.float32, jnp.bfloat16
FAR = 1 << 20
HALO = 16
LANES = 128
LEVELS = 6
UP3, DOWN3 = 32, 32


def reach(count, levels):
    weights = np.ones(count >> levels, np.float64)
    for _ in range(levels):
        fine = np.zeros(2 * weights.size + 4, np.float64)
        for tap, value in zip(range(-2, 3), (0.0625, 0.25, 0.375, 0.25, 0.0625)):
            fine[2 + tap : 2 + tap + 2 * weights.size : 2] += value * weights
        weights = fine[2:-2]
    return weights


class Axis:
    def __init__(self, n, at, count):
        self.n, self.at, self.count = n, at, count

    def inside(self, index, level):
        place = index + self.at * (self.n >> level)
        return (place >= 0) & (place < self.count * (self.n >> level))

    def shrink(self, fine, coarse, level):
        far = np.abs(fine[:, None] - 2 * coarse[None, :])
        value = np.select([far == 0, far == 1, far == 2], [0.375, 0.25, 0.0625], 0.0)
        return value * self.inside(coarse, level)[None, :]

    def grow(self, coarse, fine, level):
        far = np.abs(2 * coarse[:, None] - fine[None, :])
        value = np.select([far == 0, far == 1, far == 2], [0.75, 0.5, 0.125], 0.0)
        return value * self.inside(fine, level)[None, :]

    def window(self, level, edge):
        return np.arange(-edge, (self.n >> level) + edge)

    def deep(self, lanes):
        out = self.out()
        w4, w5 = self.window(4, 30), self.window(5, 14)
        to4 = self.shrink(lanes, w4, 4)
        to5 = to4 @ self.shrink(w4, w5, 5)
        same = (lanes[:, None] == out[0][None, :]) * self.inside(out[0], 3)[None, :]
        parts = [
            same * 1.0,
            self.shrink(lanes, out[1], 4),
            to4 @ self.shrink(w4, out[2], 5),
            to5 @ self.shrink(w5, out[3], 6),
        ]
        return np.concatenate(parts, axis=1) * self.inside(lanes, 3)[:, None]

    def out(self):
        low = -4
        return [low + np.arange(size) for size in self.sizes()]

    def sizes(self):
        return [self.n // 8 + 8, self.n // 16 + 8, self.n // 32 + 8, self.n // 64 + 16]

    def back(self):
        o3, o4, o5, o6 = self.out()
        w4, w5 = self.window(4, 4), self.window(5, 4)
        from4 = self.grow(w4, o3, 3)
        from5 = self.grow(w5, w4, 4) @ from4
        parts = [
            np.eye(o3.size) * self.inside(o3, 3)[None, :],
            self.grow(o4, o3, 3),
            self.grow(o5, w4, 4) @ from4,
            self.grow(o6, w5, 5) @ from5,
        ]
        ones = self.inside(o6, 6) @ parts[3]
        return np.concatenate(parts, axis=0), ones

    def sums(self):
        weights = reach(self.count * (self.n >> 3), LEVELS - 3)
        place = self.out()[0] + self.at * (self.n >> 3)
        ok = (place >= 0) & (place < weights.size)
        return np.where(ok, weights[np.clip(place, 0, weights.size - 1)], 0.0)


def pad(x, shape):
    return np.pad(x, [(0, size - have) for size, have in zip(shape, x.shape)])


def halves(x):
    high = x.astype(np.float32).astype(jnp.bfloat16)
    low = (x - high.astype(np.float64)).astype(np.float32).astype(jnp.bfloat16)
    return high, low


def edged(n, low, size):
    ends = np.concatenate([np.arange(-4, 0), n + np.arange(4)])
    return np.concatenate([np.arange(n), ends, np.full(size - n - 8, FAR)]) + low


def col_tables(n, at, count):
    ax = Axis(n, at, count)
    if count == 2:
        sides = [1 if at == 0 else -1]
    else:
        sides = [-1, 1]
    lane = np.arange(LANES)
    own = np.arange(n)
    side = [lane - LANES if d < 0 else n + lane for d in sides]
    near = [lane if d < 0 else n - LANES + lane for d in sides]
    out1 = edged(n // 2, 0, n // 2 + LANES)
    out2 = edged(n // 4, 0, n // 4 + LANES)
    w1, w2 = ax.window(1, 16), ax.window(2, 8)
    c0 = ax.shrink(own, out1[: n // 2], 1)
    extra = []
    for k in range(len(sides)):
        block = np.concatenate(
            [ax.shrink(side[k], out1, 1), ax.shrink(near[k], out1, 1) * (out1 != out1.clip(0, n // 2 - 1))],
            axis=0,
        )
        extra.append(block)
    extra = np.concatenate(extra, axis=0)
    raw = np.concatenate([own] + side)
    c01 = ax.shrink(raw, w1, 1) @ ax.shrink(w1, out2, 2)
    o3 = ax.out()[0]
    c03 = ax.shrink(own, w1, 1) @ ax.shrink(w1, w2, 2) @ ax.shrink(w2, o3, 3)
    c03 = np.concatenate([pad(x.astype(np.float64), (n, LANES)) for x in halves(c03)], axis=1)
    three = np.concatenate([o3, np.full(LANES - o3.size, FAR)])
    sources = np.concatenate([three] + [three + d * (n // 8) for d in sides])
    stack = sum(ax.sizes())
    call = np.stack([pad(x.astype(np.float64), (sources.size, 256)) for x in halves(ax.deep(sources))])
    back, ones = ax.back()
    ec = np.stack([pad(x.astype(np.float64), (256, LANES)) for x in halves(back)])
    return dict(
        c0=c0, extra=extra, c01=c01, c03=c03, call=call, ec=ec,
        e2=ax.grow(three, out2, 2), e1=ax.grow(out2, out1, 1), e0=ax.grow(out1, own, 0),
    ), pad(ones[None], (1, LANES)), pad(ax.sums()[None], (1, LANES))


def row_tables(n, at, count):
    ax = Axis(n, at, count)
    o3 = ax.out()[0]
    t = n // 8
    rows = np.concatenate([o3[-UP3:] - t, o3, o3[:DOWN3] + t])
    deep = ax.deep(rows).T
    high, low = (x.astype(np.float64) for x in halves(deep))
    size6 = ax.sizes()[3]
    rall = np.concatenate([high, low[-size6:]], axis=0)
    rall = pad(rall, (-(-rall.shape[0] // 16) * 16, -(-rows.size // 16) * 16))
    back, ones = ax.back()
    er = np.stack([x.astype(np.float64) for x in halves(back.T)])
    return dict(rall=rall, er=er), ones[:, None], ax.sums()[:, None]


def tables(nr, nc, nx, blocks):
    def places(count):
        return (0, 1) if count == 2 else (0, 1, count - 1)

    cols = [col_tables(nc, at, nx) for at in places(nx)]
    rows = [row_tables(nr, at, blocks) for at in places(blocks)]

    def cast(x):
        return jnp.asarray(np.asarray(x, np.float32)).astype(BF16)

    by_col = {k: cast(np.stack([c[0][k] for c in cols])) for k in cols[0][0]}
    by_row = {k: cast(np.stack([r[0][k] for r in rows])) for k in rows[0][0]}
    both = np.stack([np.stack([np.stack([r[i] * c[i] for i in (1, 2)]) for c in cols]) for r in rows])
    return by_col, by_row, jnp.asarray(both.astype(np.float32))


def split(x):
    high = x.astype(BF16)
    return high, (x - high.astype(F32)).astype(BF16)


def dot(a, b):
    return jnp.dot(a, b, preferred_element_type=F32)


def right(x, c):
    high, low = split(x)
    return dot(high, c) + dot(low, c)


COLS = ("c03", "c0", "extra", "c01", "call", "ec", "e2", "e1", "e0")
ROWS = ("rall", "er")
CHUNKS = 4


def kernel(
    sizes, off_hbm, wgt_hbm, gain_hbm, h_ref, s_ref, *rest
):
    nr, nc, nx, ny, nz, ns = sizes
    names = COLS + ROWS + ("both",)
    tables_hbm, rest = dict(zip(names, rest)), rest[len(names):]
    out_ref, rest = rest[0], rest[1:]
    tab, rest = dict(zip(names, rest)), rest[len(names):]
    (
        off_ref, wgt_ref, gain_ref, h_buf, s_buf, q0, num, den, n1, d1, n2, d2, n3, d3,
        b3, z3b, z2b, z1b, wide, part, slots,
        own_sem, tab_sem, send0, recv0, send3, recv3, psend, precv,
    ) = rest
    cx, cy, cz = lax.axis_index("gx"), lax.axis_index("gy"), lax.axis_index("gz")
    row = cy * nz + cz
    blocks = ny * nz
    own_tiles = nc // LANES
    t3 = nr // 8
    m3 = t3 + 8

    def kind(at, count):
        return at if count == 2 else jnp.where(at == 0, 0, jnp.where(at == count - 1, 2, 1))

    ct, rt = kind(cx, nx), kind(row, blocks)

    loads = []
    step = nr // CHUNKS
    for k in range(CHUNKS):
        rows = pl.ds(k * step, step)
        for a, (src, dst) in enumerate(((h_ref, h_buf), (s_ref, s_buf))):
            loads.append(
                pltpu.make_async_copy(
                    src.at[rows, :],
                    dst.at[pl.ds(HALO + k * step, step), pl.ds(0, nc)],
                    own_sem.at[2 * k + a],
                )
            )
    small = [
        pltpu.make_async_copy(src, dst, own_sem.at[2 * CHUNKS + a])
        for a, (src, dst) in enumerate(((off_hbm, off_ref), (wgt_hbm, wgt_ref), (gain_hbm, gain_ref)))
    ]
    fetch = {}
    for i, name in enumerate(names):
        src = tables_hbm[name]
        src = src.at[ct] if name in COLS else src.at[rt] if name in ROWS else src.at[rt, ct]
        fetch[name] = pltpu.make_async_copy(src, tab[name], tab_sem.at[i])
    for copy in loads[:2] + small + loads[2:]:
        copy.start()

    up, down = row > 0, row < blocks - 1
    send_row, recv_row = {0: None, 1: down, 2: up}, {0: None, 1: up, 2: down}
    if ns == 1:
        send_col, recv_col = {0: None, 1: None}, {0: None, 1: None}
        to_col = {0: cx, 1: 1 - cx}
        src_col = {1: pl.multiple_of((1 - cx) * (nc - LANES), LANES)}
        near_tile = {1: (1 - cx) * (own_tiles - 1)}
    else:
        send_col = {0: None, 1: cx < nx - 1, 2: cx > 0}
        recv_col = {0: None, 1: cx > 0, 2: cx < nx - 1}
        to_col = {0: cx, 1: cx + 1, 2: cx - 1}
        src_col = {1: nc - LANES, 2: 0}
        near_tile = {1: 0, 2: own_tiles - 1}
    kinds = [(rp, cp) for rp in (0, 1, 2) for cp in range(1 + ns) if rp or cp]

    def device(rp, cp):
        target = row + {0: 0, 1: 1, 2: -1}[rp]
        return {"gx": to_col[cp], "gy": target // nz, "gz": target % nz}

    def also(a, b):
        return b if a is None else a if b is None else jnp.logical_and(a, b)

    def sends(rp, cp):
        return also(send_row[rp], send_col[cp])

    def comes(rp, cp):
        return also(recv_row[rp], recv_col[cp])

    def given(flag, body):
        if flag is None:
            body()
        else:
            pl.when(flag)(body)

    axes = (("gx", nx, cx), ("gz", nz, cz), ("gy", ny, cy))
    barrier = pltpu.get_barrier_semaphore()
    for d in kinds:
        given(sends(*d), lambda: pl.semaphore_signal(barrier, inc=1, device_id=device(*d)))
    for name, count, me in axes:
        for s in range(1, count):
            pl.semaphore_signal(barrier, inc=1, device_id={name: (me + s) % count})

    for copy in fetch.values():
        copy.start()

    zero = jnp.zeros((HALO, LANES), F32)
    for x in (num, den):
        for c in range(own_tiles + ns):
            x[c, 0:HALO, :] = zero
            x[c, nr + HALO : nr + 2 * HALO, :] = zero
            x[c, nr + 2 * HALO :, :] = zero
    zero = jnp.zeros((8, LANES), F32)
    for x in (n1, d1, n2, d2):
        for c in range(own_tiles + ns):
            x[c, 0:8, :] = zero
            x[c, x.shape[1] - 8 :, :] = zero
    z3b[m3:, :] = zero
    for k in range(1 + ns):
        for a in range(2):
            b3[k, a, UP3 + m3 + DOWN3 :, :] = zero

    def rim(i, a):
        rp, cp = kinds[i]
        src, dst = ((h_ref, h_buf), (s_ref, s_buf))[a]
        rs = {0: (0, HALO, nr), 1: (nr - HALO, 0, HALO), 2: (0, nr + HALO, HALO)}[rp]
        cs = (0, 0, nc) if cp == 0 else (src_col[cp], nc + (cp - 1) * LANES, LANES)
        return pltpu.make_async_remote_copy(
            src_ref=src.at[pl.ds(rs[0], rs[2]), pl.ds(cs[0], cs[2])],
            dst_ref=dst.at[pl.ds(rs[1], rs[2]), pl.ds(cs[1], cs[2])],
            send_sem=send0.at[2 * i + a],
            recv_sem=recv0.at[2 * i + a],
            device_id=device(rp, cp),
        )

    def rim3(i):
        rp, cp = kinds[i]
        rs = {0: (UP3, UP3, m3), 1: (UP3 + m3 - UP3, 0, UP3), 2: (UP3, UP3 + m3, DOWN3)}[rp]
        return pltpu.make_async_remote_copy(
            src_ref=b3.at[0, :, pl.ds(rs[0], rs[2]), :],
            dst_ref=b3.at[cp, :, pl.ds(rs[1], rs[2]), :],
            send_sem=send3.at[i],
            recv_sem=recv3.at[i],
            device_id=device(rp, cp),
        )

    lane8 = lax.broadcasted_iota(jnp.int32, (8, LANES), 1)
    line8 = lax.broadcasted_iota(jnp.int32, (8, LANES), 0)

    def spread(table):
        line = jnp.zeros((8, LANES), F32)
        for i in range(table.shape[0]):
            line = jnp.where(lane8 == i, table[i], line)
        return line

    for copy in small:
        copy.wait()
    wgt_row, off_row = spread(wgt_ref), spread(off_ref)

    def level0(base, count, c):
        rows = pl.ds(base, count)
        ids = s_buf[rows, c * LANES : (c + 1) * LANES]

        def look(table):
            return jnp.concatenate(
                [jnp.take_along_axis(table, ids[r : r + 8], axis=1) for r in range(0, count, 8)], axis=0
            )

        weight = look(wgt_row)
        moved = h_buf[rows, c * LANES : (c + 1) * LANES] + look(off_row)
        num[c, rows, :] = weight * moved
        den[c, rows, :] = weight
        return moved

    near = sum(jnp.int32(1) if comes(*d) is None else comes(*d).astype(jnp.int32) for d in kinds)

    def meet():
        pl.semaphore_wait(barrier, near + (nx + ny + nz - 3))
        for i, d in enumerate(kinds):
            @functools.partial(given, sends(*d))
            def _():
                for a in range(2):
                    rim(i, a).start()

    meet()

    inner = 32
    for k in range(CHUNKS):
        with jax.named_scope("level0_%d" % k):
            loads[2 * k].wait()
            loads[2 * k + 1].wait()

            def some(i, carry):
                base = pl.multiple_of(HALO + k * step + i * inner, 16)
                for c in range(own_tiles):
                    q0[c, pl.ds(base - HALO, inner), :] = level0(base, inner, c)
                return carry

            lax.fori_loop(0, step // inner, some, 0)


    def taps(src, c, start, count):
        x = [src[c, pl.ds(start + a, count, stride=2), :] for a in range(-2, 3)]
        return 0.375 * x[2] + (0.25 * (x[1] + x[3]) + 0.0625 * (x[0] + x[4]))

    def hold(x, c, p, first):
        if first:
            ok = jnp.logical_or(line8 >= 4, up)
        else:
            ok = jnp.logical_or(line8 < 4, down)
        x[c, p : p + 8, :] = jnp.where(ok, x[c, p : p + 8, :], 0.0)

    last1, last2 = nr // 2 + 8, nr // 4 + 8

    def ends1(x, c):
        hold(x, c, 8, True)
        hold(x, c, last1, False)

    def ends2(x, c):
        hold(x, c, 8, True)
        hold(x, c, last2, False)

    def rows1(src, dst, c, p, count):
        dst[c, p : p + count, :] = taps(src, c, 2 * p - 8, count)

    def rows2(src, dst, c, p, count):
        dst[c, p : p + count, :] = taps(src, c, 2 * p - 12, count)

    with jax.named_scope("rowpyr"):
        for src, one, two, three in ((num, n1, n2, n3), (den, d1, d2, d3)):
            for c in range(own_tiles):
                rows1(src, one, c, 8, nr // 2 + 16)
                ends1(one, c)
                rows2(one, two, c, 8, nr // 4 + 8)
                ends2(two, c)
                three[c] = taps(two, c, 4, m3)

    def wide_of(x, rows, tiles):
        return jnp.concatenate([x[c, rows, :] for c in tiles], axis=1)

    own_range = range(own_tiles)
    with jax.named_scope("p3"):
        fetch["c03"].wait()
        x = jnp.concatenate([wide_of(n3, slice(None), own_range), wide_of(d3, slice(None), own_range)], axis=0)
        x = right(x, tab["c03"][...])
        x = x[:, :LANES] + x[:, LANES:]
        b3[0, 0, UP3 : UP3 + m3, :] = x[:m3]
        b3[0, 1, UP3 : UP3 + m3, :] = x[m3:]
        for i, d in enumerate(kinds):
            given(sends(*d), lambda: rim3(i).start())
        fetch["both"].wait()
        reach3 = tab["both"][1]
        sum_n, sum_d = jnp.sum(x[:m3] * reach3), jnp.sum(x[m3:] * reach3)
        part[0] = jnp.where(line8 == 0, sum_n, jnp.where(line8 == 1, sum_d, 0.0))

    starts = (0, nx - 1, nx + nz - 2)

    def phase(k):
        name, count, me = axes[k]
        return [
            pltpu.make_async_remote_copy(
                src_ref=part.at[k],
                dst_ref=slots.at[starts[k] + s - 1],
                send_sem=psend.at[starts[k] + s - 1],
                recv_sem=precv.at[starts[k] + s - 1],
                device_id={name: (me + s) % count},
            )
            for s in range(1, count)
        ]

    def finish(k):
        total = part[k]
        for s, copy in enumerate(phase(k)):
            copy.wait()
            total = total + slots[starts[k] + s]
        return total

    for copy in phase(0):
        copy.start()

    def take(i):
        @functools.partial(given, sends(*kinds[i]))
        def _():
            for a in range(2):
                rim(i, a).wait_send()

        @functools.partial(given, comes(*kinds[i]))
        def _():
            for a in range(2):
                rim(i, a).wait_recv()

    with jax.named_scope("w_side"):
        for i, d in enumerate(kinds):
            if d[0] == 0:
                take(i)

    def cleared(c, base, count):
        for x in (num, den):
            x[c, pl.ds(base, count), :] = jnp.zeros((count, LANES), F32)

    with jax.named_scope("side"):
        for k in range(1, 1 + ns):
            c = own_tiles + k - 1

            def side():
                def some(i, carry):
                    level0(pl.multiple_of(HALO + i * inner, 16), inner, c)
                    return carry

                lax.fori_loop(0, nr // inner, some, 0)

            given(recv_col[k], side)
            if recv_col[k] is not None:
                pl.when(jnp.logical_not(recv_col[k]))(lambda: cleared(c, HALO, nr))

    with jax.named_scope("w_phase0"):
        part[1] = finish(0)
        for copy in phase(1):
            copy.start()

    with jax.named_scope("w_rims"):
        for i, d in enumerate(kinds):
            if d[0] != 0:
                take(i)
    with jax.named_scope("rims"):
        for rp, base in ((1, 0), (2, nr + HALO)):
            for cp in range(1 + ns):
                tiles = own_range if cp == 0 else (own_tiles + cp - 1,)

                def edge():
                    for c in tiles:
                        level0(base, HALO, c)

                given(comes(rp, cp), edge)

        for src, one, two in ((num, n1, n2), (den, d1, d2)):
            for c in range(own_tiles + ns):
                if c < own_tiles:
                    rows1(src, one, c, 8, 8)
                    rows1(src, one, c, last1, 16)
                else:
                    rows1(src, one, c, 8, nr // 2 + 16)
                ends1(one, c)
                if c < own_tiles:
                    rows2(one, two, c, 8, 8)
                    rows2(one, two, c, last2, 8)
                else:
                    rows2(one, two, c, 8, nr // 4 + 8)
                ends2(two, c)

    def ratio(n, d):
        return jnp.where(d > 0, n / d, 0.0)

    all_range = range(own_tiles + ns)
    body1, body2 = slice(8, nr // 2 + 24), slice(8, nr // 4 + 24)

    def level1(x):
        edge = jnp.concatenate(
            [y for k in range(1, 1 + ns) for y in (x[own_tiles + k - 1, body1, :], x[near_tile[k], body1, :])],
            axis=1,
        )
        own = right(wide_of(x, body1, own_range), tab["c0"][...])
        edge = right(edge, tab["extra"][...])
        half = nc // 2
        return jnp.concatenate([own + edge[:, :half], edge[:, half:]], axis=1)

    with jax.named_scope("q1"):
        fetch["c0"].wait()
        fetch["extra"].wait()
        q1 = ratio(level1(n1), level1(d1))
    with jax.named_scope("q2"):
        fetch["c01"].wait()
        q2 = ratio(
            right(wide_of(n2, body2, all_range), tab["c01"][...]),
            right(wide_of(d2, body2, all_range), tab["c01"][...]),
        )

    with jax.named_scope("w_phase1"):
        part[2] = finish(1)
        for copy in phase(2):
            copy.start()

    with jax.named_scope("w_b3"):
        for i, d in enumerate(kinds):
            given(sends(*d), lambda: rim3(i).wait_send())
            given(comes(*d), lambda: rim3(i).wait_recv())
        for i, (rp, cp) in enumerate(kinds):
            flag = comes(rp, cp)
            if flag is not None:
                rs = {0: (UP3, m3), 1: (0, UP3), 2: (UP3 + m3, DOWN3)}[rp]

                def clear():
                    b3[cp, :, rs[0] : rs[0] + rs[1], :] = jnp.zeros((2, rs[1], LANES), F32)

                pl.when(jnp.logical_not(flag))(clear)
        for name in ("call", "ec", "e2", "e1", "e0", "rall", "er"):
            fetch[name].wait()

    s3, s4, s5, s6 = (nr // 8 + 8, nr // 16 + 8, nr // 32 + 8, nr // 64 + 16)
    stack = s3 + s4 + s5 + s6
    with jax.named_scope("deep"):
        packed = []
        for a in range(2):
            x = jnp.concatenate([b3[k, a] for k in range(1 + ns)], axis=1)
            high, low = split(x)
            rall = tab["rall"][...]
            x = dot(rall, high) + dot(rall, low)
            packed += [x[: stack - s6], x[stack - s6 : stack] + x[stack : stack + s6]]
        high, low = split(jnp.concatenate(packed, axis=0))
        x = dot(high, tab["call"][0]) + dot(low, tab["call"][0]) + dot(high, tab["call"][1])

        def level_of(shape, dim, cuts):
            index = lax.broadcasted_iota(jnp.int32, shape, dim)
            return sum((index >= cut).astype(jnp.int32) for cut in cuts)

        c3, c4, c5 = nc // 8 + 8, nc // 16 + 8, nc // 32 + 8
        shape = (stack, 256)
        at_row = level_of(shape, 0, (s3, s3 + s4, s3 + s4 + s5))
        at_col = level_of(shape, 1, (c3, c3 + c4, c3 + c4 + c5))
        gains = [gain_ref[level] - gain_ref[level - 1] for level in (3, 4, 5)] + [-gain_ref[5]]
        factor = jnp.where(
            at_row == 0, gains[0], jnp.where(at_row == 1, gains[1], jnp.where(at_row == 2, gains[2], gains[3]))
        )
        d = x[stack:]
        x = jnp.where(jnp.logical_and(at_row == at_col, d > 0), factor * (x[:stack] / d), 0.0)
        high, low = split(x)
        er = tab["er"]
        x = dot(er[0], high) + dot(er[0], low) + dot(er[1], high)
        high, low = split(x)
        ec = tab["ec"]
        z3 = dot(high, ec[0]) + dot(low, ec[0]) + dot(high, ec[1])

    with jax.named_scope("w_phase2"):
        total = finish(2)
    with jax.named_scope("z2"):
        top_sum = jnp.sum(jnp.where(line8 == 0, total, 0.0), axis=0, keepdims=True)
        top_weight = jnp.sum(jnp.where(line8 == 1, total, 0.0), axis=0, keepdims=True)
        top_mean = top_sum / top_weight
        z3b[0:m3, :] = z3 + top_mean * tab["both"][0]

        def grow_rows(src, dst, put, get, count):
            x, y, w = (src[get + (slice(k, k + count), slice(None))] for k in (1, 2, 3))
            dst[put + (pl.ds(0, count, stride=2), slice(None))] = 0.125 * (x + w) + 0.75 * y
            dst[put + (pl.ds(1, count, stride=2), slice(None))] = 0.5 * (y + w)

        def block(x, put, p, first):
            ok = jnp.logical_or(line8 >= 4, up) if first else jnp.logical_or(line8 < 4, down)
            x[put + (slice(p, p + 8), slice(None))] = jnp.where(ok, x[put + (slice(p, p + 8), slice(None))], 0.0)

        grow_rows(z3b, z2b, (0,), (), nr // 8 + 8)
        block(z2b, (0,), 0, True)
        block(z2b, (0,), nr // 4, False)
        z2 = right(z2b[0], tab["e2"][...]) + (gain_ref[2] - gain_ref[1]) * q2
        tiles2 = z2.shape[1] // LANES
        for c in range(tiles2):
            z2b[c] = z2[:, c * LANES : (c + 1) * LANES]
    with jax.named_scope("z1"):
        for c in range(tiles2):
            grow_rows(z2b, z1b, (c,), (c,), nr // 4 + 8)
            block(z1b, (c,), 0, True)
            block(z1b, (c,), nr // 2, False)
        z1 = right(wide_of(z1b, slice(None), range(tiles2)), tab["e1"][...]) + (gain_ref[1] - gain_ref[0]) * q1
    with jax.named_scope("e0"):
        full = right(z1, tab["e0"][...])
        for c in own_range:
            wide[c] = full[:, c * LANES : (c + 1) * LANES]
    with jax.named_scope("out"):
        gain = gain_ref[0]
        chunk = 32
        for c in own_range:
            for m in range(0, nr // 2, chunk):
                x, y, w = (wide[c, pl.ds(m + k, chunk), :] for k in (3, 4, 5))
                even, odd = pl.ds(2 * m, chunk, stride=2), pl.ds(2 * m + 1, chunk, stride=2)
                q0[c, even, :] = gain * q0[c, even, :] + (0.125 * (x + w) + 0.75 * y)
                q0[c, odd, :] = gain * q0[c, odd, :] + 0.5 * (y + w)
                out_ref[pl.ds(2 * m, 2 * chunk), c * LANES : (c + 1) * LANES] = q0[c, pl.ds(2 * m, 2 * chunk), :]


def local(mesh_shape, heights, scene_ids, scene_offset, scene_weight, band_gain):
    nx, ny, nz = mesh_shape
    nr, nc = heights.shape
    ns = 1 if nx == 2 else 2
    by_col, by_row, both = tables(nr, nc, nx, ny * nz)
    given = [by_col[k] for k in COLS] + [by_row[k] for k in ROWS] + [both]
    skip = [1] * len(COLS) + [1] * len(ROWS) + [2]
    sizes = (nr, nc, nx, ny, nz, ns)
    ext = (nr + 2 * HALO, nc + ns * LANES)
    own_tiles = nc // LANES
    tiles = own_tiles + ns
    m3 = nr // 8 + 8
    rows_b = -(-(UP3 + m3 + DOWN3) // 16) * 16
    if rows_b == UP3 + m3 + DOWN3:
        rows_b += 16
    peers = nx + ny + nz - 3
    messages = 3 * (1 + ns) - 1
    hbm = pl.BlockSpec(memory_space=pltpu.HBM)
    return pl.pallas_call(
        functools.partial(kernel, sizes),
        out_shape=pltpu.VMEM((nr, nc), F32),
        in_specs=[hbm] * (5 + len(given)),
        out_specs=pl.BlockSpec(memory_space=pltpu.VMEM),
        scratch_shapes=[pltpu.VMEM(x.shape[k:], x.dtype) for x, k in zip(given, skip)]
        + [
            pltpu.SMEM(scene_offset.shape, F32),
            pltpu.SMEM(scene_weight.shape, F32),
            pltpu.SMEM(band_gain.shape, F32),
            pltpu.VMEM(ext, F32),
            pltpu.VMEM(ext, jnp.int32),
            pltpu.VMEM((own_tiles, nr, LANES), F32),
        ]
        + [pltpu.VMEM((tiles, nr + 3 * HALO, LANES), F32)] * 2
        + [pltpu.VMEM((tiles, nr // 2 + 32, LANES), F32)] * 2
        + [pltpu.VMEM((tiles, nr // 4 + 24, LANES), F32)] * 2
        + [pltpu.VMEM((own_tiles, m3, LANES), F32)] * 2
        + [
            pltpu.VMEM((1 + ns, 2, rows_b, LANES), F32),
            pltpu.VMEM((m3 + 8, LANES), F32),
            pltpu.VMEM((nc // 4 // LANES + 1, nr // 4 + 16, LANES), F32),
            pltpu.VMEM((nc // 4 // LANES + 1, nr // 2 + 16, LANES), F32),
            pltpu.VMEM((own_tiles, nr // 2 + 16, LANES), F32),
            pltpu.VMEM((3, 8, LANES), F32),
            pltpu.VMEM((peers, 8, LANES), F32),
            pltpu.SemaphoreType.DMA((2 * CHUNKS + 3,)),
            pltpu.SemaphoreType.DMA((len(given),)),
            pltpu.SemaphoreType.DMA((2 * messages,)),
            pltpu.SemaphoreType.DMA((2 * messages,)),
            pltpu.SemaphoreType.DMA((messages,)),
            pltpu.SemaphoreType.DMA((messages,)),
            pltpu.SemaphoreType.DMA((peers,)),
            pltpu.SemaphoreType.DMA((peers,)),
        ],
        compiler_params=pltpu.CompilerParams(collective_id=0, has_side_effects=True),
    )(scene_offset, scene_weight, band_gain, heights, scene_ids, *given)


def solution(mesh):
    placed = (P(("gy", "gz"), "gx"), P(("gy", "gz"), "gx"), P(), P(), P())
    shape = tuple(mesh.shape[name] for name in ("gx", "gy", "gz"))
    return jax.shard_map(
        functools.partial(local, shape), mesh=mesh, in_specs=placed,
        out_specs=P(("gy", "gz"), "gx"), check_vma=False,
    )
```

time: 25.1 us -> 19.9 us (0.79)
  Pallas kernels: 23.9 us -> 18.8 us
    pallas_call x1, Pallas kernels: 23.9 us -> 18.8 us  [local(): pl.pallas_call(functools.partial(kernel, sizes), out_shape=pltpu.VMEM((nr...]
where the time goes in v2:
time: 19.9 us; the launch traced here: 19.8 us
  Pallas kernels  18.8 us (94%)
  local copies, waits for them, and re-layouts  0.97 us (5%)
    pallas_call x1, Pallas kernels, local(): pl.pallas_call(functools.partial(kernel, sizes), out_shape=pltpu.VMEM((nr...  18.8 us
    unnamed x1, local copies, waits for them, and re-layouts  0.97 us

profile of v2, /device:TPU:0, one launch (start us, length us, event | category | flops | bytes accessed | tf_op | source)
XLA Modules:
  0.0 19.8 jit_solution(3973162314471812964)
XLA Ops:
  0.0 18.8 %shard_map.163 = f32[512,512]{1,0:T(8,128)S(1)} custom-call(f32[16]{0:T(128)} %off_hbm.1, f32[16]{0:T(128)} %wgt_hbm.1, f32[6]{0:T(128)} %gain_hbm.1, f32[512,512]{1,0:T(8,128)} %h_ref.1, s32[512,512]{1,0:T(8,128)} %s_ref.1, bf16[2,512,256]{2,1,0:T(8,128)(2,1)} %constant.36.rest_0_, bf16[2,512,256]{2,1,0:T(8,128)(2,1)} %constant.37.rest_1_, ...), custom_call_target="tpu_custom_call" | custom-call | tf_op jit(solution)/shard_map/pallas_call | solution.py:680
  18.8 1.0 %copy.19 = f32[512,512]{1,0:T(8,128)} copy(f32[512,512]{1,0:T(8,128)S(1)} %shard_map.163) | data formatting | bytes 2097152

commit v3 on v2

v3 whole, which is shorter than its diff:
```python
import functools

import jax
import jax.numpy as jnp
import numpy as np
from jax import lax
from jax.experimental import pallas as pl
from jax.experimental.pallas import tpu as pltpu
from jax.sharding import PartitionSpec as P

F32, BF16 = jnp.float32, jnp.bfloat16
FAR = 1 << 20
HALO = 16
LANES = 128
LEVELS = 6
MIDDLE = (3, 4, 5)


def reach(count, levels):
    weights = np.ones(count >> levels, np.float64)
    for _ in range(levels):
        fine = np.zeros(2 * weights.size + 4, np.float64)
        for tap, value in zip(range(-2, 3), (0.0625, 0.25, 0.375, 0.25, 0.0625)):
            fine[2 + tap : 2 + tap + 2 * weights.size : 2] += value * weights
        weights = fine[2:-2]
    return weights


class Axis:
    def __init__(self, n, at, count):
        self.n, self.at, self.count = n, at, count

    def inside(self, index, level):
        place = index + self.at * (self.n >> level)
        return (place >= 0) & (place < self.count * (self.n >> level))

    def shrink(self, fine, coarse, level):
        far = np.abs(fine[:, None] - 2 * coarse[None, :])
        value = np.select([far == 0, far == 1, far == 2], [0.375, 0.25, 0.0625], 0.0)
        return value * self.inside(coarse, level)[None, :]

    def grow(self, coarse, fine, level):
        far = np.abs(2 * coarse[:, None] - fine[None, :])
        value = np.select([far == 0, far == 1, far == 2], [0.75, 0.5, 0.125], 0.0)
        return value * self.inside(fine, level)[None, :]

    def window(self, level, edge):
        return np.arange(-edge, (self.n >> level) + edge)

    def deep(self, lanes, shift=0):
        out = [x + shift * (self.n >> level) for level, x in zip((3, 4, 5, 6), self.out())]
        w4, w5 = self.window(4, 30), self.window(5, 14)
        to4 = self.shrink(lanes, w4, 4)
        to5 = to4 @ self.shrink(w4, w5, 5)
        same = (lanes[:, None] == out[0][None, :]) * self.inside(out[0], 3)[None, :]
        parts = [
            same * 1.0,
            self.shrink(lanes, out[1], 4),
            to4 @ self.shrink(w4, out[2], 5),
            to5 @ self.shrink(w5, out[3], 6),
        ]
        return np.concatenate(parts, axis=1) * self.inside(lanes, 3)[:, None]

    def out(self):
        low = -4
        return [low + np.arange(size) for size in self.sizes()]

    def sizes(self):
        return [self.n // 8 + 8, self.n // 16 + 8, self.n // 32 + 8, self.n // 64 + 16]

    def back(self):
        o3, o4, o5, o6 = self.out()
        w4, w5 = self.window(4, 4), self.window(5, 4)
        from4 = self.grow(w4, o3, 3)
        from5 = self.grow(w5, w4, 4) @ from4
        parts = [
            np.eye(o3.size) * self.inside(o3, 3)[None, :],
            self.grow(o4, o3, 3),
            self.grow(o5, w4, 4) @ from4,
            self.grow(o6, w5, 5) @ from5,
        ]
        return np.concatenate(parts, axis=0)

    def sums(self):
        return reach(self.count * self.n, LEVELS)[self.at * self.n : (self.at + 1) * self.n]

    def ones(self, level):
        x = self.inside(self.window(6, 4), 6) * 1.0
        for k in range(5, level - 1, -1):
            x = x @ self.grow(self.window(k + 1, 4), self.window(k, 4), k)
        return x


def pad(x, shape):
    return np.pad(x, [(0, size - have) for size, have in zip(shape, x.shape)])


def halves(x):
    high = x.astype(np.float32).astype(jnp.bfloat16)
    low = (x - high.astype(np.float64)).astype(np.float32).astype(jnp.bfloat16)
    return high, low


def spaced(n):
    size = -(-(n + 8) // LANES) * LANES
    return np.concatenate([np.arange(-4, n + 4), np.full(size - n - 8, FAR)])


def col_tables(n, at, count):
    ax = Axis(n, at, count)
    shifts = [1 if at == 0 else -1] if count == 2 else [1, -1]
    lane = np.arange(LANES)
    own = np.arange(n)
    out1, out2 = spaced(n // 2), spaced(n // 4)
    w1, w2 = ax.window(1, 16), ax.window(2, 8)
    middle = np.isin(lane, MIDDLE)[None, :]
    s1, s2 = [], []
    for d in shifts:
        near = n - LANES + lane if d > 0 else lane
        over1, over2 = (lane - 4 + (n >> level if d > 0 else 0) for level in (1, 2))
        s1.append(ax.shrink(near, over1, 1) * middle)
        s2.append(ax.shrink(near, w1, 1) @ ax.shrink(w1, over2, 2) * middle)
    s1, s2 = (np.stack([np.stack([x, np.roll(x, LANES // 2, 1)]) for x in y]) for y in (s1, s2))
    o3 = ax.out()[0]
    to2 = ax.shrink(own, w1, 1)
    c03 = to2 @ ax.shrink(w1, w2, 2) @ ax.shrink(w2, o3, 3)
    c03 = np.concatenate([pad(x.astype(np.float64), (n, LANES)) for x in halves(c03)], axis=1)
    three = np.concatenate([o3, np.full(LANES - o3.size, FAR)])
    call = []
    for d in [0] + shifts:
        call.append([pad(x.astype(np.float64), (LANES, 256)) for x in halves(ax.deep(three, d))])
    call = np.stack([np.concatenate([x[k] for x in call], axis=1) for k in range(2)])
    back = ax.back()
    ec = np.stack([pad(x.astype(np.float64), (256, LANES)) for x in halves(back)])
    return dict(
        c1=ax.shrink(own, out1, 1), c2=to2 @ ax.shrink(w1, out2, 2), s1=s1, s2=s2, c03=c03, call=call,
        ec=ec, e2=ax.grow(three, out2, 2), e1=ax.grow(out2, out1, 1), e0=ax.grow(out1, own, 0),
    ), dict(line=np.stack([ax.sums(), ax.ones(0)[4:-4]]))


def row_tables(n, at, count):
    ax = Axis(n, at, count)
    o3 = ax.out()[0]
    deep = ax.deep(o3).T
    high, low = (x.astype(np.float64) for x in halves(deep))
    size6 = ax.sizes()[3]
    rall = np.concatenate([high, low[-size6:]], axis=0)
    rall = pad(rall, (-(-rall.shape[0] // 16) * 16, o3.size))
    back = ax.back()
    er = np.stack([x.astype(np.float64) for x in halves(back.T)])
    first = np.repeat(ax.sums()[:, None], LANES, 1)
    second = np.repeat(pad(ax.ones(1), (n // 2 + 16,))[:, None], LANES, 1)
    return dict(rall=rall, er=er), dict(first=first, second=second)


def tables(nr, nc, nx, blocks):
    def places(count):
        return (0, 1) if count == 2 else (0, 1, count - 1)

    cols = [col_tables(nc, at, nx) for at in places(nx)]
    rows = [row_tables(nr, at, blocks) for at in places(blocks)]

    def cast(x):
        return jnp.asarray(np.asarray(x, np.float32)).astype(BF16)

    def keep(x):
        return jnp.asarray(np.asarray(x, np.float32))

    out = {}
    for some in (cols, rows):
        for k in some[0][0]:
            out[k] = cast(np.stack([x[0][k] for x in some]))
        for k in some[0][1]:
            out[k] = keep(np.stack([x[1][k] for x in some]))
    return out


def split(x):
    high = x.astype(BF16)
    return high, (x - high.astype(F32)).astype(BF16)


def dot(a, b):
    return jnp.dot(a, b, preferred_element_type=F32)


def right(x, c):
    high, low = split(x)
    return dot(high, c) + dot(low, c)


COLS = ("line", "c03", "call", "c1", "c2", "s1", "s2", "ec", "e2", "e1", "e0")
ROWS = ("first", "rall", "er", "second")
CHUNKS = 4


def kernel(
    sizes, off_hbm, wgt_hbm, gain_hbm, h_ref, s_ref, *rest
):
    nr, nc, nx, ny, nz, ns = sizes
    names = COLS + ROWS
    tables_hbm, rest = dict(zip(names, rest)), rest[len(names):]
    out_ref, rest = rest[0], rest[1:]
    tab, rest = dict(zip(names, rest)), rest[len(names):]
    (
        off_ref, wgt_ref, gain_ref, h_buf, s_buf, q0, num, den, n1, d1, n2, d2, n3, d3,
        x1, x2, g, y1, y2, side_s, side_r, edge_s, edge_r, z3b, z2b, z1b, wide, part, slots,
        own_sem, tab_sem, send0, recv0, psend, precv,
    ) = rest
    cx, cy, cz = lax.axis_index("gx"), lax.axis_index("gy"), lax.axis_index("gz")
    row = cy * nz + cz
    blocks = ny * nz
    own_tiles = nc // LANES
    t3 = nr // 8
    m3 = t3 + 8

    def kind(at, count):
        return at if count == 2 else jnp.where(at == 0, 0, jnp.where(at == count - 1, 2, 1))

    ct, rt = kind(cx, nx), kind(row, blocks)

    loads = []
    step = nr // CHUNKS
    for k in range(CHUNKS):
        rows = pl.ds(k * step, step)
        for a, (src, dst) in enumerate(((h_ref, h_buf), (s_ref, s_buf))):
            loads.append(
                pltpu.make_async_copy(
                    src.at[rows, :],
                    dst.at[pl.ds(HALO + k * step, step), pl.ds(0, nc)],
                    own_sem.at[2 * k + a],
                )
            )
    small = [
        pltpu.make_async_copy(src, dst, own_sem.at[2 * CHUNKS + a])
        for a, (src, dst) in enumerate(((off_hbm, off_ref), (wgt_hbm, wgt_ref), (gain_hbm, gain_ref)))
    ]
    fetch = {}
    for i, name in enumerate(names):
        src = tables_hbm[name]
        src = src.at[ct] if name in COLS else src.at[rt]
        fetch[name] = pltpu.make_async_copy(src, tab[name], tab_sem.at[i])
    early = ["first", "line"]
    for copy in loads[:2] + small + [fetch[name] for name in early] + loads[2:]:
        copy.start()

    up, down = row > 0, row < blocks - 1
    send_row, recv_row = {0: None, 1: down, 2: up}, {0: None, 1: up, 2: down}
    if ns == 1:
        send_col, recv_col = {0: None, 1: None}, {0: None, 1: None}
        to_col = {0: cx, 1: 1 - cx}
        near_tile = {1: (1 - cx) * (own_tiles - 1)}
        into1, into2 = {1: (1 - cx) * (x1.shape[1] - 1)}, {1: (1 - cx) * (x2.shape[1] - 1)}
    else:
        send_col = {0: None, 1: cx < nx - 1, 2: cx > 0}
        recv_col = {0: None, 1: cx > 0, 2: cx < nx - 1}
        to_col = {0: cx, 1: cx + 1, 2: cx - 1}
        near_tile = {1: own_tiles - 1, 2: 0}
        into1, into2 = {1: 0, 2: x1.shape[1] - 1}, {1: 0, 2: x2.shape[1] - 1}
    kinds = [(rp, cp) for rp in (0, 1, 2) for cp in range(1 + ns) if rp or cp]

    def device(rp, cp):
        target = row + {0: 0, 1: 1, 2: -1}[rp]
        return {"gx": to_col[cp], "gy": target // nz, "gz": target % nz}

    def also(a, b):
        return b if a is None else a if b is None else jnp.logical_and(a, b)

    def sends(rp, cp):
        return also(send_row[rp], send_col[cp])

    def comes(rp, cp):
        return also(recv_row[rp], recv_col[cp])

    def given(flag, body):
        if flag is None:
            body()
        else:
            pl.when(flag)(body)

    everyone = nx * blocks
    me = row * nx + cx

    def peer(s):
        other = (me + s) % everyone
        line = other // nx
        return {"gx": other % nx, "gy": line // nz, "gz": line % nz}

    barrier = pltpu.get_barrier_semaphore()

    def greet(s, carry):
        pl.semaphore_signal(barrier, inc=1, device_id=peer(s))
        return carry

    lax.fori_loop(1, everyone, greet, 0)

    for name, copy in fetch.items():
        if name not in early:
            copy.start()

    zero = jnp.zeros((HALO, LANES), F32)
    for x in (num, den):
        for c in range(own_tiles):
            x[c, 0:HALO, :] = zero
            x[c, nr + HALO : nr + 2 * HALO, :] = zero
            x[c, nr + 2 * HALO :, :] = zero
    zero = jnp.zeros((8, LANES), F32)
    for x in (n1, d1, n2, d2):
        for c in range(own_tiles):
            x[c, 0:8, :] = zero
            x[c, x.shape[1] - 8 :, :] = zero
    z3b[m3:, :] = zero

    def edge(i):
        rp, cp = kinds[i]
        if rp == 0:
            src, dst = side_s.at[cp - 1], side_r.at[cp - 1]
        elif cp == 0:
            src, dst = edge_s.at[rp - 1, 0], edge_r.at[rp - 1, 0]
        else:
            src, dst = edge_s.at[rp - 1, cp, pl.ds(0, 4)], edge_r.at[rp - 1, cp, pl.ds(0, 4)]
        return pltpu.make_async_remote_copy(
            src_ref=src, dst_ref=dst, send_sem=send0.at[i], recv_sem=recv0.at[i], device_id=device(rp, cp)
        )

    lane8 = lax.broadcasted_iota(jnp.int32, (8, LANES), 1)
    line8 = lax.broadcasted_iota(jnp.int32, (8, LANES), 0)

    def spread(table):
        line = jnp.zeros((8, LANES), F32)
        for i in range(table.shape[0]):
            line = jnp.where(lane8 == i, table[i], line)
        return line

    for copy in small:
        copy.wait()
    wgt_row = spread(wgt_ref)

    def tree(ids, table):
        values = [table[i] for i in range(table.shape[0])]
        bit = 1
        while len(values) > 1:
            mask = (ids & bit) != 0
            values = [jnp.where(mask, values[i + 1], values[i]) for i in range(0, len(values), 2)]
            bit *= 2
        return values[0]

    def level0(base, count, c):
        rows = pl.ds(base, count)
        ids = s_buf[rows, c * LANES : (c + 1) * LANES]
        weight = jnp.concatenate(
            [jnp.take_along_axis(wgt_row, ids[r : r + 8], axis=1) for r in range(0, count, 8)], axis=0
        )
        moved = h_buf[rows, c * LANES : (c + 1) * LANES] + tree(ids, off_ref)
        numer = weight * moved
        num[c, rows, :] = numer
        den[c, rows, :] = weight
        return moved, numer, weight

    def summary(s):
        return pltpu.make_async_remote_copy(
            src_ref=part,
            dst_ref=slots.at[s - 1],
            send_sem=psend.at[s - 1],
            recv_sem=precv.at[s - 1],
            device_id=peer(s),
        )

    def send_edges(wanted):
        for i, d in enumerate(kinds):
            if wanted(d):
                given(sends(*d), lambda: edge(i).start())

    with jax.named_scope("level0"):
        fetch["first"].wait()
        sums = [[0.0] * own_tiles, [0.0] * own_tiles]
        for k in range(CHUNKS):
            loads[2 * k].wait()
            loads[2 * k + 1].wait()
            weights = tab["first"][k * step : (k + 1) * step, :]
            for c in range(own_tiles):
                moved, numer, weight = level0(HALO + k * step, step, c)
                q0[c, k * step : (k + 1) * step, :] = moved
                for a, x in enumerate((numer, weight)):
                    x = (x * weights).reshape(step // 8, 8, LANES)
                    sums[a][c] = sums[a][c] + jnp.sum(x, axis=0)
        fetch["line"].wait()
        flat = []
        for a in range(2):
            x = sum(sums[a][c] * tab["line"][0:1, c * LANES : (c + 1) * LANES] for c in range(own_tiles))
            x = jnp.sum(x, axis=0, keepdims=True)
            flat.append(x + pltpu.roll(x, LANES // 2, axis=1))
        lane1 = lax.broadcasted_iota(jnp.int32, (1, LANES), 1)
        part[...] = jnp.where(lane1 < LANES // 2, flat[0], flat[1])

    with jax.named_scope("meet"):
        pl.semaphore_wait(barrier, everyone - 1)

    def tell(s, carry):
        summary(s).start()
        return carry

    lax.fori_loop(1, everyone, tell, 0)

    def taps(src, c, start, count):
        x = [src[c, pl.ds(start + a, count, stride=2), :] for a in range(-2, 3)]
        return 0.375 * x[2] + (0.25 * (x[1] + x[3]) + 0.0625 * (x[0] + x[4]))

    def hold(x, c, p, first):
        if first:
            ok = jnp.logical_or(line8 >= 4, up)
        else:
            ok = jnp.logical_or(line8 < 4, down)
        x[c, p : p + 8, :] = jnp.where(ok, x[c, p : p + 8, :], 0.0)

    last1, last2 = nr // 2 + 8, nr // 4 + 8

    def ends1(x, c):
        hold(x, c, 8, True)
        hold(x, c, last1, False)

    def ends2(x, c):
        hold(x, c, 8, True)
        hold(x, c, last2, False)

    def rows1(src, dst, c, p, count):
        dst[c, p : p + count, :] = taps(src, c, 2 * p - 8, count)

    def rows2(src, dst, c, p, count):
        dst[c, p : p + count, :] = taps(src, c, 2 * p - 12, count)

    with jax.named_scope("rowpyr"):
        for src, one, two, three in ((num, n1, n2, n3), (den, d1, d2, d3)):
            for c in range(own_tiles):
                rows1(src, one, c, 8, nr // 2 + 16)
                ends1(one, c)
                rows2(one, two, c, 8, nr // 4 + 8)
                ends2(two, c)
                three[c] = taps(two, c, 4, m3)

    def wide_of(x, rows, tiles):
        return jnp.concatenate([x[c, rows, :] for c in tiles], axis=1)

    own_range = range(own_tiles)
    size1, size2 = x1.shape[2], x2.shape[2]
    s3, s4, s5, s6 = (nr // 8 + 8, nr // 16 + 8, nr // 32 + 8, nr // 64 + 16)
    stack = s3 + s4 + s5 + s6
    tops = (0, s3, s3 + s4, s3 + s4 + s5)
    bottoms = tuple(top + (nr >> level) for top, level in zip(tops, (3, 4, 5, 6)))

    def level_of(shape, dim, cuts):
        index = lax.broadcasted_iota(jnp.int32, shape, dim)
        return sum((index >= cut).astype(jnp.int32) for cut in cuts)

    c3, c4, c5 = nc // 8 + 8, nc // 16 + 8, nc // 32 + 8
    lane_cuts = (c3, c3 + c4, c3 + c4 + c5)
    middle = jnp.logical_and(line8 >= MIDDLE[0], line8 <= MIDDLE[-1])

    def pack(n, d):
        return jnp.where(middle, n, pltpu.roll(d, 4, axis=0))

    def unpack(x):
        return jnp.where(middle, x, 0.0), jnp.where(middle, pltpu.roll(x, 4, axis=0), 0.0)

    def unpack_lanes(x):
        low = lax.broadcasted_iota(jnp.int32, x.shape, 1) < LANES // 2
        return jnp.where(low, x, 0.0), jnp.where(low, pltpu.roll(x, LANES // 2, axis=1), 0.0)

    with jax.named_scope("p3"):
        fetch["c03"].wait()
        fetch["rall"].wait()
        x = jnp.concatenate([wide_of(n3, slice(None), own_range), wide_of(d3, slice(None), own_range)], axis=0)
        x = right(x, tab["c03"][...])
        x = x[:, :LANES] + x[:, LANES:]
        high, low = split(jnp.concatenate([x[:m3], x[m3:]], axis=1))
        rall = tab["rall"][...]
        x = dot(rall, high) + dot(rall, low)
        x = jnp.concatenate([x[: stack - s6], x[stack - s6 : stack] + x[stack : stack + s6]], axis=0)
        fetch["call"].wait()
        high, low = split(jnp.concatenate([x[:, :LANES], x[:, LANES:]], axis=0))
        x = dot(high, tab["call"][0]) + dot(low, tab["call"][0]) + dot(high, tab["call"][1])

    base_g = size1 + size2

    with jax.named_scope("g_pack"):
        for c in range(2):
            index = lane8 + c * LANES
            for k in range(1 + ns):
                piece = [x[a * stack : (a + 1) * stack, k * 256 + c * LANES : k * 256 + (c + 1) * LANES] for a in (0, 1)]
                for a in range(2):
                    if k == 0:
                        g[a, c] = piece[a]
                    else:
                        side_s[k - 1, base_g + (2 * a + c) * stack : base_g + (2 * a + c + 1) * stack, :] = piece[a]
                for rp, firsts in ((1, bottoms), (2, tops)):
                    line = []
                    for a in range(2):
                        b = [piece[a][f : f + 8] for f in firsts]
                        line.append(
                            jnp.where(
                                index < lane_cuts[0], b[0],
                                jnp.where(index < lane_cuts[1], b[1], jnp.where(index < lane_cuts[2], b[2], b[3])),
                            )
                        )
                    edge_s[rp - 1, k, (5 if k == 0 else 2) + c] = pack(*line)

    body1, body2 = slice(8, 8 + size1), slice(8, 8 + size2)

    with jax.named_scope("x_side"):
        fetch["s1"].wait()
        fetch["s2"].wait()
        for k in range(1, 1 + ns):
            for base, n, d, body, name, at in (
                (0, n1, d1, body1, "s1", nr // 2), (size1, n2, d2, body2, "s2", nr // 4),
            ):
                x = right(n[near_tile[k], body, :], tab[name][k - 1, 0])
                x = x + right(d[near_tile[k], body, :], tab[name][k - 1, 1])
                side_s[k - 1, base : base + x.shape[0], :] = x
                edge_s[0, k, 0 if base == 0 else 1] = x[at : at + 8]
                edge_s[1, k, 0 if base == 0 else 1] = x[0:8]

    with jax.named_scope("x_own"):
        for n, d, body, name, dst, at, first in (
            (n1, d1, body1, "c1", x1, nr // 2, 0), (n2, d2, body2, "c2", x2, nr // 4, 3),
        ):
            fetch[name].wait()
            both = [right(wide_of(x, body, own_range), tab[name][...]) for x in (n, d)]
            for c in range(dst.shape[1]):
                both_c = [x[:, c * LANES : (c + 1) * LANES] for x in both]
                for a in range(2):
                    dst[a, c] = both_c[a]
                edge_s[0, 0, first + c] = pack(*(x[at : at + 8] for x in both_c))
                edge_s[1, 0, first + c] = pack(*(x[0:8] for x in both_c))

    with jax.named_scope("send"):
        send_edges(lambda d: d[0] != 0)
        send_edges(lambda d: d[0] == 0)

    def ratio(n, d):
        return jnp.where(d > 0, n / d, 0.0)

    def await_edges(wanted):
        for i, d in enumerate(kinds):
            if wanted(d):
                given(sends(*d), lambda: edge(i).wait_send())
                given(comes(*d), lambda: edge(i).wait_recv())

    def q_rows(x, y, rows, gain):
        for c in range(x.shape[1]):
            y[rows, c * LANES : (c + 1) * LANES] = gain * ratio(x[0, c, rows, :], x[1, c, rows, :])

    gain1, gain2 = gain_ref[1] - gain_ref[0], gain_ref[2] - gain_ref[1]

    with jax.named_scope("w_side"):
        await_edges(lambda d: d[0] == 0)
    with jax.named_scope("add_side"):
        for k in range(1, 1 + ns):
            def add():
                for base, size, x, into in ((0, size1, x1, into1[k]), (size1, size2, x2, into2[k])):
                    more = unpack_lanes(side_r[k - 1, base : base + size, :])
                    for a in range(2):
                        x[a, into] = x[a, into] + more[a]
                for a in range(2):
                    for c in range(2):
                        base = base_g + (2 * a + c) * stack
                        g[a, c] = g[a, c] + side_r[k - 1, base : base + stack, :]

            given(recv_col[k], add)
    with jax.named_scope("q"):
        q_rows(x1, y1, slice(0, size1), gain1)
        q_rows(x2, y2, slice(0, size2), gain2)

    with jax.named_scope("w_edges"):
        await_edges(lambda d: d[0] != 0)
        for name in ("ec", "e2", "e1", "e0", "er", "second"):
            fetch[name].wait()
    with jax.named_scope("edges"):
        for rp, at1, at2, firsts in ((1, 0, 0, tops), (2, nr // 2, nr // 4, bottoms)):
            for cp in range(1 + ns):

                def add():
                    if cp == 0:
                        for first, x, at in ((0, x1, at1), (3, x2, at2)):
                            for c in range(x.shape[1]):
                                for a, more in enumerate(unpack(edge_r[rp - 1, 0, first + c])):
                                    x[a, c, at : at + 8, :] = x[a, c, at : at + 8, :] + more
                    else:
                        for first, x, at, into in ((0, x1, at1, into1[cp]), (1, x2, at2, into2[cp])):
                            for a, more in enumerate(unpack_lanes(edge_r[rp - 1, cp, first])):
                                x[a, into, at : at + 8, :] = x[a, into, at : at + 8, :] + more
                    for c in range(2):
                        for a, more in enumerate(unpack(edge_r[rp - 1, cp, (5 if cp == 0 else 2) + c])):
                            for f in firsts:
                                g[a, c, f : f + 8, :] = g[a, c, f : f + 8, :] + more

                given(comes(rp, cp), add)
        for x, y, at, gain in ((x1, y1, nr // 2, gain1), (x2, y2, nr // 4, gain2)):
            q_rows(x, y, slice(0, 8), gain)
            q_rows(x, y, slice(at, at + 8), gain)

    with jax.named_scope("deep"):
        shape = (stack, 256)
        at_row = level_of(shape, 0, tops[1:])
        at_col = level_of(shape, 1, lane_cuts)
        gains = [gain_ref[level] - gain_ref[level - 1] for level in (3, 4, 5)] + [-gain_ref[5]]
        factor = jnp.where(
            at_row == 0, gains[0], jnp.where(at_row == 1, gains[1], jnp.where(at_row == 2, gains[2], gains[3]))
        )
        n, d = (jnp.concatenate([g[a, 0], g[a, 1]], axis=1) for a in range(2))
        x = jnp.where(jnp.logical_and(at_row == at_col, d > 0), factor * (n / d), 0.0)
        high, low = split(x)
        er = tab["er"]
        x = dot(er[0], high) + dot(er[0], low) + dot(er[1], high)
        high, low = split(x)
        ec = tab["ec"]
        z3 = dot(high, ec[0]) + dot(low, ec[0]) + dot(high, ec[1])

    with jax.named_scope("z2"):
        z3b[0:m3, :] = z3

        def grow_rows(src, dst, put, get, count):
            x, y, w = (src[get + (slice(k, k + count), slice(None))] for k in (1, 2, 3))
            dst[put + (pl.ds(0, count, stride=2), slice(None))] = 0.125 * (x + w) + 0.75 * y
            dst[put + (pl.ds(1, count, stride=2), slice(None))] = 0.5 * (y + w)

        def block(x, put, p, first):
            ok = jnp.logical_or(line8 >= 4, up) if first else jnp.logical_or(line8 < 4, down)
            x[put + (slice(p, p + 8), slice(None))] = jnp.where(ok, x[put + (slice(p, p + 8), slice(None))], 0.0)

        grow_rows(z3b, z2b, (0,), (), nr // 8 + 8)
        block(z2b, (0,), 0, True)
        block(z2b, (0,), nr // 4, False)
        z2 = right(z2b[0], tab["e2"][...]) + y2[...]
        tiles2 = z2.shape[1] // LANES
        for c in range(tiles2):
            z2b[c] = z2[:, c * LANES : (c + 1) * LANES]
    with jax.named_scope("z1"):
        for c in range(tiles2):
            grow_rows(z2b, z1b, (c,), (c,), nr // 4 + 8)
            block(z1b, (c,), 0, True)
            block(z1b, (c,), nr // 2, False)
        z1 = right(wide_of(z1b, slice(None), range(tiles2)), tab["e1"][...]) + y1[...]
    with jax.named_scope("e0"):
        full = right(z1, tab["e0"][...])

    with jax.named_scope("w_top"):
        def hear(s, carry):
            summary(s).wait()
            return carry

        lax.fori_loop(1, everyone, hear, 0)
    with jax.named_scope("top"):
        total = part[...] + jnp.sum(slots[...], axis=0)
        top_sum = jnp.sum(jnp.where(lane1 < LANES // 2, total, 0.0), axis=1, keepdims=True)
        top_weight = jnp.sum(jnp.where(lane1 < LANES // 2, 0.0, total), axis=1, keepdims=True)
        top_line = (top_sum / top_weight) * tab["line"][1:2, :]
        for c in own_range:
            cols = slice(c * LANES, (c + 1) * LANES)
            wide[c] = full[:, cols] + tab["second"][...] * top_line[:, cols]
    with jax.named_scope("out"):
        gain = gain_ref[0]
        chunk = 32
        for c in own_range:
            for m in range(0, nr // 2, chunk):
                x, y, w = (wide[c, pl.ds(m + k, chunk), :] for k in (3, 4, 5))
                even, odd = pl.ds(2 * m, chunk, stride=2), pl.ds(2 * m + 1, chunk, stride=2)
                q0[c, even, :] = gain * q0[c, even, :] + (0.125 * (x + w) + 0.75 * y)
                q0[c, odd, :] = gain * q0[c, odd, :] + 0.5 * (y + w)
                out_ref[pl.ds(2 * m, 2 * chunk), c * LANES : (c + 1) * LANES] = q0[c, pl.ds(2 * m, 2 * chunk), :]


def local(mesh_shape, heights, scene_ids, scene_offset, scene_weight, band_gain):
    nx, ny, nz = mesh_shape
    nr, nc = heights.shape
    ns = 1 if nx == 2 else 2
    made = tables(nr, nc, nx, ny * nz)
    given = [made[k] for k in COLS + ROWS]
    sizes = (nr, nc, nx, ny, nz, ns)
    ext = (nr + 2 * HALO, nc)
    tiles = nc // LANES
    own_tiles = tiles
    m3 = nr // 8 + 8
    size1, size2, stack = nr // 2 + 16, nr // 4 + 16, nr // 8 + nr // 16 + nr // 32 + nr // 64 + 40
    tiles1, tiles2 = nc // 2 // LANES + 1, nc // 4 // LANES + 1
    beside = size1 + size2 + 4 * stack
    peers = nx * ny * nz - 1
    messages = 3 * (1 + ns) - 1
    hbm = pl.BlockSpec(memory_space=pltpu.HBM)
    return pl.pallas_call(
        functools.partial(kernel, sizes),
        out_shape=pltpu.VMEM((nr, nc), F32),
        in_specs=[hbm] * (5 + len(given)),
        out_specs=pl.BlockSpec(memory_space=pltpu.VMEM),
        scratch_shapes=[pltpu.VMEM(x.shape[1:], x.dtype) for x in given]
        + [
            pltpu.SMEM(scene_offset.shape, F32),
            pltpu.SMEM(scene_weight.shape, F32),
            pltpu.SMEM(band_gain.shape, F32),
            pltpu.VMEM(ext, F32),
            pltpu.VMEM(ext, jnp.int32),
            pltpu.VMEM((own_tiles, nr, LANES), F32),
        ]
        + [pltpu.VMEM((tiles, nr + 3 * HALO, LANES), F32)] * 2
        + [pltpu.VMEM((tiles, nr // 2 + 32, LANES), F32)] * 2
        + [pltpu.VMEM((tiles, nr // 4 + 24, LANES), F32)] * 2
        + [pltpu.VMEM((own_tiles, m3, LANES), F32)] * 2
        + [
            pltpu.VMEM((2, tiles1, size1, LANES), F32),
            pltpu.VMEM((2, tiles2, size2, LANES), F32),
            pltpu.VMEM((2, 2, stack, LANES), F32),
            pltpu.VMEM((size1, tiles1 * LANES), F32),
            pltpu.VMEM((size2, tiles2 * LANES), F32),
            pltpu.VMEM((ns, beside, LANES), F32),
            pltpu.VMEM((ns, beside, LANES), F32),
            pltpu.VMEM((2, 1 + ns, 7, 8, LANES), F32),
            pltpu.VMEM((2, 1 + ns, 7, 8, LANES), F32),
            pltpu.VMEM((m3 + 8, LANES), F32),
            pltpu.VMEM((tiles2, nr // 4 + 16, LANES), F32),
            pltpu.VMEM((tiles2, nr // 2 + 16, LANES), F32),
            pltpu.VMEM((own_tiles, nr // 2 + 16, LANES), F32),
            pltpu.VMEM((1, LANES), F32),
            pltpu.VMEM((peers, 1, LANES), F32),
            pltpu.SemaphoreType.DMA((2 * CHUNKS + 3,)),
            pltpu.SemaphoreType.DMA((len(given),)),
            pltpu.SemaphoreType.DMA((messages,)),
            pltpu.SemaphoreType.DMA((messages,)),
            pltpu.SemaphoreType.DMA((peers,)),
            pltpu.SemaphoreType.DMA((peers,)),
        ],
        compiler_params=pltpu.CompilerParams(collective_id=0, has_side_effects=True),
    )(scene_offset, scene_weight, band_gain, heights, scene_ids, *given)


def solution(mesh):
    placed = (P(("gy", "gz"), "gx"), P(("gy", "gz"), "gx"), P(), P(), P())
    shape = tuple(mesh.shape[name] for name in ("gx", "gy", "gz"))
    return jax.shard_map(
        functools.partial(local, shape), mesh=mesh, in_specs=placed,
        out_specs=P(("gy", "gz"), "gx"), check_vma=False,
    )
```

time: 19.9 us -> 17.8 us (0.89)
  Pallas kernels: 18.8 us -> 16.6 us
    pallas_call x1, Pallas kernels: 18.8 us -> 16.6 us  [local(): pl.pallas_call(functools.partial(kernel, sizes), out_shape=pltpu.VMEM((nr...]
where the time goes in v3:
time: 17.8 us; the launch traced here: 17.6 us
  Pallas kernels  16.6 us (93%)
  local copies, waits for them, and re-layouts  0.97 us (5%)
    pallas_call x1, Pallas kernels, local(): pl.pallas_call(functools.partial(kernel, sizes), out_shape=pltpu.VMEM((nr...  16.6 us
    unnamed x1, local copies, waits for them, and re-layouts  0.97 us

profile of v3, /device:TPU:0, one launch (start us, length us, event | category | flops | bytes accessed | tf_op | source)
XLA Modules:
  0.0 17.6 jit_solution(5259549194685317096)
XLA Ops:
  0.0 16.6 %shard_map.190 = f32[512,512]{1,0:T(8,128)S(1)} custom-call(f32[16]{0:T(128)} %off_hbm.1, f32[16]{0:T(128)} %wgt_hbm.1, f32[6]{0:T(128)} %gain_hbm.1, f32[512,512]{1,0:T(8,128)} %h_ref.1, s32[512,512]{1,0:T(8,128)} %s_ref.1, f32[2,2,512]{2,1,0:T(2,128)} %constant.40.clone.rest_0_, bf16[2,512,256]{2,1,0:T(8,128)(2,1)} %constant.45.rest_1_, ...), custom_call_target="tpu_custom_call" | custom-call | tf_op jit(solution)/shard_map/pallas_call | solution.py:689
  16.6 1.0 %copy.22 = f32[512,512]{1,0:T(8,128)} copy(f32[512,512]{1,0:T(8,128)S(1)} %shard_map.190) | data formatting | bytes 2097152

commit v4 on v3

--- a/solution.py
+++ b/solution.py
@@ -175,6 +175,24 @@
     return out
 
 
+def merge(made):
+    arrays, places = [], {}
+    for at, group in enumerate(COLS + ROWS):
+        lanes = max(made[name].shape[-1] for name in group)
+        parts, start = [], 0
+        for name in group:
+            x = made[name]
+            rows, width = x.shape[-2:]
+            x = x.reshape(x.shape[0], -1, rows, width)
+            tall = -(-rows // 16) * 16 if len(group) > 1 else rows
+            x = jnp.pad(x, ((0, 0), (0, 0), (0, tall - rows), (0, lanes - width)))
+            places[name] = (at, start, tall, rows, width)
+            start += x.shape[1] * tall
+            parts.append(x.reshape(x.shape[0], -1, lanes))
+        arrays.append(jnp.concatenate(parts, axis=1))
+    return arrays, places
+
+
 def split(x):
     high = x.astype(BF16)
     return high, (x - high.astype(F32)).astype(BF16)
@@ -189,19 +207,20 @@
     return dot(high, c) + dot(low, c)
 
 
-COLS = ("line", "c03", "call", "c1", "c2", "s1", "s2", "ec", "e2", "e1", "e0")
-ROWS = ("first", "rall", "er", "second")
+COLS = (("call", "e0"), ("c03", "c2", "e2"), ("c1", "e1"), ("s1", "s2", "ec"), ("line",))
+ROWS = (("rall", "er"), ("first",), ("second",))
+OWN_TILES, SIDE_TILES = 5, 2
 CHUNKS = 4
 
 
 def kernel(
-    sizes, off_hbm, wgt_hbm, gain_hbm, h_ref, s_ref, *rest
+    sizes, places, off_hbm, wgt_hbm, gain_hbm, h_ref, s_ref, *rest
 ):
     nr, nc, nx, ny, nz, ns = sizes
-    names = COLS + ROWS
-    tables_hbm, rest = dict(zip(names, rest)), rest[len(names):]
+    count = len(COLS) + len(ROWS)
+    tables_hbm, rest = rest[:count], rest[count:]
     out_ref, rest = rest[0], rest[1:]
-    tab, rest = dict(zip(names, rest)), rest[len(names):]
+    tab, rest = rest[:count], rest[count:]
     (
         off_ref, wgt_ref, gain_ref, h_buf, s_buf, q0, num, den, n1, d1, n2, d2, n3, d3,
         x1, x2, g, y1, y2, side_s, side_r, edge_s, edge_r, z3b, z2b, z1b, wide, part, slots,
@@ -228,20 +247,32 @@
                 pltpu.make_async_copy(
                     src.at[rows, :],
                     dst.at[pl.ds(HALO + k * step, step), pl.ds(0, nc)],
-                    own_sem.at[2 * k + a],
+                    own_sem.at[k],
                 )
             )
     small = [
-        pltpu.make_async_copy(src, dst, own_sem.at[2 * CHUNKS + a])
+        pltpu.make_async_copy(src, dst, own_sem.at[CHUNKS + a])
         for a, (src, dst) in enumerate(((off_hbm, off_ref), (wgt_hbm, wgt_ref), (gain_hbm, gain_ref)))
     ]
-    fetch = {}
-    for i, name in enumerate(names):
-        src = tables_hbm[name]
-        src = src.at[ct] if name in COLS else src.at[rt]
-        fetch[name] = pltpu.make_async_copy(src, tab[name], tab_sem.at[i])
-    early = ["first", "line"]
-    for copy in loads[:2] + small + [fetch[name] for name in early] + loads[2:]:
+    fetch = [
+        pltpu.make_async_copy(src.at[ct if i < len(COLS) else rt], tab[i], tab_sem.at[i])
+        for i, src in enumerate(tables_hbm)
+    ]
+    early = (places["line"][0], places["first"][0])
+    ready = set()
+
+    def await_tables(*names):
+        for name in names:
+            if places[name][0] not in ready:
+                ready.add(places[name][0])
+                fetch[places[name][0]].wait()
+
+    def table(name, k=0, rows=None):
+        at, start, tall, height, width = places[name]
+        first, last = rows or (0, height)
+        return tab[at][start + k * tall + first : start + k * tall + last, :width]
+
+    for copy in loads[:2] + small + [fetch[i] for i in early] + loads[2:]:
         copy.start()
 
     up, down = row > 0, row < blocks - 1
@@ -294,8 +325,8 @@
 
     lax.fori_loop(1, everyone, greet, 0)
 
-    for name, copy in fetch.items():
-        if name not in early:
+    for i, copy in enumerate(fetch):
+        if i not in early:
             copy.start()
 
     zero = jnp.zeros((HALO, LANES), F32)
@@ -315,10 +346,9 @@
         rp, cp = kinds[i]
         if rp == 0:
             src, dst = side_s.at[cp - 1], side_r.at[cp - 1]
-        elif cp == 0:
-            src, dst = edge_s.at[rp - 1, 0], edge_r.at[rp - 1, 0]
         else:
-            src, dst = edge_s.at[rp - 1, cp, pl.ds(0, 4)], edge_r.at[rp - 1, cp, pl.ds(0, 4)]
+            place = pl.ds(0, OWN_TILES) if cp == 0 else pl.ds(0, SIDE_TILES)
+            src, dst = edge_s.at[rp - 1, cp, place], edge_r.at[rp - 1, cp, place]
         return pltpu.make_async_remote_copy(
             src_ref=src, dst_ref=dst, send_sem=send0.at[i], recv_sem=recv0.at[i], device_id=device(rp, cp)
         )
@@ -361,8 +391,8 @@
         return pltpu.make_async_remote_copy(
             src_ref=part,
             dst_ref=slots.at[s - 1],
-            send_sem=psend.at[s - 1],
-            recv_sem=precv.at[s - 1],
+            send_sem=psend,
+            recv_sem=precv,
             device_id=peer(s),
         )
 
@@ -372,35 +402,36 @@
                 given(sends(*d), lambda: edge(i).start())
 
     with jax.named_scope("level0"):
-        fetch["first"].wait()
+        await_tables("line", "first")
+        line = table("line")
         sums = [[0.0] * own_tiles, [0.0] * own_tiles]
         for k in range(CHUNKS):
-            loads[2 * k].wait()
-            loads[2 * k + 1].wait()
-            weights = tab["first"][k * step : (k + 1) * step, :]
+            both = pl.ds(0, 2 * step)
+            pltpu.make_async_copy(h_ref.at[both, :], h_buf.at[both, pl.ds(0, nc)], own_sem.at[k]).wait()
+            weights = table("first", 0, (k * step, (k + 1) * step))
             for c in range(own_tiles):
                 moved, numer, weight = level0(HALO + k * step, step, c)
                 q0[c, k * step : (k + 1) * step, :] = moved
                 for a, x in enumerate((numer, weight)):
                     x = (x * weights).reshape(step // 8, 8, LANES)
                     sums[a][c] = sums[a][c] + jnp.sum(x, axis=0)
-        fetch["line"].wait()
         flat = []
         for a in range(2):
-            x = sum(sums[a][c] * tab["line"][0:1, c * LANES : (c + 1) * LANES] for c in range(own_tiles))
+            x = sum(sums[a][c] * line[0:1, c * LANES : (c + 1) * LANES] for c in range(own_tiles))
             x = jnp.sum(x, axis=0, keepdims=True)
             flat.append(x + pltpu.roll(x, LANES // 2, axis=1))
         lane1 = lax.broadcasted_iota(jnp.int32, (1, LANES), 1)
         part[...] = jnp.where(lane1 < LANES // 2, flat[0], flat[1])
 
-    with jax.named_scope("meet"):
-        pl.semaphore_wait(barrier, everyone - 1)
-
-    def tell(s, carry):
-        summary(s).start()
-        return carry
-
-    lax.fori_loop(1, everyone, tell, 0)
+    def meet():
+        with jax.named_scope("meet"):
+            pl.semaphore_wait(barrier, everyone - 1)
+
+        def tell(s, carry):
+            summary(s).start()
+            return carry
+
+        lax.fori_loop(1, everyone, tell, 0)
 
     def taps(src, c, start, count):
         x = [src[c, pl.ds(start + a, count, stride=2), :] for a in range(-2, 3)]
@@ -438,6 +469,7 @@
                 ends2(two, c)
                 three[c] = taps(two, c, 4, m3)
 
+    meet()
     def wide_of(x, rows, tiles):
         return jnp.concatenate([x[c, rows, :] for c in tiles], axis=1)
 
@@ -467,74 +499,109 @@
         return jnp.where(low, x, 0.0), jnp.where(low, pltpu.roll(x, LANES // 2, axis=1), 0.0)
 
     with jax.named_scope("p3"):
-        fetch["c03"].wait()
-        fetch["rall"].wait()
+        await_tables("c03", "rall", "call")
         x = jnp.concatenate([wide_of(n3, slice(None), own_range), wide_of(d3, slice(None), own_range)], axis=0)
-        x = right(x, tab["c03"][...])
+        x = right(x, table("c03"))
         x = x[:, :LANES] + x[:, LANES:]
         high, low = split(jnp.concatenate([x[:m3], x[m3:]], axis=1))
-        rall = tab["rall"][...]
+        rall = table("rall")
         x = dot(rall, high) + dot(rall, low)
         x = jnp.concatenate([x[: stack - s6], x[stack - s6 : stack] + x[stack : stack + s6]], axis=0)
-        fetch["call"].wait()
         high, low = split(jnp.concatenate([x[:, :LANES], x[:, LANES:]], axis=0))
-        x = dot(high, tab["call"][0]) + dot(low, tab["call"][0]) + dot(high, tab["call"][1])
+        x = dot(high, table("call", 0)) + dot(low, table("call", 0)) + dot(high, table("call", 1))
 
     base_g = size1 + size2
 
+    def own_lines(x1_, x2_, g_):
+        last = x1_[2] + pltpu.roll(x2_[1], 8, axis=1) + pltpu.roll(g_[1], 16, axis=1)
+        return [x1_[0], x1_[1], x2_[0], g_[0], last]
+
+    def ends(x, c, last):
+        return jnp.concatenate([x[c, 8:16, :], x[c, last : last + 8, :]], axis=0)
+
+    with jax.named_scope("edge_own"):
+        await_tables("s1", "s2", "c1", "c2")
+
+        def own_ends(n, d, last, name):
+            y = jnp.concatenate(
+                [jnp.concatenate([ends(x, c, last) for c in own_range], axis=1) for x in (n, d)], axis=0
+            )
+            return right(y, table(name))
+
+        own1, own2 = own_ends(n1, d1, last1, "c1"), own_ends(n2, d2, last2, "c2")
+
+    def tile(x, at, c):
+        return x[at : at + 8, c * LANES : (c + 1) * LANES]
+
     with jax.named_scope("g_pack"):
-        for c in range(2):
-            index = lane8 + c * LANES
-            for k in range(1 + ns):
-                piece = [x[a * stack : (a + 1) * stack, k * 256 + c * LANES : k * 256 + (c + 1) * LANES] for a in (0, 1)]
+        for k in range(1 + ns):
+            piece = [
+                [x[a * stack : (a + 1) * stack, k * 256 + c * LANES : k * 256 + (c + 1) * LANES] for c in (0, 1)]
+                for a in (0, 1)
+            ]
+            for a in range(2):
+                for c in range(2):
+                    if k == 0:
+                        g[a, c] = piece[a][c]
+                    else:
+                        side_s[k - 1, base_g + (2 * a + c) * stack : base_g + (2 * a + c + 1) * stack, :] = piece[a][c]
+            for rp, firsts in ((1, bottoms), (2, tops)):
+                deep = []
                 for a in range(2):
-                    if k == 0:
-                        g[a, c] = piece[a]
-                    else:
-                        side_s[k - 1, base_g + (2 * a + c) * stack : base_g + (2 * a + c + 1) * stack, :] = piece[a]
-                for rp, firsts in ((1, bottoms), (2, tops)):
-                    line = []
-                    for a in range(2):
-                        b = [piece[a][f : f + 8] for f in firsts]
-                        line.append(
+                    lines = []
+                    for c in range(2):
+                        index = lane8 + c * LANES
+                        b = [piece[a][c][f : f + 8] for f in firsts]
+                        lines.append(
                             jnp.where(
                                 index < lane_cuts[0], b[0],
                                 jnp.where(index < lane_cuts[1], b[1], jnp.where(index < lane_cuts[2], b[2], b[3])),
                             )
                         )
-                    edge_s[rp - 1, k, (5 if k == 0 else 2) + c] = pack(*line)
-
-    body1, body2 = slice(8, 8 + size1), slice(8, 8 + size2)
-
-    with jax.named_scope("x_side"):
-        fetch["s1"].wait()
-        fetch["s2"].wait()
-        for k in range(1, 1 + ns):
-            for base, n, d, body, name, at in (
-                (0, n1, d1, body1, "s1", nr // 2), (size1, n2, d2, body2, "s2", nr // 4),
-            ):
-                x = right(n[near_tile[k], body, :], tab[name][k - 1, 0])
-                x = x + right(d[near_tile[k], body, :], tab[name][k - 1, 1])
-                side_s[k - 1, base : base + x.shape[0], :] = x
-                edge_s[0, k, 0 if base == 0 else 1] = x[at : at + 8]
-                edge_s[1, k, 0 if base == 0 else 1] = x[0:8]
-
-    with jax.named_scope("x_own"):
-        for n, d, body, name, dst, at, first in (
-            (n1, d1, body1, "c1", x1, nr // 2, 0), (n2, d2, body2, "c2", x2, nr // 4, 3),
-        ):
-            fetch[name].wait()
-            both = [right(wide_of(x, body, own_range), tab[name][...]) for x in (n, d)]
-            for c in range(dst.shape[1]):
-                both_c = [x[:, c * LANES : (c + 1) * LANES] for x in both]
-                for a in range(2):
-                    dst[a, c] = both_c[a]
-                edge_s[0, 0, first + c] = pack(*(x[at : at + 8] for x in both_c))
-                edge_s[1, 0, first + c] = pack(*(x[0:8] for x in both_c))
+                    deep.append(lines)
+                at = 8 * (2 - rp)
+                if k == 0:
+                    packed = [
+                        own_lines(
+                            [tile(own1, 16 * a + at, c) for c in range(3)],
+                            [tile(own2, 16 * a + at, c) for c in range(2)],
+                            deep[a],
+                        )
+                        for a in range(2)
+                    ]
+                    for t in range(OWN_TILES):
+                        edge_s[rp - 1, 0, t] = pack(packed[0][t], packed[1][t])
+                else:
+                    lines = []
+                    for n, d, last, name in ((n1, d1, last1, "s1"), (n2, d2, last2, "s2")):
+                        first = 8 if rp == 2 else last
+                        y = right(n[near_tile[k], first : first + 8, :], table(name, 2 * (k - 1) + 0))
+                        lines.append(y + right(d[near_tile[k], first : first + 8, :], table(name, 2 * (k - 1) + 1)))
+                    edge_s[rp - 1, k, 0] = pack(deep[0][0], deep[1][0])
+                    edge_s[rp - 1, k, 1] = (
+                        lines[0] + pltpu.roll(lines[1], 8, axis=1)
+                        + pltpu.roll(pack(deep[0][1], deep[1][1]), 16, axis=1)
+                    )
 
     with jax.named_scope("send"):
         send_edges(lambda d: d[0] != 0)
+
+    body1, body2 = slice(8, 8 + size1), slice(8, 8 + size2)
+
+    with jax.named_scope("x_side"):
+        for k in range(1, 1 + ns):
+            for base, n, d, body, name in ((0, n1, d1, body1, "s1"), (size1, n2, d2, body2, "s2")):
+                y = right(n[near_tile[k], body, :], table(name, 2 * (k - 1) + 0))
+                y = y + right(d[near_tile[k], body, :], table(name, 2 * (k - 1) + 1))
+                side_s[k - 1, base : base + y.shape[0], :] = y
         send_edges(lambda d: d[0] == 0)
+
+    with jax.named_scope("x_own"):
+        for n, d, body, name, dst in ((n1, d1, body1, "c1", x1), (n2, d2, body2, "c2", x2)):
+            for a, y in enumerate((n, d)):
+                y = right(wide_of(y, body, own_range), table(name))
+                for c in range(dst.shape[1]):
+                    dst[a, c] = y[:, c * LANES : (c + 1) * LANES]
 
     def ratio(n, d):
         return jnp.where(d > 0, n / d, 0.0)
@@ -572,24 +639,36 @@
 
     with jax.named_scope("w_edges"):
         await_edges(lambda d: d[0] != 0)
-        for name in ("ec", "e2", "e1", "e0", "er", "second"):
-            fetch[name].wait()
+        await_tables("ec", "e2", "e1", "e0", "er", "second")
+    packed_lanes = jnp.logical_and(lane8 % (LANES // 2) >= MIDDLE[0], lane8 % (LANES // 2) <= MIDDLE[-1])
     with jax.named_scope("edges"):
         for rp, at1, at2, firsts in ((1, 0, 0, tops), (2, nr // 2, nr // 4, bottoms)):
             for cp in range(1 + ns):
 
                 def add():
+                    got = edge_r.at[rp - 1, cp]
+                    tail = unpack(got[OWN_TILES - 1]) if cp == 0 else None
                     if cp == 0:
-                        for first, x, at in ((0, x1, at1), (3, x2, at2)):
-                            for c in range(x.shape[1]):
-                                for a, more in enumerate(unpack(edge_r[rp - 1, 0, first + c])):
-                                    x[a, c, at : at + 8, :] = x[a, c, at : at + 8, :] + more
+                        adds1 = [unpack(got[0]), unpack(got[1]), [jnp.where(lane8 < 8, y, 0.0) for y in tail]]
+                        adds2 = [
+                            unpack(got[2]),
+                            [jnp.where(lane8 < 8, pltpu.roll(y, LANES - 8, axis=1), 0.0) for y in tail],
+                        ]
+                        for x, at, adds in ((x1, at1, adds1), (x2, at2, adds2)):
+                            for c, more in enumerate(adds):
+                                for a in range(2):
+                                    x[a, c, at : at + 8, :] = x[a, c, at : at + 8, :] + more[a]
+                        deep = [unpack(got[3]), tail]
                     else:
-                        for first, x, at, into in ((0, x1, at1, into1[cp]), (1, x2, at2, into2[cp])):
-                            for a, more in enumerate(unpack_lanes(edge_r[rp - 1, cp, first])):
+                        y = got[1]
+                        both = ((x1, at1, into1[cp], y), (x2, at2, into2[cp], pltpu.roll(y, LANES - 8, axis=1)))
+                        for x, at, into, part_ in both:
+                            for a, more in enumerate(unpack_lanes(jnp.where(packed_lanes, part_, 0.0))):
                                 x[a, into, at : at + 8, :] = x[a, into, at : at + 8, :] + more
+                        deep = [unpack(got[0]), unpack(y)]
+                    deep[1] = [jnp.where(lane8 < 32, pltpu.roll(y, LANES - 16, axis=1), 0.0) for y in deep[1]]
                     for c in range(2):
-                        for a, more in enumerate(unpack(edge_r[rp - 1, cp, (5 if cp == 0 else 2) + c])):
+                        for a, more in enumerate(deep[c]):
                             for f in firsts:
                                 g[a, c, f : f + 8, :] = g[a, c, f : f + 8, :] + more
 
@@ -609,10 +688,10 @@
         n, d = (jnp.concatenate([g[a, 0], g[a, 1]], axis=1) for a in range(2))
         x = jnp.where(jnp.logical_and(at_row == at_col, d > 0), factor * (n / d), 0.0)
         high, low = split(x)
-        er = tab["er"]
+        er = [table("er", k) for k in (0, 1)]
         x = dot(er[0], high) + dot(er[0], low) + dot(er[1], high)
         high, low = split(x)
-        ec = tab["ec"]
+        ec = [table("ec", k) for k in (0, 1)]
         z3 = dot(high, ec[0]) + dot(low, ec[0]) + dot(high, ec[1])
 
     with jax.named_scope("z2"):
@@ -630,7 +709,7 @@
         grow_rows(z3b, z2b, (0,), (), nr // 8 + 8)
         block(z2b, (0,), 0, True)
         block(z2b, (0,), nr // 4, False)
-        z2 = right(z2b[0], tab["e2"][...]) + y2[...]
+        z2 = right(z2b[0], table("e2")) + y2[...]
         tiles2 = z2.shape[1] // LANES
         for c in range(tiles2):
             z2b[c] = z2[:, c * LANES : (c + 1) * LANES]
@@ -639,24 +718,22 @@
             grow_rows(z2b, z1b, (c,), (c,), nr // 4 + 8)
             block(z1b, (c,), 0, True)
             block(z1b, (c,), nr // 2, False)
-        z1 = right(wide_of(z1b, slice(None), range(tiles2)), tab["e1"][...]) + y1[...]
+        z1 = right(wide_of(z1b, slice(None), range(tiles2)), table("e1")) + y1[...]
     with jax.named_scope("e0"):
-        full = right(z1, tab["e0"][...])
+        full = right(z1, table("e0"))
 
     with jax.named_scope("w_top"):
-        def hear(s, carry):
-            summary(s).wait()
-            return carry
-
-        lax.fori_loop(1, everyone, hear, 0)
+        everything = pltpu.make_async_copy(slots, slots, precv)
+        everything.wait()
+        pltpu.make_async_copy(slots, slots, psend).wait()
     with jax.named_scope("top"):
         total = part[...] + jnp.sum(slots[...], axis=0)
         top_sum = jnp.sum(jnp.where(lane1 < LANES // 2, total, 0.0), axis=1, keepdims=True)
         top_weight = jnp.sum(jnp.where(lane1 < LANES // 2, 0.0, total), axis=1, keepdims=True)
-        top_line = (top_sum / top_weight) * tab["line"][1:2, :]
+        top_line = (top_sum / top_weight) * line[1:2, :]
         for c in own_range:
             cols = slice(c * LANES, (c + 1) * LANES)
-            wide[c] = full[:, cols] + tab["second"][...] * top_line[:, cols]
+            wide[c] = full[:, cols] + table("second") * top_line[:, cols]
     with jax.named_scope("out"):
         gain = gain_ref[0]
         chunk = 32
@@ -674,7 +751,7 @@
     nr, nc = heights.shape
     ns = 1 if nx == 2 else 2
     made = tables(nr, nc, nx, ny * nz)
-    given = [made[k] for k in COLS + ROWS]
+    given, places = merge(made)
     sizes = (nr, nc, nx, ny, nz, ns)
     ext = (nr + 2 * HALO, nc)
     tiles = nc // LANES
@@ -687,7 +764,7 @@
     messages = 3 * (1 + ns) - 1
     hbm = pl.BlockSpec(memory_space=pltpu.HBM)
     return pl.pallas_call(
-        functools.partial(kernel, sizes),
+        functools.partial(kernel, sizes, places),
         out_shape=pltpu.VMEM((nr, nc), F32),
         in_specs=[hbm] * (5 + len(given)),
         out_specs=pl.BlockSpec(memory_space=pltpu.VMEM),
@@ -712,20 +789,20 @@
             pltpu.VMEM((size2, tiles2 * LANES), F32),
             pltpu.VMEM((ns, beside, LANES), F32),
             pltpu.VMEM((ns, beside, LANES), F32),
-            pltpu.VMEM((2, 1 + ns, 7, 8, LANES), F32),
-            pltpu.VMEM((2, 1 + ns, 7, 8, LANES), F32),
+            pltpu.VMEM((2, 1 + ns, OWN_TILES, 8, LANES), F32),
+            pltpu.VMEM((2, 1 + ns, OWN_TILES, 8, LANES), F32),
             pltpu.VMEM((m3 + 8, LANES), F32),
             pltpu.VMEM((tiles2, nr // 4 + 16, LANES), F32),
             pltpu.VMEM((tiles2, nr // 2 + 16, LANES), F32),
             pltpu.VMEM((own_tiles, nr // 2 + 16, LANES), F32),
             pltpu.VMEM((1, LANES), F32),
             pltpu.VMEM((peers, 1, LANES), F32),
-            pltpu.SemaphoreType.DMA((2 * CHUNKS + 3,)),
+            pltpu.SemaphoreType.DMA((CHUNKS + 3,)),
             pltpu.SemaphoreType.DMA((len(given),)),
             pltpu.SemaphoreType.DMA((messages,)),
             pltpu.SemaphoreType.DMA((messages,)),
-            pltpu.SemaphoreType.DMA((peers,)),
-            pltpu.SemaphoreType.DMA((peers,)),
+            pltpu.SemaphoreType.DMA(()),
+            pltpu.SemaphoreType.DMA(()),
         ],
         compiler_params=pltpu.CompilerParams(collective_id=0, has_side_effects=True),
     )(scene_offset, scene_weight, band_gain, heights, scene_ids, *given)

time: 17.8 us -> 15.8 us (0.89)
  the two profiles are of different devices: /device:TPU:0 before, /device:TPU:5 now
where the time goes in v4:
time: 15.8 us; the launch traced here: 15.6 us
  Pallas kernels  14.6 us (92%)
  local copies, waits for them, and re-layouts  0.97 us (6%)
    pallas_call x1, Pallas kernels, local(): pl.pallas_call(functools.partial(kernel, sizes, places), out_shape=pltpu....  14.6 us
    unnamed x1, local copies, waits for them, and re-layouts  0.97 us

profile of v4, /device:TPU:5, one launch (start us, length us, event | category | flops | bytes accessed | tf_op | source)
XLA Modules:
  0.0 15.6 jit_solution(16145345749226046508)
XLA Ops:
  0.0 14.6 %shard_map.190 = f32[512,512]{1,0:T(8,128)S(1)} custom-call(f32[16]{0:T(128)} %off_hbm.1, f32[16]{0:T(128)} %wgt_hbm.1, f32[6]{0:T(128)} %gain_hbm.1, f32[512,512]{1,0:T(8,128)} %h_ref.1, s32[512,512]{1,0:T(8,128)} %s_ref.1, bf16[2,640,512]{2,1,0:T(8,128)(2,1)} %constant.55.rest_0_, bf16[2,1152,256]{2,1,0:T(8,128)(2,1)} %constant.59.rest_1_, ...), custom_call_target="tpu_custom_call" | custom-call | tf_op jit(solution)/shard_map/pallas_call | solution.py:766
  14.6 1.0 %copy.22 = f32[512,512]{1,0:T(8,128)} copy(f32[512,512]{1,0:T(8,128)S(1)} %shard_map.190) | data formatting | bytes 2097152

commit v5 on v4

--- a/solution.py
+++ b/solution.py
@@ -81,8 +81,10 @@
         ]
         return np.concatenate(parts, axis=0)
 
-    def sums(self):
-        return reach(self.count * self.n, LEVELS)[self.at * self.n : (self.at + 1) * self.n]
+    def sums(self, level, place):
+        weights = reach(self.count * (self.n >> level), LEVELS - level)
+        place = place + self.at * (self.n >> level)
+        return np.where((place >= 0) & (place < weights.size), weights[np.clip(place, 0, weights.size - 1)], 0.0)
 
     def ones(self, level):
         x = self.inside(self.window(6, 4), 6) * 1.0
@@ -131,11 +133,12 @@
         call.append([pad(x.astype(np.float64), (LANES, 256)) for x in halves(ax.deep(three, d))])
     call = np.stack([np.concatenate([x[k] for x in call], axis=1) for k in range(2)])
     back = ax.back()
-    ec = np.stack([pad(x.astype(np.float64), (256, LANES)) for x in halves(back)])
+    to0 = ax.grow(w2, w1, 1) @ ax.grow(w1, own, 0)
+    ec0 = np.stack([pad(x.astype(np.float64), (256, n)) for x in halves(back @ ax.grow(o3, w2, 2) @ to0)])
     return dict(
         c1=ax.shrink(own, out1, 1), c2=to2 @ ax.shrink(w1, out2, 2), s1=s1, s2=s2, c03=c03, call=call,
-        ec=ec, e2=ax.grow(three, out2, 2), e1=ax.grow(out2, out1, 1), e0=ax.grow(out1, own, 0),
-    ), dict(line=np.stack([ax.sums(), ax.ones(0)[4:-4]]))
+        ec0=ec0, e1=ax.grow(out2, out1, 1), e0=ax.grow(out1, own, 0),
+    ), dict(line=np.stack([ax.sums(0, own), ax.ones(0)[4:-4]]))
 
 
 def row_tables(n, at, count):
@@ -148,9 +151,11 @@
     rall = pad(rall, (-(-rall.shape[0] // 16) * 16, o3.size))
     back = ax.back()
     er = np.stack([x.astype(np.float64) for x in halves(back.T)])
-    first = np.repeat(ax.sums()[:, None], LANES, 1)
+    first = np.repeat(ax.sums(3, o3)[:, None], LANES, 1)
+    w2 = ax.window(2, 8)
+    r12 = (ax.grow(o3, w2, 2) @ ax.grow(w2, np.arange(-4, n // 2 + 12), 1)).T
     second = np.repeat(pad(ax.ones(1), (n // 2 + 16,))[:, None], LANES, 1)
-    return dict(rall=rall, er=er), dict(first=first, second=second)
+    return dict(rall=rall, er=er, r12=r12), dict(first=first, second=second)
 
 
 def tables(nr, nc, nx, blocks):
@@ -207,8 +212,8 @@
     return dot(high, c) + dot(low, c)
 
 
-COLS = (("call", "e0"), ("c03", "c2", "e2"), ("c1", "e1"), ("s1", "s2", "ec"), ("line",))
-ROWS = (("rall", "er"), ("first",), ("second",))
+COLS = (("c03", "c2"), ("call", "e0"), ("c1", "e1"), ("s1", "s2"), ("ec0",), ("line",))
+ROWS = (("rall", "er", "r12"), ("first", "second"))
 OWN_TILES, SIDE_TILES = 5, 2
 CHUNKS = 4
 
@@ -223,7 +228,7 @@
     tab, rest = rest[:count], rest[count:]
     (
         off_ref, wgt_ref, gain_ref, h_buf, s_buf, q0, num, den, n1, d1, n2, d2, n3, d3,
-        x1, x2, g, y1, y2, side_s, side_r, edge_s, edge_r, z3b, z2b, z1b, wide, part, slots,
+        x1, x2, g, factor, y1, y2, side_s, side_r, edge_s, edge_r, z2b, z1b, wide, part, slots,
         own_sem, tab_sem, send0, recv0, psend, precv,
     ) = rest
     cx, cy, cz = lax.axis_index("gx"), lax.axis_index("gy"), lax.axis_index("gz")
@@ -258,7 +263,6 @@
         pltpu.make_async_copy(src.at[ct if i < len(COLS) else rt], tab[i], tab_sem.at[i])
         for i, src in enumerate(tables_hbm)
     ]
-    early = (places["line"][0], places["first"][0])
     ready = set()
 
     def await_tables(*names):
@@ -272,7 +276,7 @@
         first, last = rows or (0, height)
         return tab[at][start + k * tall + first : start + k * tall + last, :width]
 
-    for copy in loads[:2] + small + [fetch[i] for i in early] + loads[2:]:
+    for copy in loads[:2] + small + loads[2:]:
         copy.start()
 
     up, down = row > 0, row < blocks - 1
@@ -317,17 +321,27 @@
         line = other // nx
         return {"gx": other % nx, "gy": line // nz, "gz": line % nz}
 
+    def places_of(at, count):
+        return [jnp.where(at + d < count, at + d, at + d - count) for d in range(count)]
+
+    def others(body):
+        if everyone <= 64:
+            xs, ys, zs = places_of(cx, nx), places_of(cy, ny), places_of(cz, nz)
+            for s in range(1, everyone):
+                line = s // nx
+                body(s, {"gx": xs[s % nx], "gy": ys[line // nz], "gz": zs[line % nz]})
+        else:
+            def step_(s, carry):
+                body(s, peer(s))
+                return carry
+
+            lax.fori_loop(1, everyone, step_, 0)
+
     barrier = pltpu.get_barrier_semaphore()
-
-    def greet(s, carry):
-        pl.semaphore_signal(barrier, inc=1, device_id=peer(s))
-        return carry
-
-    lax.fori_loop(1, everyone, greet, 0)
-
-    for i, copy in enumerate(fetch):
-        if i not in early:
-            copy.start()
+    others(lambda s, who: pl.semaphore_signal(barrier, inc=1, device_id=who))
+
+    for copy in fetch:
+        copy.start()
 
     zero = jnp.zeros((HALO, LANES), F32)
     for x in (num, den):
@@ -340,7 +354,6 @@
         for c in range(own_tiles):
             x[c, 0:8, :] = zero
             x[c, x.shape[1] - 8 :, :] = zero
-    z3b[m3:, :] = zero
 
     def edge(i):
         rp, cp = kinds[i]
@@ -382,18 +395,17 @@
             [jnp.take_along_axis(wgt_row, ids[r : r + 8], axis=1) for r in range(0, count, 8)], axis=0
         )
         moved = h_buf[rows, c * LANES : (c + 1) * LANES] + tree(ids, off_ref)
-        numer = weight * moved
-        num[c, rows, :] = numer
+        num[c, rows, :] = weight * moved
         den[c, rows, :] = weight
-        return moved, numer, weight
-
-    def summary(s):
+        return moved
+
+    def summary(s, who):
         return pltpu.make_async_remote_copy(
             src_ref=part,
             dst_ref=slots.at[s - 1],
             send_sem=psend,
             recv_sem=precv,
-            device_id=peer(s),
+            device_id=who,
         )
 
     def send_edges(wanted):
@@ -402,36 +414,19 @@
                 given(sends(*d), lambda: edge(i).start())
 
     with jax.named_scope("level0"):
-        await_tables("line", "first")
-        line = table("line")
-        sums = [[0.0] * own_tiles, [0.0] * own_tiles]
         for k in range(CHUNKS):
             both = pl.ds(0, 2 * step)
             pltpu.make_async_copy(h_ref.at[both, :], h_buf.at[both, pl.ds(0, nc)], own_sem.at[k]).wait()
-            weights = table("first", 0, (k * step, (k + 1) * step))
             for c in range(own_tiles):
-                moved, numer, weight = level0(HALO + k * step, step, c)
-                q0[c, k * step : (k + 1) * step, :] = moved
-                for a, x in enumerate((numer, weight)):
-                    x = (x * weights).reshape(step // 8, 8, LANES)
-                    sums[a][c] = sums[a][c] + jnp.sum(x, axis=0)
-        flat = []
-        for a in range(2):
-            x = sum(sums[a][c] * line[0:1, c * LANES : (c + 1) * LANES] for c in range(own_tiles))
-            x = jnp.sum(x, axis=0, keepdims=True)
-            flat.append(x + pltpu.roll(x, LANES // 2, axis=1))
-        lane1 = lax.broadcasted_iota(jnp.int32, (1, LANES), 1)
-        part[...] = jnp.where(lane1 < LANES // 2, flat[0], flat[1])
+                q0[c, k * step : (k + 1) * step, :] = level0(HALO + k * step, step, c)
+
+    lane1 = lax.broadcasted_iota(jnp.int32, (1, LANES), 1)
 
     def meet():
         with jax.named_scope("meet"):
             pl.semaphore_wait(barrier, everyone - 1)
 
-        def tell(s, carry):
-            summary(s).start()
-            return carry
-
-        lax.fori_loop(1, everyone, tell, 0)
+        others(lambda s, who: summary(s, who).start())
 
     def taps(src, c, start, count):
         x = [src[c, pl.ds(start + a, count, stride=2), :] for a in range(-2, 3)]
@@ -469,7 +464,20 @@
                 ends2(two, c)
                 three[c] = taps(two, c, 4, m3)
 
-    meet()
+    with jax.named_scope("sums"):
+        await_tables("line", "first")
+        flat = []
+        for x in (n3, d3):
+            y = sum(x[c] * table("line", 0, (0, 1))[:, c * LANES : (c + 1) * LANES] for c in range(own_tiles))
+            y = jnp.sum(y * table("first"), axis=0, keepdims=True)
+            flat.append(y + pltpu.roll(y, LANES // 2, axis=1))
+        part[...] = jnp.where(lane1 < LANES // 2, flat[0], flat[1])
+
+    early_half = cz < nz // 2 if nz > 1 else None
+    if early_half is None:
+        meet()
+    else:
+        pl.when(jnp.logical_not(early_half))(meet)
     def wide_of(x, rows, tiles):
         return jnp.concatenate([x[c, rows, :] for c in tiles], axis=1)
 
@@ -508,7 +516,13 @@
         x = dot(rall, high) + dot(rall, low)
         x = jnp.concatenate([x[: stack - s6], x[stack - s6 : stack] + x[stack : stack + s6]], axis=0)
         high, low = split(jnp.concatenate([x[:, :LANES], x[:, LANES:]], axis=0))
-        x = dot(high, table("call", 0)) + dot(low, table("call", 0)) + dot(high, table("call", 1))
+        x = dot(high, table("call", 0)) + dot(low, table("call", 0))
+        tail = stack - 32
+        more = [dot(high[a * stack + tail : (a + 1) * stack], table("call", 1)) for a in range(2)]
+        x = jnp.concatenate(
+            [y for a in range(2) for y in (x[a * stack : a * stack + tail], x[a * stack + tail : (a + 1) * stack] + more[a])],
+            axis=0,
+        )
 
     base_g = size1 + size2
 
@@ -529,6 +543,15 @@
             return right(y, table(name))
 
         own1, own2 = own_ends(n1, d1, last1, "c1"), own_ends(n2, d2, last2, "c2")
+
+    with jax.named_scope("edge_side"):
+        side_ends = []
+        for k in range(1, 1 + ns):
+            pair = []
+            for n, d, last, name in ((n1, d1, last1, "s1"), (n2, d2, last2, "s2")):
+                y = right(ends(n, near_tile[k], last), table(name, 2 * (k - 1)))
+                pair.append(y + right(ends(d, near_tile[k], last), table(name, 2 * (k - 1) + 1)))
+            side_ends.append(pair)
 
     def tile(x, at, c):
         return x[at : at + 8, c * LANES : (c + 1) * LANES]
@@ -572,16 +595,15 @@
                     for t in range(OWN_TILES):
                         edge_s[rp - 1, 0, t] = pack(packed[0][t], packed[1][t])
                 else:
-                    lines = []
-                    for n, d, last, name in ((n1, d1, last1, "s1"), (n2, d2, last2, "s2")):
-                        first = 8 if rp == 2 else last
-                        y = right(n[near_tile[k], first : first + 8, :], table(name, 2 * (k - 1) + 0))
-                        lines.append(y + right(d[near_tile[k], first : first + 8, :], table(name, 2 * (k - 1) + 1)))
+                    lines = [y[at : at + 8] for y in side_ends[k - 1]]
                     edge_s[rp - 1, k, 0] = pack(deep[0][0], deep[1][0])
                     edge_s[rp - 1, k, 1] = (
                         lines[0] + pltpu.roll(lines[1], 8, axis=1)
                         + pltpu.roll(pack(deep[0][1], deep[1][1]), 16, axis=1)
                     )
+
+    if early_half is not None:
+        pl.when(early_half)(meet)
 
     with jax.named_scope("send"):
         send_edges(lambda d: d[0] != 0)
@@ -637,9 +659,50 @@
         q_rows(x1, y1, slice(0, size1), gain1)
         q_rows(x2, y2, slice(0, size2), gain2)
 
+    def grow_rows(src, dst, first, count):
+        x, y, w = (src[first + k : first + k + count, :] for k in (1, 2, 3))
+        dst[pl.ds(2 * first, count, stride=2), :] = 0.125 * (x + w) + 0.75 * y
+        dst[pl.ds(2 * first + 1, count, stride=2), :] = 0.5 * (y + w)
+
+    def block(x, c, p, first):
+        ok = jnp.logical_or(line8 >= 4, up) if first else jnp.logical_or(line8 < 4, down)
+        x[c, p : p + 8, :] = jnp.where(ok, x[c, p : p + 8, :], 0.0)
+
+    tiles2 = range(x2.shape[1])
+
+    def mask_ends():
+        for c in tiles2:
+            block(z1b, c, 0, True)
+            block(z1b, c, nr // 2, False)
+
+    def upward(parts):
+        z = jnp.concatenate([jnp.concatenate([z1b[c, p, :] for c in tiles2], axis=1) for p in parts], axis=0)
+        z = right(z, table("e1")) + jnp.concatenate([y1[p, :] for p in parts], axis=0)
+        return right(z, table("e0"))
+
+    with jax.named_scope("factor"):
+        shape = (stack, 256)
+        at_row = level_of(shape, 0, tops[1:])
+        at_col = level_of(shape, 1, lane_cuts)
+        gains = [gain_ref[level] - gain_ref[level - 1] for level in (3, 4, 5)] + [-gain_ref[5]]
+        value = jnp.where(
+            at_row == 0, gains[0], jnp.where(at_row == 1, gains[1], jnp.where(at_row == 2, gains[2], gains[3]))
+        )
+        factor[...] = jnp.where(at_row == at_col, value, 0.0)
+
+    with jax.named_scope("base"):
+        await_tables("e1", "e0")
+        for c in tiles2:
+            z2b[c] = y2[:, c * LANES : (c + 1) * LANES]
+            grow_rows(z2b.at[c], z1b.at[c], 0, nr // 4 + 8)
+        mask_ends()
+        base = upward((slice(0, size1),))
+        for c in own_range:
+            wide[c] = base[:, c * LANES : (c + 1) * LANES]
+
     with jax.named_scope("w_edges"):
         await_edges(lambda d: d[0] != 0)
-        await_tables("ec", "e2", "e1", "e0", "er", "second")
+        await_tables("ec0", "r12", "er", "second")
     packed_lanes = jnp.logical_and(lane8 % (LANES // 2) >= MIDDLE[0], lane8 % (LANES // 2) <= MIDDLE[-1])
     with jax.named_scope("edges"):
         for rp, at1, at2, firsts in ((1, 0, 0, tops), (2, nr // 2, nr // 4, bottoms)):
@@ -676,51 +739,28 @@
         for x, y, at, gain in ((x1, y1, nr // 2, gain1), (x2, y2, nr // 4, gain2)):
             q_rows(x, y, slice(0, 8), gain)
             q_rows(x, y, slice(at, at + 8), gain)
+    with jax.named_scope("fix"):
+        for c in tiles2:
+            for at in (0, nr // 4):
+                z2b[c, at : at + 8, :] = y2[at : at + 8, c * LANES : (c + 1) * LANES]
+                grow_rows(z2b.at[c], z1b.at[c], at, 8)
+        mask_ends()
+        parts = (slice(0, 16), slice(nr // 2, nr // 2 + 16))
+        base = upward(parts)
+        for c in own_range:
+            for i, p in enumerate(parts):
+                wide[c, p, :] = base[16 * i : 16 * i + 16, c * LANES : (c + 1) * LANES]
 
     with jax.named_scope("deep"):
-        shape = (stack, 256)
-        at_row = level_of(shape, 0, tops[1:])
-        at_col = level_of(shape, 1, lane_cuts)
-        gains = [gain_ref[level] - gain_ref[level - 1] for level in (3, 4, 5)] + [-gain_ref[5]]
-        factor = jnp.where(
-            at_row == 0, gains[0], jnp.where(at_row == 1, gains[1], jnp.where(at_row == 2, gains[2], gains[3]))
-        )
         n, d = (jnp.concatenate([g[a, 0], g[a, 1]], axis=1) for a in range(2))
-        x = jnp.where(jnp.logical_and(at_row == at_col, d > 0), factor * (n / d), 0.0)
+        x = jnp.where(d > 0, factor[...] * (n / d), 0.0)
         high, low = split(x)
         er = [table("er", k) for k in (0, 1)]
         x = dot(er[0], high) + dot(er[0], low) + dot(er[1], high)
         high, low = split(x)
-        ec = [table("ec", k) for k in (0, 1)]
-        z3 = dot(high, ec[0]) + dot(low, ec[0]) + dot(high, ec[1])
-
-    with jax.named_scope("z2"):
-        z3b[0:m3, :] = z3
-
-        def grow_rows(src, dst, put, get, count):
-            x, y, w = (src[get + (slice(k, k + count), slice(None))] for k in (1, 2, 3))
-            dst[put + (pl.ds(0, count, stride=2), slice(None))] = 0.125 * (x + w) + 0.75 * y
-            dst[put + (pl.ds(1, count, stride=2), slice(None))] = 0.5 * (y + w)
-
-        def block(x, put, p, first):
-            ok = jnp.logical_or(line8 >= 4, up) if first else jnp.logical_or(line8 < 4, down)
-            x[put + (slice(p, p + 8), slice(None))] = jnp.where(ok, x[put + (slice(p, p + 8), slice(None))], 0.0)
-
-        grow_rows(z3b, z2b, (0,), (), nr // 8 + 8)
-        block(z2b, (0,), 0, True)
-        block(z2b, (0,), nr // 4, False)
-        z2 = right(z2b[0], table("e2")) + y2[...]
-        tiles2 = z2.shape[1] // LANES
-        for c in range(tiles2):
-            z2b[c] = z2[:, c * LANES : (c + 1) * LANES]
-    with jax.named_scope("z1"):
-        for c in range(tiles2):
-            grow_rows(z2b, z1b, (c,), (c,), nr // 4 + 8)
-            block(z1b, (c,), 0, True)
-            block(z1b, (c,), nr // 2, False)
-        z1 = right(wide_of(z1b, slice(None), range(tiles2)), table("e1")) + y1[...]
-    with jax.named_scope("e0"):
-        full = right(z1, table("e0"))
+        x = dot(high, table("ec0")) + dot(low, table("ec0")) + dot(high, table("ec0", 1))
+        high, low = split(x)
+        full = dot(table("r12"), high) + dot(table("r12"), low)
 
     with jax.named_scope("w_top"):
         everything = pltpu.make_async_copy(slots, slots, precv)
@@ -730,10 +770,10 @@
         total = part[...] + jnp.sum(slots[...], axis=0)
         top_sum = jnp.sum(jnp.where(lane1 < LANES // 2, total, 0.0), axis=1, keepdims=True)
         top_weight = jnp.sum(jnp.where(lane1 < LANES // 2, 0.0, total), axis=1, keepdims=True)
-        top_line = (top_sum / top_weight) * line[1:2, :]
+        top_line = (top_sum / top_weight) * table("line", 0, (1, 2))
         for c in own_range:
             cols = slice(c * LANES, (c + 1) * LANES)
-            wide[c] = full[:, cols] + table("second") * top_line[:, cols]
+            wide[c] = wide[c] + (full[:, cols] + table("second") * top_line[:, cols])
     with jax.named_scope("out"):
         gain = gain_ref[0]
         chunk = 32
@@ -785,13 +825,13 @@
             pltpu.VMEM((2, tiles1, size1, LANES), F32),
             pltpu.VMEM((2, tiles2, size2, LANES), F32),
             pltpu.VMEM((2, 2, stack, LANES), F32),
+            pltpu.VMEM((stack, 256), F32),
             pltpu.VMEM((size1, tiles1 * LANES), F32),
             pltpu.VMEM((size2, tiles2 * LANES), F32),
             pltpu.VMEM((ns, beside, LANES), F32),
             pltpu.VMEM((ns, beside, LANES), F32),
             pltpu.VMEM((2, 1 + ns, OWN_TILES, 8, LANES), F32),
             pltpu.VMEM((2, 1 + ns, OWN_TILES, 8, LANES), F32),
-            pltpu.VMEM((m3 + 8, LANES), F32),
             pltpu.VMEM((tiles2, nr // 4 + 16, LANES), F32),
             pltpu.VMEM((tiles2, nr // 2 + 16, LANES), F32),
             pltpu.VMEM((own_tiles, nr // 2 + 16, LANES), F32),

time: 15.8 us -> 14.2 us (0.90)
  Pallas kernels: 14.6 us -> 13.1 us
    pallas_call x1, Pallas kernels: 14.6 us -> 13.1 us  [local(): pl.pallas_call(functools.partial(kernel, sizes, places), out_shape=pltpu....]
where the time goes in v5:
time: 14.2 us; the launch traced here: 14 us
  Pallas kernels  13.1 us (92%)
  local copies, waits for them, and re-layouts  0.97 us (7%)
    pallas_call x1, Pallas kernels, local(): pl.pallas_call(functools.partial(kernel, sizes, places), out_shape=pltpu....  13.1 us
    unnamed x1, local copies, waits for them, and re-layouts  0.97 us

profile of v5, /device:TPU:5, one launch (start us, length us, event | category | flops | bytes accessed | tf_op | source)
XLA Modules:
  0.0 14.0 jit_solution(17109632764479556531)
XLA Ops:
  0.0 13.1 %shard_map.190 = f32[512,512]{1,0:T(8,128)S(1)} custom-call(f32[16]{0:T(128)} %off_hbm.1, f32[16]{0:T(128)} %wgt_hbm.1, f32[6]{0:T(128)} %gain_hbm.1, f32[512,512]{1,0:T(8,128)} %h_ref.1, s32[512,512]{1,0:T(8,128)} %s_ref.1, bf16[2,1024,256]{2,1,0:T(8,128)(2,1)} %constant.60.rest_0_, bf16[2,640,512]{2,1,0:T(8,128)(2,1)} %constant.64.rest_1_, ...), custom_call_target="tpu_custom_call" | custom-call | tf_op jit(solution)/shard_map/pallas_call | solution.py:806
  13.1 1.0 %copy.22 = f32[512,512]{1,0:T(8,128)} copy(f32[512,512]{1,0:T(8,128)S(1)} %shard_map.190) | data formatting | bytes 2097152

commit v6 on v5

--- a/solution.py
+++ b/solution.py
@@ -150,12 +150,15 @@
     rall = np.concatenate([high, low[-size6:]], axis=0)
     rall = pad(rall, (-(-rall.shape[0] // 16) * 16, o3.size))
     back = ax.back()
-    er = np.stack([x.astype(np.float64) for x in halves(back.T)])
+    deep_rows = -(-o3.size // 16) * 16
+    er = np.stack([pad(x.astype(np.float64), (deep_rows, x.shape[1])) for x in halves(back.T)])
     first = np.repeat(ax.sums(3, o3)[:, None], LANES, 1)
-    w2 = ax.window(2, 8)
-    r12 = (ax.grow(o3, w2, 2) @ ax.grow(w2, np.arange(-4, n // 2 + 12), 1)).T
-    second = np.repeat(pad(ax.ones(1), (n // 2 + 16,))[:, None], LANES, 1)
-    return dict(rall=rall, er=er, r12=r12), dict(first=first, second=second)
+    w1, w2 = ax.window(1, 8), ax.window(2, 8)
+    r012 = (ax.grow(o3, w2, 2) @ ax.grow(w2, w1, 1) @ ax.grow(w1, np.arange(n), 0)).T
+    high, low = (pad(x.astype(np.float64), (n, deep_rows)) for x in halves(r012))
+    r012 = np.concatenate([high, low, high], axis=1)
+    second = np.repeat(pad(ax.ones(3), (deep_rows,))[:, None], LANES, 1)
+    return dict(rall=rall, er=er, r012=r012), dict(first=first, second=second)
 
 
 def tables(nr, nc, nx, blocks):
@@ -213,7 +216,7 @@
 
 
 COLS = (("c03", "c2"), ("call", "e0"), ("c1", "e1"), ("s1", "s2"), ("ec0",), ("line",))
-ROWS = (("rall", "er", "r12"), ("first", "second"))
+ROWS = (("rall", "er", "r012"), ("first", "second"))
 OWN_TILES, SIDE_TILES = 5, 2
 CHUNKS = 4
 
@@ -227,7 +230,7 @@
     out_ref, rest = rest[0], rest[1:]
     tab, rest = rest[:count], rest[count:]
     (
-        off_ref, wgt_ref, gain_ref, h_buf, s_buf, q0, num, den, n1, d1, n2, d2, n3, d3,
+        off_ref, wgt_ref, gain_ref, h_buf, s_buf, q0, num, den, out0, n1, d1, n2, d2, n3, d3,
         x1, x2, g, factor, y1, y2, side_s, side_r, edge_s, edge_r, z2b, z1b, wide, part, slots,
         own_sem, tab_sem, send0, recv0, psend, precv,
     ) = rest
@@ -413,55 +416,68 @@
             if wanted(d):
                 given(sends(*d), lambda: edge(i).start())
 
+    lane1 = lax.broadcasted_iota(jnp.int32, (1, LANES), 1)
+
+    def meet():
+        with jax.named_scope("meet"):
+            pl.semaphore_wait(barrier, everyone - 1)
+
+        others(lambda s, who: summary(s, who).start())
+
+    def taps(src, c, start, count):
+        x = [src[c, pl.ds(start + a, count, stride=2), :] for a in range(-2, 3)]
+        return 0.375 * x[2] + (0.25 * (x[1] + x[3]) + 0.0625 * (x[0] + x[4]))
+
+    def hold(x, c, p, first):
+        if first:
+            ok = jnp.logical_or(line8 >= 4, up)
+        else:
+            ok = jnp.logical_or(line8 < 4, down)
+        x[c, p : p + 8, :] = jnp.where(ok, x[c, p : p + 8, :], 0.0)
+
+    last1, last2 = nr // 2 + 8, nr // 4 + 8
+
+    def rows1(src, dst, c, p, count):
+        dst[c, p : p + count, :] = taps(src, c, 2 * p - 8, count)
+
+    def rows2(src, dst, c, p, count):
+        dst[c, p : p + count, :] = taps(src, c, 2 * p - 12, count)
+
+    pairs = ((num, n1, n2, n3), (den, d1, d2, d3))
+    part1, part2 = step // 2, nr // 8
+
+    def group1(k):
+        count = part1 if k < CHUNKS - 1 else part1 + 16
+        for src, one, _, _ in pairs:
+            for c in range(own_tiles):
+                rows1(src, one, c, 8 + k * part1, count)
+                if k == 0:
+                    hold(one, c, 8, True)
+                if k == CHUNKS - 1:
+                    hold(one, c, last1, False)
+
+    def group2(k):
+        for _, one, two, _ in pairs:
+            for c in range(own_tiles):
+                rows2(one, two, c, 8 + k * part2, part2 + 8 * k)
+                hold(two, c, last2 if k else 8, not k)
+
     with jax.named_scope("level0"):
         for k in range(CHUNKS):
             both = pl.ds(0, 2 * step)
             pltpu.make_async_copy(h_ref.at[both, :], h_buf.at[both, pl.ds(0, nc)], own_sem.at[k]).wait()
             for c in range(own_tiles):
                 q0[c, k * step : (k + 1) * step, :] = level0(HALO + k * step, step, c)
-
-    lane1 = lax.broadcasted_iota(jnp.int32, (1, LANES), 1)
-
-    def meet():
-        with jax.named_scope("meet"):
-            pl.semaphore_wait(barrier, everyone - 1)
-
-        others(lambda s, who: summary(s, who).start())
-
-    def taps(src, c, start, count):
-        x = [src[c, pl.ds(start + a, count, stride=2), :] for a in range(-2, 3)]
-        return 0.375 * x[2] + (0.25 * (x[1] + x[3]) + 0.0625 * (x[0] + x[4]))
-
-    def hold(x, c, p, first):
-        if first:
-            ok = jnp.logical_or(line8 >= 4, up)
-        else:
-            ok = jnp.logical_or(line8 < 4, down)
-        x[c, p : p + 8, :] = jnp.where(ok, x[c, p : p + 8, :], 0.0)
-
-    last1, last2 = nr // 2 + 8, nr // 4 + 8
-
-    def ends1(x, c):
-        hold(x, c, 8, True)
-        hold(x, c, last1, False)
-
-    def ends2(x, c):
-        hold(x, c, 8, True)
-        hold(x, c, last2, False)
-
-    def rows1(src, dst, c, p, count):
-        dst[c, p : p + count, :] = taps(src, c, 2 * p - 8, count)
-
-    def rows2(src, dst, c, p, count):
-        dst[c, p : p + count, :] = taps(src, c, 2 * p - 12, count)
+            if k:
+                group1(k - 1)
+            if k == CHUNKS - 1:
+                group2(0)
 
     with jax.named_scope("rowpyr"):
-        for src, one, two, three in ((num, n1, n2, n3), (den, d1, d2, d3)):
+        group1(CHUNKS - 1)
+        group2(1)
+        for _, _, two, three in pairs:
             for c in range(own_tiles):
-                rows1(src, one, c, 8, nr // 2 + 16)
-                ends1(one, c)
-                rows2(one, two, c, 8, nr // 4 + 8)
-                ends2(two, c)
                 three[c] = taps(two, c, 4, m3)
 
     with jax.named_scope("sums"):
@@ -515,14 +531,14 @@
         rall = table("rall")
         x = dot(rall, high) + dot(rall, low)
         x = jnp.concatenate([x[: stack - s6], x[stack - s6 : stack] + x[stack : stack + s6]], axis=0)
-        high, low = split(jnp.concatenate([x[:, :LANES], x[:, LANES:]], axis=0))
-        x = dot(high, table("call", 0)) + dot(low, table("call", 0))
-        tail = stack - 32
-        more = [dot(high[a * stack + tail : (a + 1) * stack], table("call", 1)) for a in range(2)]
-        x = jnp.concatenate(
-            [y for a in range(2) for y in (x[a * stack : a * stack + tail], x[a * stack + tail : (a + 1) * stack] + more[a])],
-            axis=0,
-        )
+        def across(y):
+            y = jnp.concatenate([y[:, :LANES], y[:, LANES:]], axis=0)
+            high, low = split(y)
+            return high, dot(high, table("call", 0)) + dot(low, table("call", 0))
+
+        rows_all = x
+        high, y = across(jnp.concatenate([x[f : f + 8] for firsts in (bottoms, tops) for f in firsts], axis=0))
+        deep_ends = y + dot(high, table("call", 1))
 
     base_g = size1 + size2
 
@@ -558,23 +574,15 @@
 
     with jax.named_scope("g_pack"):
         for k in range(1 + ns):
-            piece = [
-                [x[a * stack : (a + 1) * stack, k * 256 + c * LANES : k * 256 + (c + 1) * LANES] for c in (0, 1)]
-                for a in (0, 1)
-            ]
-            for a in range(2):
-                for c in range(2):
-                    if k == 0:
-                        g[a, c] = piece[a][c]
-                    else:
-                        side_s[k - 1, base_g + (2 * a + c) * stack : base_g + (2 * a + c + 1) * stack, :] = piece[a][c]
-            for rp, firsts in ((1, bottoms), (2, tops)):
+            for rp in (1, 2):
                 deep = []
                 for a in range(2):
                     lines = []
                     for c in range(2):
                         index = lane8 + c * LANES
-                        b = [piece[a][c][f : f + 8] for f in firsts]
+                        first = a * 64 + (rp - 1) * 32
+                        lane = k * 256 + c * LANES
+                        b = [deep_ends[first + 8 * l : first + 8 * l + 8, lane : lane + LANES] for l in range(4)]
                         lines.append(
                             jnp.where(
                                 index < lane_cuts[0], b[0],
@@ -610,6 +618,24 @@
 
     body1, body2 = slice(8, 8 + size1), slice(8, 8 + size2)
 
+    with jax.named_scope("g"):
+        high, y = across(rows_all)
+        tail = stack - 32
+        more = [dot(high[a * stack + tail : (a + 1) * stack], table("call", 1)) for a in range(2)]
+        for a in range(2):
+            for c in range(2):
+                for k in range(1 + ns):
+                    lanes_ = slice(k * 256 + c * LANES, k * 256 + (c + 1) * LANES)
+                    upper = y[a * stack : a * stack + tail, lanes_]
+                    lower = y[a * stack + tail : (a + 1) * stack, lanes_] + more[a][:, lanes_]
+                    if k == 0:
+                        g[a, c, :tail] = upper
+                        g[a, c, tail:] = lower
+                    else:
+                        first = base_g + (2 * a + c) * stack
+                        side_s[k - 1, first : first + tail, :] = upper
+                        side_s[k - 1, first + tail : first + stack, :] = lower
+
     with jax.named_scope("x_side"):
         for k in range(1, 1 + ns):
             for base, n, d, body, name in ((0, n1, d1, body1, "s1"), (size1, n2, d2, body2, "s2")):
@@ -675,6 +701,14 @@
             block(z1b, c, 0, True)
             block(z1b, c, nr // 2, False)
 
+    gain0 = gain_ref[0]
+
+    def rise(c, m, count):
+        x, y, w = (wide[c, m + k : m + k + count, :] for k in (3, 4, 5))
+        even, odd = pl.ds(2 * m, count, stride=2), pl.ds(2 * m + 1, count, stride=2)
+        out0[c, even, :] = gain0 * q0[c, even, :] + (0.125 * (x + w) + 0.75 * y)
+        out0[c, odd, :] = gain0 * q0[c, odd, :] + 0.5 * (y + w)
+
     def upward(parts):
         z = jnp.concatenate([jnp.concatenate([z1b[c, p, :] for c in tiles2], axis=1) for p in parts], axis=0)
         z = right(z, table("e1")) + jnp.concatenate([y1[p, :] for p in parts], axis=0)
@@ -699,10 +733,13 @@
         base = upward((slice(0, size1),))
         for c in own_range:
             wide[c] = base[:, c * LANES : (c + 1) * LANES]
+        for c in own_range:
+            for m in range(0, nr // 2, 32):
+                rise(c, m, 32)
 
     with jax.named_scope("w_edges"):
         await_edges(lambda d: d[0] != 0)
-        await_tables("ec0", "r12", "er", "second")
+        await_tables("ec0", "r012", "er", "second")
     packed_lanes = jnp.logical_and(lane8 % (LANES // 2) >= MIDDLE[0], lane8 % (LANES // 2) <= MIDDLE[-1])
     with jax.named_scope("edges"):
         for rp, at1, at2, firsts in ((1, 0, 0, tops), (2, nr // 2, nr // 4, bottoms)):
@@ -750,6 +787,8 @@
         for c in own_range:
             for i, p in enumerate(parts):
                 wide[c, p, :] = base[16 * i : 16 * i + 16, c * LANES : (c + 1) * LANES]
+            rise(c, 0, 8)
+            rise(c, nr // 2 - 8, 8)
 
     with jax.named_scope("deep"):
         n, d = (jnp.concatenate([g[a, 0], g[a, 1]], axis=1) for a in range(2))
@@ -759,8 +798,6 @@
         x = dot(er[0], high) + dot(er[0], low) + dot(er[1], high)
         high, low = split(x)
         x = dot(high, table("ec0")) + dot(low, table("ec0")) + dot(high, table("ec0", 1))
-        high, low = split(x)
-        full = dot(table("r12"), high) + dot(table("r12"), low)
 
     with jax.named_scope("w_top"):
         everything = pltpu.make_async_copy(slots, slots, precv)
@@ -771,19 +808,19 @@
         top_sum = jnp.sum(jnp.where(lane1 < LANES // 2, total, 0.0), axis=1, keepdims=True)
         top_weight = jnp.sum(jnp.where(lane1 < LANES // 2, 0.0, total), axis=1, keepdims=True)
         top_line = (top_sum / top_weight) * table("line", 0, (1, 2))
-        for c in own_range:
-            cols = slice(c * LANES, (c + 1) * LANES)
-            wide[c] = wide[c] + (full[:, cols] + table("second") * top_line[:, cols])
+        ones = table("second")
+        x = x + jnp.concatenate(
+            [ones * top_line[:, c * LANES : (c + 1) * LANES] for c in own_range], axis=1
+        )
+        high, low = split(x)
+        x = jnp.concatenate([high, high, low], axis=0)
     with jax.named_scope("out"):
-        gain = gain_ref[0]
-        chunk = 32
-        for c in own_range:
-            for m in range(0, nr // 2, chunk):
-                x, y, w = (wide[c, pl.ds(m + k, chunk), :] for k in (3, 4, 5))
-                even, odd = pl.ds(2 * m, chunk, stride=2), pl.ds(2 * m + 1, chunk, stride=2)
-                q0[c, even, :] = gain * q0[c, even, :] + (0.125 * (x + w) + 0.75 * y)
-                q0[c, odd, :] = gain * q0[c, odd, :] + 0.5 * (y + w)
-                out_ref[pl.ds(2 * m, 2 * chunk), c * LANES : (c + 1) * LANES] = q0[c, pl.ds(2 * m, 2 * chunk), :]
+        for r in range(0, nr, 128):
+            y = dot(table("r012", 0, (r, r + 128)), x)
+            for c in own_range:
+                out_ref[r : r + 128, c * LANES : (c + 1) * LANES] = (
+                    out0[c, r : r + 128, :] + y[:, c * LANES : (c + 1) * LANES]
+                )
 
 
 def local(mesh_shape, heights, scene_ids, scene_offset, scene_weight, band_gain):
@@ -818,6 +855,7 @@
             pltpu.VMEM((own_tiles, nr, LANES), F32),
         ]
         + [pltpu.VMEM((tiles, nr + 3 * HALO, LANES), F32)] * 2
+        + [pltpu.VMEM((own_tiles, nr, LANES), F32)]
         + [pltpu.VMEM((tiles, nr // 2 + 32, LANES), F32)] * 2
         + [pltpu.VMEM((tiles, nr // 4 + 24, LANES), F32)] * 2
         + [pltpu.VMEM((own_tiles, m3, LANES), F32)] * 2

time: 14.2 us -> 13.7 us (0.965)
  Pallas kernels: 13.1 us -> 12.6 us
    pallas_call x1, Pallas kernels: 13.1 us -> 12.6 us  [local(): pl.pallas_call(functools.partial(kernel, sizes, places), out_shape=pltpu....]
where the time goes in v6:
time: 13.7 us; the launch traced here: 13.6 us
  Pallas kernels  12.6 us (92%)
  local copies, waits for them, and re-layouts  0.97 us (7%)
    pallas_call x1, Pallas kernels, local(): pl.pallas_call(functools.partial(kernel, sizes, places), out_shape=pltpu....  12.6 us
    unnamed x1, local copies, waits for them, and re-layouts  0.97 us

profile of v6, /device:TPU:5, one launch (start us, length us, event | category | flops | bytes accessed | tf_op | source)
XLA Modules:
  0.0 13.6 jit_solution(17157054013428834634)
XLA Ops:
  0.0 12.6 %shard_map.190 = f32[512,512]{1,0:T(8,128)S(1)} custom-call(f32[16]{0:T(128)} %off_hbm.1, f32[16]{0:T(128)} %wgt_hbm.1, f32[6]{0:T(128)} %gain_hbm.1, f32[512,512]{1,0:T(8,128)} %h_ref.1, s32[512,512]{1,0:T(8,128)} %s_ref.1, bf16[2,1024,256]{2,1,0:T(8,128)(2,1)} %constant.58.rest_0_, bf16[2,640,512]{2,1,0:T(8,128)(2,1)} %constant.62.rest_1_, ...), custom_call_target="tpu_custom_call" | custom-call | tf_op jit(solution)/shard_map/pallas_call | solution.py:843
  12.6 1.0 %copy.22 = f32[512,512]{1,0:T(8,128)} copy(f32[512,512]{1,0:T(8,128)S(1)} %shard_map.190) | data formatting | bytes 2097152

commit v7 on v6

--- a/solution.py
+++ b/solution.py
@@ -131,13 +131,14 @@
     call = []
     for d in [0] + shifts:
         call.append([pad(x.astype(np.float64), (LANES, 256)) for x in halves(ax.deep(three, d))])
-    call = np.stack([np.concatenate([x[k] for x in call], axis=1) for k in range(2)])
+    high, low = (np.concatenate([x[k] for x in call], axis=1) for k in range(2))
+    call = np.concatenate([high, high, low], axis=0)
     back = ax.back()
     to0 = ax.grow(w2, w1, 1) @ ax.grow(w1, own, 0)
     ec0 = np.stack([pad(x.astype(np.float64), (256, n)) for x in halves(back @ ax.grow(o3, w2, 2) @ to0)])
     return dict(
         c1=ax.shrink(own, out1, 1), c2=to2 @ ax.shrink(w1, out2, 2), s1=s1, s2=s2, c03=c03, call=call,
-        ec0=ec0, e1=ax.grow(out2, out1, 1), e0=ax.grow(out1, own, 0),
+        ec0=ec0, e0=np.concatenate([ax.grow(out2, out1, 1) @ ax.grow(out1, own, 0), ax.grow(out1, own, 0)], axis=0),
     ), dict(line=np.stack([ax.sums(0, own), ax.ones(0)[4:-4]]))
 
 
@@ -148,7 +149,8 @@
     high, low = (x.astype(np.float64) for x in halves(deep))
     size6 = ax.sizes()[3]
     rall = np.concatenate([high, low[-size6:]], axis=0)
-    rall = pad(rall, (-(-rall.shape[0] // 16) * 16, o3.size))
+    rall = pad(rall, (-(-rall.shape[0] // 16) * 16, -(-o3.size // 16) * 16))
+    rall = np.concatenate([rall, rall], axis=1)
     back = ax.back()
     deep_rows = -(-o3.size // 16) * 16
     er = np.stack([pad(x.astype(np.float64), (deep_rows, x.shape[1])) for x in halves(back.T)])
@@ -215,10 +217,10 @@
     return dot(high, c) + dot(low, c)
 
 
-COLS = (("c03", "c2"), ("call", "e0"), ("c1", "e1"), ("s1", "s2"), ("ec0",), ("line",))
+COLS = (("c03", "c2"), ("call", "e0"), ("c1",), ("s1", "s2"), ("ec0",), ("line",))
 ROWS = (("rall", "er", "r012"), ("first", "second"))
 OWN_TILES, SIDE_TILES = 5, 2
-CHUNKS = 4
+CHUNKS = 8
 
 
 def kernel(
@@ -358,6 +360,12 @@
             x[c, 0:8, :] = zero
             x[c, x.shape[1] - 8 :, :] = zero
 
+    for rp, cp in kinds:
+        if rp and comes(rp, cp) is not None:
+            @pl.when(jnp.logical_not(comes(rp, cp)))
+            def _():
+                edge_r[rp - 1, cp] = jnp.zeros((OWN_TILES, 8, LANES), F32)
+
     def edge(i):
         rp, cp = kinds[i]
         if rp == 0:
@@ -489,11 +497,12 @@
             flat.append(y + pltpu.roll(y, LANES // 2, axis=1))
         part[...] = jnp.where(lane1 < LANES // 2, flat[0], flat[1])
 
-    early_half = cz < nz // 2 if nz > 1 else None
+    early_half = jnp.logical_and(cz > 0, cz < nz // 2) if nz > 1 else None
+    first_plane = cz == 0
     if early_half is None:
         meet()
     else:
-        pl.when(jnp.logical_not(early_half))(meet)
+        pl.when(cz >= nz // 2)(meet)
     def wide_of(x, rows, tiles):
         return jnp.concatenate([x[c, rows, :] for c in tiles], axis=1)
 
@@ -516,7 +525,7 @@
         return jnp.where(middle, n, pltpu.roll(d, 4, axis=0))
 
     def unpack(x):
-        return jnp.where(middle, x, 0.0), jnp.where(middle, pltpu.roll(x, 4, axis=0), 0.0)
+        return [jnp.where(middle, x, 0.0), jnp.where(middle, pltpu.roll(x, 4, axis=0), 0.0)]
 
     def unpack_lanes(x):
         low = lax.broadcasted_iota(jnp.int32, x.shape, 1) < LANES // 2
@@ -528,17 +537,17 @@
         x = right(x, table("c03"))
         x = x[:, :LANES] + x[:, LANES:]
         high, low = split(jnp.concatenate([x[:m3], x[m3:]], axis=1))
-        rall = table("rall")
-        x = dot(rall, high) + dot(rall, low)
+        gap = jnp.zeros((-m3 % 16, 2 * LANES), BF16)
+        x = dot(table("rall"), jnp.concatenate([high, gap, low, gap], axis=0))
         x = jnp.concatenate([x[: stack - s6], x[stack - s6 : stack] + x[stack : stack + s6]], axis=0)
         def across(y):
             y = jnp.concatenate([y[:, :LANES], y[:, LANES:]], axis=0)
             high, low = split(y)
-            return high, dot(high, table("call", 0)) + dot(low, table("call", 0))
+            return high, dot(jnp.concatenate([high, low], axis=1), table("call", 0, (0, 2 * LANES)))
 
         rows_all = x
         high, y = across(jnp.concatenate([x[f : f + 8] for firsts in (bottoms, tops) for f in firsts], axis=0))
-        deep_ends = y + dot(high, table("call", 1))
+        deep_ends = y + dot(high, table("call", 0, (2 * LANES, 3 * LANES)))
 
     base_g = size1 + size2
 
@@ -614,14 +623,17 @@
         pl.when(early_half)(meet)
 
     with jax.named_scope("send"):
-        send_edges(lambda d: d[0] != 0)
+        if early_half is None:
+            send_edges(lambda d: d[0] != 0)
+        else:
+            pl.when(jnp.logical_not(first_plane))(lambda: send_edges(lambda d: d[0] != 0))
 
     body1, body2 = slice(8, 8 + size1), slice(8, 8 + size2)
 
     with jax.named_scope("g"):
         high, y = across(rows_all)
         tail = stack - 32
-        more = [dot(high[a * stack + tail : (a + 1) * stack], table("call", 1)) for a in range(2)]
+        more = [dot(high[a * stack + tail : (a + 1) * stack], table("call", 0, (2 * LANES, 3 * LANES))) for a in range(2)]
         for a in range(2):
             for c in range(2):
                 for k in range(1 + ns):
@@ -642,7 +654,10 @@
                 y = right(n[near_tile[k], body, :], table(name, 2 * (k - 1) + 0))
                 y = y + right(d[near_tile[k], body, :], table(name, 2 * (k - 1) + 1))
                 side_s[k - 1, base : base + y.shape[0], :] = y
-        send_edges(lambda d: d[0] == 0)
+        if early_half is None:
+            send_edges(lambda d: d[0] == 0)
+        else:
+            pl.when(jnp.logical_not(first_plane))(lambda: send_edges(lambda d: d[0] == 0))
 
     with jax.named_scope("x_own"):
         for n, d, body, name, dst in ((n1, d1, body1, "c1", x1), (n2, d2, body2, "c2", x2)):
@@ -650,6 +665,13 @@
                 y = right(wide_of(y, body, own_range), table(name))
                 for c in range(dst.shape[1]):
                     dst[a, c] = y[:, c * LANES : (c + 1) * LANES]
+
+    if early_half is not None:
+
+        @pl.when(first_plane)
+        def _():
+            meet()
+            send_edges(lambda d: True)
 
     def ratio(n, d):
         return jnp.where(d > 0, n / d, 0.0)
@@ -710,9 +732,9 @@
         out0[c, odd, :] = gain0 * q0[c, odd, :] + 0.5 * (y + w)
 
     def upward(parts):
-        z = jnp.concatenate([jnp.concatenate([z1b[c, p, :] for c in tiles2], axis=1) for p in parts], axis=0)
-        z = right(z, table("e1")) + jnp.concatenate([y1[p, :] for p in parts], axis=0)
-        return right(z, table("e0"))
+        z = [jnp.concatenate([z1b[c, p, :] for p in parts], axis=0) for c in tiles2]
+        z.append(jnp.concatenate([y1[p, :] for p in parts], axis=0))
+        return right(jnp.concatenate(z, axis=1), table("e0"))
 
     with jax.named_scope("factor"):
         shape = (stack, 256)
@@ -725,7 +747,7 @@
         factor[...] = jnp.where(at_row == at_col, value, 0.0)
 
     with jax.named_scope("base"):
-        await_tables("e1", "e0")
+        await_tables("e0")
         for c in tiles2:
             z2b[c] = y2[:, c * LANES : (c + 1) * LANES]
             grow_rows(z2b.at[c], z1b.at[c], 0, nr // 4 + 8)
@@ -743,36 +765,33 @@
     packed_lanes = jnp.logical_and(lane8 % (LANES // 2) >= MIDDLE[0], lane8 % (LANES // 2) <= MIDDLE[-1])
     with jax.named_scope("edges"):
         for rp, at1, at2, firsts in ((1, 0, 0, tops), (2, nr // 2, nr // 4, bottoms)):
-            for cp in range(1 + ns):
-
-                def add():
-                    got = edge_r.at[rp - 1, cp]
-                    tail = unpack(got[OWN_TILES - 1]) if cp == 0 else None
-                    if cp == 0:
-                        adds1 = [unpack(got[0]), unpack(got[1]), [jnp.where(lane8 < 8, y, 0.0) for y in tail]]
-                        adds2 = [
-                            unpack(got[2]),
-                            [jnp.where(lane8 < 8, pltpu.roll(y, LANES - 8, axis=1), 0.0) for y in tail],
-                        ]
-                        for x, at, adds in ((x1, at1, adds1), (x2, at2, adds2)):
-                            for c, more in enumerate(adds):
-                                for a in range(2):
-                                    x[a, c, at : at + 8, :] = x[a, c, at : at + 8, :] + more[a]
-                        deep = [unpack(got[3]), tail]
-                    else:
-                        y = got[1]
-                        both = ((x1, at1, into1[cp], y), (x2, at2, into2[cp], pltpu.roll(y, LANES - 8, axis=1)))
-                        for x, at, into, part_ in both:
-                            for a, more in enumerate(unpack_lanes(jnp.where(packed_lanes, part_, 0.0))):
-                                x[a, into, at : at + 8, :] = x[a, into, at : at + 8, :] + more
-                        deep = [unpack(got[0]), unpack(y)]
-                    deep[1] = [jnp.where(lane8 < 32, pltpu.roll(y, LANES - 16, axis=1), 0.0) for y in deep[1]]
-                    for c in range(2):
-                        for a, more in enumerate(deep[c]):
-                            for f in firsts:
-                                g[a, c, f : f + 8, :] = g[a, c, f : f + 8, :] + more
-
-                given(comes(rp, cp), add)
+            def moved_to(y, by, ok):
+                return [jnp.where(ok, pltpu.roll(z, LANES - by, axis=1), 0.0) for z in y]
+
+            got = edge_r.at[rp - 1, 0]
+            tail = unpack(got[OWN_TILES - 1])
+            adds1 = [unpack(got[0]), unpack(got[1]), [jnp.where(lane8 < 8, y, 0.0) for y in tail]]
+            adds2 = [unpack(got[2]), moved_to(tail, 8, lane8 < 8)]
+            deep = [unpack(got[3]), moved_to(tail, 16, lane8 < 32)]
+            for cp in range(1, 1 + ns):
+                y = edge_r[rp - 1, cp, 1]
+                for a, more in enumerate(unpack(edge_r[rp - 1, cp, 0])):
+                    deep[0][a] = deep[0][a] + more
+                for a, more in enumerate(moved_to(unpack(y), 16, lane8 < 32)):
+                    deep[1][a] = deep[1][a] + more
+            for x, at, adds in ((x1, at1, adds1), (x2, at2, adds2)):
+                for c, more in enumerate(adds):
+                    for a in range(2):
+                        x[a, c, at : at + 8, :] = x[a, c, at : at + 8, :] + more[a]
+            for cp in range(1, 1 + ns):
+                y = edge_r[rp - 1, cp, 1]
+                for x, at, into, z in ((x1, at1, into1[cp], y), (x2, at2, into2[cp], pltpu.roll(y, LANES - 8, axis=1))):
+                    for a, more in enumerate(unpack_lanes(jnp.where(packed_lanes, z, 0.0))):
+                        x[a, into, at : at + 8, :] = x[a, into, at : at + 8, :] + more
+            for c in range(2):
+                for a in range(2):
+                    for f in firsts:
+                        g[a, c, f : f + 8, :] = g[a, c, f : f + 8, :] + deep[c][a]
         for x, y, at, gain in ((x1, y1, nr // 2, gain1), (x2, y2, nr // 4, gain2)):
             q_rows(x, y, slice(0, 8), gain)
             q_rows(x, y, slice(at, at + 8), gain)

time: 13.7 us -> 13.3 us (0.971)
  the two profiles are of different devices: /device:TPU:5 before, /device:TPU:0 now
where the time goes in v7:
time: 13.3 us; the launch traced here: 13.2 us
  Pallas kernels  12.2 us (92%)
  local copies, waits for them, and re-layouts  0.97 us (7%)
    pallas_call x1, Pallas kernels, local(): pl.pallas_call(functools.partial(kernel, sizes, places), out_shape=pltpu....  12.2 us
    unnamed x1, local copies, waits for them, and re-layouts  0.97 us

profile of v7, /device:TPU:0, one launch (start us, length us, event | category | flops | bytes accessed | tf_op | source)
XLA Modules:
  0.0 13.2 jit_solution(15728937324042223174)
XLA Ops:
  0.0 12.2 %shard_map.181 = f32[512,512]{1,0:T(8,128)S(1)} custom-call(f32[16]{0:T(128)} %off_hbm.1, f32[16]{0:T(128)} %wgt_hbm.1, f32[6]{0:T(128)} %gain_hbm.1, f32[512,512]{1,0:T(8,128)} %h_ref.1, s32[512,512]{1,0:T(8,128)} %s_ref.1, bf16[2,1024,256]{2,1,0:T(8,128)(2,1)} %constant.55.rest_0_, bf16[2,1024,512]{2,1,0:T(8,128)(2,1)} %constant.58.rest_1_, ...), custom_call_target="tpu_custom_call" | custom-call | tf_op jit(solution)/shard_map/pallas_call | solution.py:862
  12.2 1.0 %copy.21 = f32[512,512]{1,0:T(8,128)} copy(f32[512,512]{1,0:T(8,128)S(1)} %shard_map.181) | data formatting | bytes 2097152

commit v8 on v7

--- a/solution.py
+++ b/solution.py
@@ -135,10 +135,14 @@
     call = np.concatenate([high, high, low], axis=0)
     back = ax.back()
     to0 = ax.grow(w2, w1, 1) @ ax.grow(w1, own, 0)
+    from1, from2 = ax.grow(out1, own, 0), ax.grow(out2, out1, 1) @ ax.grow(out1, own, 0)
+    m1, m2 = n // 2, n // 4
+    e0 = np.concatenate([from2[:m2], from1[:m1], from1[m1 : m1 + 8], from2[m2 : m2 + 8]], axis=0)
+    e0 = pad(e0, (m1 + m2 + LANES, n))
     ec0 = np.stack([pad(x.astype(np.float64), (256, n)) for x in halves(back @ ax.grow(o3, w2, 2) @ to0)])
     return dict(
         c1=ax.shrink(own, out1, 1), c2=to2 @ ax.shrink(w1, out2, 2), s1=s1, s2=s2, c03=c03, call=call,
-        ec0=ec0, e0=np.concatenate([ax.grow(out2, out1, 1) @ ax.grow(out1, own, 0), ax.grow(out1, own, 0)], axis=0),
+        ec0=ec0, e0=e0,
     ), dict(line=np.stack([ax.sums(0, own), ax.ones(0)[4:-4]]))
 
 
@@ -218,9 +222,10 @@
 
 
 COLS = (("c03", "c2"), ("call", "e0"), ("c1",), ("s1", "s2"), ("ec0",), ("line",))
-ROWS = (("rall", "er", "r012"), ("first", "second"))
+ROWS = (("rall", "er"), ("first", "second"), ("r012",))
 OWN_TILES, SIDE_TILES = 5, 2
-CHUNKS = 8
+CHUNKS = 4
+PIECES = 4
 
 
 def kernel(
@@ -229,10 +234,10 @@
     nr, nc, nx, ny, nz, ns = sizes
     count = len(COLS) + len(ROWS)
     tables_hbm, rest = rest[:count], rest[count:]
-    out_ref, rest = rest[0], rest[1:]
-    tab, rest = rest[:count], rest[count:]
+    out0, us_ref, r012_ref, rest = *rest[:3], rest[3:]
+    tab, rest = (*rest[: count - 1], r012_ref), rest[count - 1 :]
     (
-        off_ref, wgt_ref, gain_ref, h_buf, s_buf, q0, num, den, out0, n1, d1, n2, d2, n3, d3,
+        off_ref, wgt_ref, gain_ref, h_buf, s_buf, q0, num, den, n1, d1, n2, d2, n3, d3,
         x1, x2, g, factor, y1, y2, side_s, side_r, edge_s, edge_r, z2b, z1b, wide, part, slots,
         own_sem, tab_sem, send0, recv0, psend, precv,
     ) = rest
@@ -733,7 +738,14 @@
 
     def upward(parts):
         z = [jnp.concatenate([z1b[c, p, :] for p in parts], axis=0) for c in tiles2]
-        z.append(jnp.concatenate([y1[p, :] for p in parts], axis=0))
+        z += [
+            jnp.concatenate([y1[p, c * LANES : (c + 1) * LANES] for p in parts], axis=0)
+            for c in range(x1.shape[1])
+        ]
+        first, second = (lax.broadcasted_iota(jnp.int32, z[0].shape, 1) < k for k in (8, 16))
+        t2 = len(tiles2) - 1
+        ends = jnp.where(first, z[-1], jnp.where(second, pltpu.roll(z[t2], 8, axis=1), 0.0))
+        z = z[:t2] + z[t2 + 1 : -1] + [ends]
         return right(jnp.concatenate(z, axis=1), table("e0"))
 
     with jax.named_scope("factor"):
@@ -832,14 +844,23 @@
             [ones * top_line[:, c * LANES : (c + 1) * LANES] for c in own_range], axis=1
         )
         high, low = split(x)
-        x = jnp.concatenate([high, high, low], axis=0)
-    with jax.named_scope("out"):
-        for r in range(0, nr, 128):
-            y = dot(table("r012", 0, (r, r + 128)), x)
-            for c in own_range:
-                out_ref[r : r + 128, c * LANES : (c + 1) * LANES] = (
-                    out0[c, r : r + 128, :] + y[:, c * LANES : (c + 1) * LANES]
-                )
+        us_ref[...] = jnp.concatenate([high, high, low], axis=0)
+
+
+def last(base_ref, us_ref, rows_ref, out_ref, buf, sem):
+    nr, nc = buf.shape
+    step = nr // sem.shape[0]
+    writes = []
+    for k in range(sem.shape[0]):
+        here = slice(k * step, (k + 1) * step)
+        y = dot(rows_ref[here, :], us_ref[...])
+        for c in range(base_ref.shape[0]):
+            cols = slice(c * LANES, (c + 1) * LANES)
+            buf[here, cols] = base_ref[c, here, :] + y[:, cols]
+        writes.append(pltpu.make_async_copy(buf.at[here, :], out_ref.at[here, :], sem.at[k]))
+        writes[-1].start()
+    for write in writes:
+        write.wait()
 
 
 def local(mesh_shape, heights, scene_ids, scene_offset, scene_weight, band_gain):
@@ -859,12 +880,18 @@
     peers = nx * ny * nz - 1
     messages = 3 * (1 + ns) - 1
     hbm = pl.BlockSpec(memory_space=pltpu.HBM)
-    return pl.pallas_call(
+    deep_rows = made["r012"].shape[-1]
+    vmem = pl.BlockSpec(memory_space=pltpu.VMEM)
+    kept = pl.pallas_call(
         functools.partial(kernel, sizes, places),
-        out_shape=pltpu.VMEM((nr, nc), F32),
+        out_shape=(
+            pltpu.VMEM((own_tiles, nr, LANES), F32),
+            pltpu.VMEM((deep_rows, nc), BF16),
+            pltpu.VMEM((nr, deep_rows), BF16),
+        ),
         in_specs=[hbm] * (5 + len(given)),
-        out_specs=pl.BlockSpec(memory_space=pltpu.VMEM),
-        scratch_shapes=[pltpu.VMEM(x.shape[1:], x.dtype) for x in given]
+        out_specs=(vmem, vmem, vmem),
+        scratch_shapes=[pltpu.VMEM(x.shape[1:], x.dtype) for x in given[:-1]]
         + [
             pltpu.SMEM(scene_offset.shape, F32),
             pltpu.SMEM(scene_weight.shape, F32),
@@ -874,7 +901,6 @@
             pltpu.VMEM((own_tiles, nr, LANES), F32),
         ]
         + [pltpu.VMEM((tiles, nr + 3 * HALO, LANES), F32)] * 2
-        + [pltpu.VMEM((own_tiles, nr, LANES), F32)]
         + [pltpu.VMEM((tiles, nr // 2 + 32, LANES), F32)] * 2
         + [pltpu.VMEM((tiles, nr // 4 + 24, LANES), F32)] * 2
         + [pltpu.VMEM((own_tiles, m3, LANES), F32)] * 2
@@ -903,6 +929,14 @@
         ],
         compiler_params=pltpu.CompilerParams(collective_id=0, has_side_effects=True),
     )(scene_offset, scene_weight, band_gain, heights, scene_ids, *given)
+    return pl.pallas_call(
+        last,
+        out_shape=jax.ShapeDtypeStruct((nr, nc), F32),
+        in_specs=[vmem] * 3,
+        out_specs=pl.BlockSpec(memory_space=pltpu.HBM),
+        scratch_shapes=[pltpu.VMEM((nr, nc), F32), pltpu.SemaphoreType.DMA((PIECES,))],
+        compiler_params=pltpu.CompilerParams(vmem_limit_bytes=16 * 1024 * 1024),
+    )(*kept)
 
 
 def solution(mesh):

time: 13.3 us -> 13.2 us (level)
  local copies, waits for them, and re-layouts: 0.97 us -> 0 us
  Pallas kernels: 12.2 us -> 13 us
    unnamed x1 -> x0, local copies, waits for them, and re-layouts: 0.97 us -> none
    pallas_call x1 -> x2, Pallas kernels: 12.2 us -> 13 us  [the longest x1 11.8 us: local(): pl.pallas_call(functools.partial(kernel, sizes, places), out_shape=(pltpu...]
where the time goes in v8:
time: 13.2 us; the launch traced here: 13 us
  Pallas kernels  13 us (98%)
    pallas_call x1, Pallas kernels, local(): pl.pallas_call(functools.partial(kernel, sizes, places), out_shape=(pltpu...  11.8 us
    pallas_call x1, Pallas kernels, local(): pl.pallas_call(last, out_shape=jax.ShapeDtypeStruct((nr, nc), F32), in_sp...  1.19 us

profile of v8, /device:TPU:0, one launch (start us, length us, event | category | flops | bytes accessed | tf_op | source)
XLA Modules:
  0.0 13.0 jit_solution(5616413888753180530)
XLA Ops:
  0.0 11.8 %shard_map.181 = (f32[4,512,128]{2,1,0:T(8,128)S(1)}, bf16[240,512]{1,0:T(8,128)(2,1)S(1)}, bf16[512,240]{1,0:T(8,128)(2,1)S(1)}) custom-call(f32[16]{0:T(128)} %off_hbm.1, f32[16]{0:T(128)} %wgt_hbm.1, f32[6]{0:T(128)} %gain_hbm.1, f32[512,512]{1,0:T(8,128)} %h_ref.1, s32[512,512]{1,0:T(8,128)} %s_ref.1, bf16[2,1024,256]{2,1,0:T(8,128)(2,1)} %constant.49.rest_0_, ...), custom_call_target="tpu_custom_call" | custom-call | tf_op jit(solution)/shard_map/pallas_call | solution.py:885
  11.8 1.2 %shard_map.182 = f32[512,512]{1,0:T(8,128)} custom-call(f32[4,512,128]{2,1,0:T(8,128)S(1)} %get-tuple-element.8.base_ref, bf16[240,512]{1,0:T(8,128)(2,1)S(1)} %get-tuple-element.9.us_ref, bf16[512,240]{1,0:T(8,128)(2,1)S(1)} %get-tuple-element.10.rows_ref), custom_call_target="tpu_custom_call" | custom-call | tf_op jit(solution)/shard_map/pallas_call | solution.py:932

commit v9 on v8

--- a/solution.py
+++ b/solution.py
@@ -221,7 +221,7 @@
     return dot(high, c) + dot(low, c)
 
 
-COLS = (("c03", "c2"), ("call", "e0"), ("c1",), ("s1", "s2"), ("ec0",), ("line",))
+COLS = (("c03", "c2"), ("call", "e0", "ec0"), ("c1",), ("s1", "s2"), ("line",))
 ROWS = (("rall", "er"), ("first", "second"), ("r012",))
 OWN_TILES, SIDE_TILES = 5, 2
 CHUNKS = 4
@@ -439,7 +439,7 @@
 
     def taps(src, c, start, count):
         x = [src[c, pl.ds(start + a, count, stride=2), :] for a in range(-2, 3)]
-        return 0.375 * x[2] + (0.25 * (x[1] + x[3]) + 0.0625 * (x[0] + x[4]))
+        return 6.0 * x[2] + (4.0 * (x[1] + x[3]) + (x[0] + x[4]))
 
     def hold(x, c, p, first):
         if first:
@@ -563,6 +563,10 @@
     def ends(x, c, last):
         return jnp.concatenate([x[c, 8:16, :], x[c, last : last + 8, :]], axis=0)
 
+    def filtered(y, name):
+        m, cut_ = table(name), (table(name).shape[1] // LANES - 1) * LANES
+        return jnp.concatenate([right(y, m[:, :cut_]), right(y[:, nc // 2 :], m[nc // 2 :, cut_:])], axis=1)
+
     with jax.named_scope("edge_own"):
         await_tables("s1", "s2", "c1", "c2")
 
@@ -570,7 +574,7 @@
             y = jnp.concatenate(
                 [jnp.concatenate([ends(x, c, last) for c in own_range], axis=1) for x in (n, d)], axis=0
             )
-            return right(y, table(name))
+            return filtered(y, name) if name == "c1" else right(y, table(name))
 
         own1, own2 = own_ends(n1, d1, last1, "c1"), own_ends(n2, d2, last2, "c2")
 
@@ -667,7 +671,8 @@
     with jax.named_scope("x_own"):
         for n, d, body, name, dst in ((n1, d1, body1, "c1", x1), (n2, d2, body2, "c2", x2)):
             for a, y in enumerate((n, d)):
-                y = right(wide_of(y, body, own_range), table(name))
+                y = wide_of(y, body, own_range)
+                y = filtered(y, name) if name == "c1" else right(y, table(name))
                 for c in range(dst.shape[1]):
                     dst[a, c] = y[:, c * LANES : (c + 1) * LANES]
 

time: 13.2 us -> 13.1 us (level)
  no operation moved by 1% of the time
where the time goes in v9:
time: 13.1 us; the launch traced here: 13 us
  Pallas kernels  12.9 us (98%)
    pallas_call x1, Pallas kernels, local(): pl.pallas_call(functools.partial(kernel, sizes, places), out_shape=(pltpu...  11.7 us
    pallas_call x1, Pallas kernels, local(): pl.pallas_call(last, out_shape=jax.ShapeDtypeStruct((nr, nc), F32), in_sp...  1.21 us

profile of v9, /device:TPU:0, one launch (start us, length us, event | category | flops | bytes accessed | tf_op | source)
XLA Modules:
  0.0 13.0 jit_solution(4051153209914908150)
XLA Ops:
  0.0 11.7 %shard_map.181 = (f32[4,512,128]{2,1,0:T(8,128)S(1)}, bf16[240,512]{1,0:T(8,128)(2,1)S(1)}, bf16[512,240]{1,0:T(8,128)(2,1)S(1)}) custom-call(f32[16]{0:T(128)} %off_hbm.1, f32[16]{0:T(128)} %wgt_hbm.1, f32[6]{0:T(128)} %gain_hbm.1, f32[512,512]{1,0:T(8,128)} %h_ref.1, s32[512,512]{1,0:T(8,128)} %s_ref.1, bf16[2,1024,256]{2,1,0:T(8,128)(2,1)} %constant.49.rest_0_, ...), custom_call_target="tpu_custom_call" | custom-call | tf_op jit(solution)/shard_map/pallas_call | solution.py:890
  11.8 1.2 %shard_map.182 = f32[512,512]{1,0:T(8,128)} custom-call(f32[4,512,128]{2,1,0:T(8,128)S(1)} %get-tuple-element.8.base_ref, bf16[240,512]{1,0:T(8,128)(2,1)S(1)} %get-tuple-element.9.us_ref, bf16[512,240]{1,0:T(8,128)(2,1)S(1)} %get-tuple-element.10.rows_ref), custom_call_target="tpu_custom_call" | custom-call | tf_op jit(solution)/shard_map/pallas_call | solution.py:937

commit v10 on v9

--- a/solution.py
+++ b/solution.py
@@ -225,7 +225,7 @@
 ROWS = (("rall", "er"), ("first", "second"), ("r012",))
 OWN_TILES, SIDE_TILES = 5, 2
 CHUNKS = 4
-PIECES = 4
+PIECES = 8
 
 
 def kernel(

time: 13.1 us -> 13.1 us (level)
  no operation moved by 1% of the time
where the time goes in v10:
time: 13.1 us; the launch traced here: 13 us
  Pallas kernels  13 us (99%)
    pallas_call x1, Pallas kernels, local(): pl.pallas_call(functools.partial(kernel, sizes, places), out_shape=(pltpu...  11.7 us
    pallas_call x1, Pallas kernels, local(): pl.pallas_call(last, out_shape=jax.ShapeDtypeStruct((nr, nc), F32), in_sp...  1.23 us

profile of v10, /device:TPU:0, one launch (start us, length us, event | category | flops | bytes accessed | tf_op | source)
XLA Modules:
  0.0 13.0 jit_solution(796777180769413493)
XLA Ops:
  0.0 11.7 %shard_map.181 = (f32[4,512,128]{2,1,0:T(8,128)S(1)}, bf16[240,512]{1,0:T(8,128)(2,1)S(1)}, bf16[512,240]{1,0:T(8,128)(2,1)S(1)}) custom-call(f32[16]{0:T(128)} %off_hbm.1, f32[16]{0:T(128)} %wgt_hbm.1, f32[6]{0:T(128)} %gain_hbm.1, f32[512,512]{1,0:T(8,128)} %h_ref.1, s32[512,512]{1,0:T(8,128)} %s_ref.1, bf16[2,1024,256]{2,1,0:T(8,128)(2,1)} %constant.49.rest_0_, ...), custom_call_target="tpu_custom_call" | custom-call | tf_op jit(solution)/shard_map/pallas_call | solution.py:890
  11.8 1.2 %shard_map.182 = f32[512,512]{1,0:T(8,128)} custom-call(f32[4,512,128]{2,1,0:T(8,128)S(1)} %get-tuple-element.8.base_ref, bf16[240,512]{1,0:T(8,128)(2,1)S(1)} %get-tuple-element.9.us_ref, bf16[512,240]{1,0:T(8,128)(2,1)S(1)} %get-tuple-element.10.rows_ref), custom_call_target="tpu_custom_call" | custom-call | tf_op jit(solution)/shard_map/pallas_call | solution.py:937
